TPU v7x, 32 devices: a whole 2x2x4 slice. The times are simulated.
32 devices in a mesh: dp: 32 (over z, y, x, core).
Axes of the slice: x: 2, y: 2, z: 4, core: 2. Of those that a mesh axis runs over, the one named last changes fastest.
Arguments:
- text_input: bfloat16 [256, 77, 384], P('dp'), may hold values from -6 to 6
- eot_index: int32 [256], P('dp'), may hold values from 4 to 76
- image_input: bfloat16 [256, 50, 384], P('dp'), may hold values from -6 to 6
- ln1_gain: float32 [1, 384], replicated, may hold values from 0.25 to 1.75
- ln1_bias: float32 [1, 384], replicated, may hold values from -1.75 to 1.75
- w_qkv: bfloat16 [1, 384, 1152], replicated, may hold values from -0.4375 to 0.4375
- w_attn_out: bfloat16 [1, 384, 384], replicated, may hold values from -0.875 to 0.875
- ln2_gain: float32 [1, 384], replicated, may hold values from 0.25 to 1.75
- ln2_bias: float32 [1, 384], replicated, may hold values from -1.75 to 1.75
- w_fc: bfloat16 [1, 384, 1536], replicated, may hold values from -0.3125 to 0.3125
- w_fc_out: bfloat16 [1, 1536, 384], replicated, may hold values from -0.15625 to 0.15625
- img_ln1_gain: float32 [1, 384], replicated, may hold values from 0.25 to 1.75
- img_ln1_bias: float32 [1, 384], replicated, may hold values from -1.75 to 1.75
- img_w_qkv: bfloat16 [1, 384, 1152], replicated, may hold values from -0.4375 to 0.4375
- img_w_attn_out: bfloat16 [1, 384, 384], replicated, may hold values from -0.875 to 0.875
- img_ln2_gain: float32 [1, 384], replicated, may hold values from 0.25 to 1.75
- img_ln2_bias: float32 [1, 384], replicated, may hold values from -1.75 to 1.75
- img_w_fc: bfloat16 [1, 384, 1536], replicated, may hold values from -0.3125 to 0.3125
- img_w_fc_out: bfloat16 [1, 1536, 384], replicated, may hold values from -0.15625 to 0.15625
- final_gain: float32 [384], replicated, may hold values from 0.25 to 1.75
- final_bias: float32 [384], replicated, may hold values from -1.75 to 1.75
- text_proj: bfloat16 [384, 384], replicated, may hold values from -0.3125 to 0.3125
- image_gain: float32 [384], replicated, may hold values from 0.25 to 1.75
- image_bias: float32 [384], replicated, may hold values from -1.75 to 1.75
- image_proj: bfloat16 [384, 384], replicated, may hold values from -0.3125 to 0.3125
- logit_scale: float32 [1], replicated, may hold values from 3.4 to 4.1
Outputs:
- loss: float32 [1], replicated
- text_input_grad: float32 [256, 77, 384], P('dp')
- image_input_grad: float32 [256, 50, 384], P('dp')
- text_layer_grads: float32 [1, 1771008], P(None, 'dp')
- image_layer_grads: float32 [1, 1771008], P(None, 'dp')
- head_grads: float32 [296448], P('dp')
- logit_scale_grad: float32 [1], replicated
Inputs may be any that keep to these rules, and one draw needn't show every extreme that they name: `eot_index`: the end token's position of each caption; slots after it are padding.
All inputs are finite; a program needn't handle non-finite values.
Results may differ from a plain program's by a relative error of at most 0.019.
Values may be sent and summed in bfloat16 or wider, within the bound.
No kernel may reach another device: no remote copies, remote signals or barrier semaphores. Data moves between devices by JAX's collectives and lax.ppermute only.
A program may use at most 128 MiB of HBM per device.

v0:
```python
import enum

import jax
import jax.numpy as jnp
from jax import lax
from jax.experimental import pallas as pl
from jax.experimental.pallas import tpu as pltpu
from jax.sharding import PartitionSpec as P

HEAD_DIM = 64
LANES = 128
WINDOW = 64

EPS = 1e-05
UNIT_EPS = 1e-06
MASKED = -1000000000.0
LIMIT = 44 * 2**20
IN_FLIGHT = 64 * 2**20
F32 = jnp.float32
BF16 = jnp.bfloat16


class Place(enum.Enum):
    FAR = enum.auto()
    FEW = enum.auto()
    RAW = enum.auto()
    AUTO = enum.auto()
    SCALAR = enum.auto()


class K(enum.Enum):
    BIAS = enum.auto()
    BIAS2 = enum.auto()
    EOT = enum.auto()
    GAIN = enum.auto()
    GAIN2 = enum.auto()
    HEAD = enum.auto()
    HEAD_BIAS = enum.auto()
    HEAD_GAIN = enum.auto()
    INPUT = enum.auto()
    LOSS = enum.auto()
    MINE = enum.auto()
    MIXED = enum.auto()
    NORMED = enum.auto()
    OTHERS = enum.auto()
    OWN = enum.auto()
    PACK = enum.auto()
    PART = enum.auto()
    PROBS = enum.auto()
    PROJ = enum.auto()
    QUERIES = enum.auto()
    QUERY = enum.auto()
    ROWS = enum.auto()
    SCALE = enum.auto()
    SCORES = enum.auto()
    SEND = enum.auto()
    SENT = enum.auto()
    SWAPPED = enum.auto()
    SHARE = enum.auto()
    UNIT = enum.auto()
    VALUES = enum.auto()
    W_FC = enum.auto()
    W_FC_OUT = enum.auto()
    W_OUT = enum.auto()
    W_QKV = enum.auto()
    WINDOWS = enum.auto()
    X = enum.auto()


def dot(left, right):
    return jnp.dot(left, right, preferred_element_type=F32)


def dot_nt(left, right):
    return lax.dot_general(left, right, (((1,), (1,)), ((), ())), preferred_element_type=F32)


def dot_tn(left, right):
    return lax.dot_general(left, right, (((0,), (0,)), ((), ())), preferred_element_type=F32)


def standard(values):
    center = values - jnp.mean(values, -1, keepdims=True)
    scale = lax.rsqrt(jnp.mean(center * center, -1, keepdims=True) + EPS)
    return center * scale, scale


def norm_back(grad, unit, scale, gain):
    scaled = grad * gain
    return scale * (
        scaled
        - jnp.mean(scaled, -1, keepdims=True)
        - unit * jnp.mean(scaled * unit, -1, keepdims=True)
    )


def head_masks(width):
    lane = lax.broadcasted_iota(jnp.int32, (1, width), 1)
    return [
        ((lane >= h * HEAD_DIM) & (lane < (h + 1) * HEAD_DIM)).astype(F32)
        for h in range(width // HEAD_DIM)
    ]


def spread(rows):
    return jnp.concatenate([rows * mask for mask in head_masks(rows.shape[1])], 0)


def collect(rows, caps):
    masks = head_masks(rows.shape[1])
    return sum(rows[h * caps : (h + 1) * caps] * mask for h, mask in enumerate(masks))


def picked_columns(caps, total, ends):
    cap = lax.broadcasted_iota(jnp.int32, (caps, 1), 0)
    at = cap
    for b in range(caps):
        at = jnp.where(cap == b, ends[b] * caps + b, at)
    column = lax.broadcasted_iota(jnp.int32, (caps, total), 1)
    chosen = jnp.where(column == at, 1.0, 0.0).astype(BF16)
    return chosen, column, at


class Plan:
    def __init__(self, dim, hidden, devices):
        self.dim, self.hidden, self.devices = dim, hidden, devices
        self.row = 3 * dim
        self.qkv_at = 2 * dim
        self.out_at = self.qkv_at + dim * self.row
        self.norm_at = self.out_at + dim * dim
        self.fc_at = self.norm_at + 2 * dim
        self.fc_out_at = self.fc_at + dim * hidden
        self.total = self.fc_out_at + hidden * dim
        self.share = -(-self.total // devices)
        self.head_total = 2 * (2 * dim + dim * dim)
        self.head_share = -(-self.head_total // devices)
        self.roots = -(-self.out_at // self.share)
        self.rows_out = -(-(self.share // LANES + 2) // 8) * 8
        self.head_rows_out = -(-(self.head_share // LANES + 2) // 8) * 8
        assert self.share // self.row + 2 <= WINDOW
        assert self.total % devices == 0 and self.head_total % devices == 0

    def column(self, device):
        if isinstance(device, int):
            return min(max(device * self.share - self.qkv_at, 0) // self.row, self.dim - 1)
        return jnp.minimum(jnp.maximum(device * self.share - self.qkv_at, 0) // self.row, self.dim - 1)


def window_tiles(plan, text, image, device, caps):
    dim = text.shape[1]
    first = plan.column(device)
    lane = lax.broadcasted_iota(jnp.int32, (text.shape[0], LANES), 1)
    left = pltpu.roll(text, (dim - first) % dim, 1)[:, :LANES]
    right = pltpu.roll(image, (dim - first + WINDOW) % dim, 1)[:, :LANES]
    both = jnp.where(lane < WINDOW, left, right).astype(BF16)
    heads = text.shape[0] // caps
    return jnp.concatenate([both[h * caps : (h + 1) * caps] for h in range(heads)], 1)


def pack_windows(plan, target, text, image, caps, common):
    width = text.shape[0] // caps * LANES
    held = plan.roots + plan.roots % 2

    def fill(device, core):
        target[device, :, :width] = window_tiles(plan, text, image, device, caps)
        if common is not None:
            target[device, :, width:] = common[core]

    if held <= 16:
        for device in range(held):
            fill(device, device % 2)
    else:

        @pl.loop(0, held // 2)
        def _(chip):
            for core in range(2):
                fill(2 * chip + core, core)

    @pl.loop(held, target.shape[0])
    def _(device):
        target[device] = jnp.zeros(target.shape[1:], BF16)


def take_rows(source, at, count):
    row, lane_at = at // LANES, at % LANES
    lane = lax.broadcasted_iota(jnp.int32, (count, LANES), 1)
    mixed = jnp.where(
        lane >= lane_at, source[pl.ds(row, count), :], source[pl.ds(row + 1, count), :]
    )
    return pltpu.roll(mixed, lax.rem(LANES - lane_at, LANES), 1)


def put_tile(target, row, block):
    count, width = block.shape
    step = width // LANES
    for j in range(step):
        piece = block[:, j * LANES : (j + 1) * LANES]
        if count == 1:
            target[row + j : row + j + 1, :] = piece
        else:
            target[pl.ds(row + j, count, stride=step), :] = piece


def front_tower(tower, ins, picked, last):
    x = ins[K.X, tower].get()[...]
    seq, caps, dim = x.shape
    total = seq * caps
    heads = dim // HEAD_DIM
    source = x.reshape(total, dim)
    unit, unused = standard(source.astype(F32))
    yield
    gain, bias = ins[K.GAIN, tower].get()[...], ins[K.BIAS, tower].get()[...]
    normed = (unit * gain + bias).astype(BF16)
    chosen, column, pick_at = picked_columns(caps, total, picked)
    last_at = pick_at
    if last is not picked:
        unused, unused, last_at = picked_columns(caps, total, last)
    pooled = dot(chosen, source)
    yield
    pooled_unit, unused = standard(pooled)
    pooled_normed = (pooled_unit * gain + bias).astype(BF16)
    w_ref = ins[K.W_QKV, tower].get()
    query = dot(pooled_normed, w_ref[0, :, :dim]).astype(BF16).astype(F32)
    yield
    through_keys = dot_nt(spread(query).astype(BF16), w_ref[0, :, dim : 2 * dim])
    yield
    scores = dot_nt(through_keys.astype(BF16), normed) * HEAD_DIM ** (-0.5)
    yield
    cap = lax.broadcasted_iota(jnp.int32, (caps, 1), 0)
    seen = jnp.where((lax.rem(column, caps) == cap) & (column <= last_at), 1.0, 0.0)
    seen = jnp.concatenate([seen] * heads, 0) > 0.5
    peak = jnp.max(jnp.where(seen, scores, MASKED), -1, keepdims=True)
    sums = jnp.sum(jnp.where(seen, jnp.exp(scores - peak), 0.0), -1, keepdims=True)
    probs = jnp.where(seen, jnp.exp(scores - (peak + jnp.log(sums))), 0.0)
    yield
    values = dot(probs.astype(BF16), normed)
    yield
    mixed = collect(dot(values.astype(BF16), w_ref[0, :, 2 * dim :]), caps).astype(BF16)
    return pooled, mixed, (normed, unit, probs, query, through_keys, values, chosen)


def attended_towers(ins):
    eot = ins[K.EOT].get()
    caps = eot.shape[0]
    seq = ins[K.X, 1].buf.shape[0]
    ends = [eot[b] for b in range(caps)]
    views = (ends, ends), ([0] * caps, [seq - 1] * caps)
    return run_together([front_tower(tower, ins, *views[tower]) for tower in range(2)])


def front_body(plan):
    def body(scalars, ins, outs, scratch):
        payload = []
        for pooled, mixed, unused in attended_towers(ins):
            payload += [pooled.astype(BF16), mixed]
        payload = jnp.concatenate(payload, 1)
        rows = outs[K.ROWS].ref

        @pl.loop(0, rows.shape[0])
        def _(chip):
            rows[chip] = payload

    return body


def pack_at(dim, hidden, caps):
    heads = dim // HEAD_DIM
    sizes = [heads * caps, heads * caps, caps, caps, caps, caps, caps, caps * hidden // dim]
    places, at = [], 0
    for size in sizes:
        places.append(slice(at, at + size))
        at += size
    return places, at


def weights_of(tower, ins):
    names = K.W_OUT, K.GAIN2, K.BIAS2, K.W_FC, K.W_FC_OUT, K.HEAD_GAIN, K.HEAD_BIAS, K.PROJ
    return [ins[name, tower] for name in names]


def side_body(plan):
    def body(scalars, ins, outs, scratch):
        dim, hidden = plan.dim, plan.hidden
        caps = ins[K.EOT].buf.shape[0]
        places, unused = pack_at(dim, hidden, caps)
        towers = attended_towers(ins)
        pack_windows(plan, outs[K.VALUES].ref, towers[0][2][5], towers[1][2][5], caps, None)
        outs[K.VALUES].push()
        kept = [], []
        for tower, (pooled, mixed, saved) in enumerate(towers):
            normed, unit, probs, query, through_keys, values, chosen = saved
            unit = unit.astype(BF16)
            for name, value in ((K.NORMED, normed), (K.UNIT, unit), (K.PROBS, probs)):
                outs[name, tower].ref[...] = value
                outs[name, tower].push()
            small = [through_keys, dot(probs.astype(BF16), unit), dot(chosen, unit), query]
            for place, value in zip(places, small):
                outs[K.PACK, tower].ref[place, :] = value
        run_together(
            [
                tower_forward(pooled, mixed, weights_of(tower, ins), kept[tower], None, None)
                for tower, (pooled, mixed, unused) in enumerate(towers)
            ]
        )
        for tower in range(2):
            pack = outs[K.PACK, tower]
            for place, value in zip(places[4:], kept[tower][:3]):
                pack.ref[place, :] = value
            for j in range(hidden // dim):
                at = places[7].start + j * caps
                pack.ref[at : at + caps, :] = kept[tower][3][:, j * dim : (j + 1) * dim]
            pack.push()

    return body


def run_together(steps):
    results = [None] * len(steps)
    live = list(range(len(steps)))
    while live:
        for index in list(live):
            try:
                next(steps[index])
            except StopIteration as stop:
                results[index] = stop.value
                live.remove(index)
    return results


def chunks(width):
    step = 512 if width % 512 == 0 else width
    return [slice(at, at + step) for at in range(0, width, step)]


def gate_slope(hidden):
    gate = jax.nn.sigmoid(1.702 * hidden)
    return gate + 1.702 * hidden * gate * (1.0 - gate)


def unit_rows_of(embed):
    length = lax.rsqrt(jnp.sum(embed * embed, -1, keepdims=True) + UNIT_EPS)
    return embed * length, length


def tower_forward(pooled, mixed, weights, kept, hidden_ref, active_ref):
    w_out, gain, bias, w_fc, w_fc_out, head_gain, head_bias, proj = weights
    middle = pooled + dot(mixed, w_out.get()[0])
    yield
    unit, unused = standard(middle)
    normed = (unit * gain.get()[...] + bias.get()[...]).astype(BF16)
    yield
    result = middle
    w_fc, w_fc_out = w_fc.get(), w_fc_out.get()
    every = []
    for cols in chunks(w_fc.shape[2]):
        hidden = dot(normed, w_fc[0, :, cols])
        active = (hidden * jax.nn.sigmoid(1.702 * hidden)).astype(BF16)
        every.append(hidden)
        if hidden_ref is not None:
            hidden_ref[:, cols] = hidden
            active_ref[:, cols] = active
        result = result + dot(active, w_fc_out[0, cols, :])
        yield
    head_unit, unused = standard(result)
    head_in = (head_unit * head_gain.get()[...][None] + head_bias.get()[...][None]).astype(BF16)
    embed = dot(head_in, proj.get()[...])
    yield
    if kept is not None:
        kept += [middle, result, embed]
        if hidden_ref is None:
            kept.append(jnp.concatenate(every, 1))
    return unit_rows_of(embed)[0].astype(BF16)


def log_sum(logits, axis):
    peak = jnp.max(logits, axis, keepdims=True)
    return peak + jnp.log(jnp.sum(jnp.exp(logits - peak), axis, keepdims=True))


def unit_gradient(multiplier, logits, own_total, other_total, matched, other):
    target = jnp.where(matched, 1.0, 0.0)
    own = 0.5 * multiplier * (jnp.exp(logits - own_total) - target)
    cross = 0.5 * multiplier * (jnp.exp(logits - other_total) - target)
    return dot(own.astype(BF16), other) + dot(cross.astype(BF16), other)


def embed_back(grad_unit, embed):
    unit_embed, length = unit_rows_of(embed)
    along = jnp.sum(unit_embed * grad_unit, -1, keepdims=True)
    return (length * (grad_unit - unit_embed * along)).astype(BF16)


def tower_backward(grad_embed, middle, result, hidden, weights, keep_hidden):
    w_out, gain, bias, w_fc, w_fc_out, head_gain, head_bias, proj = weights
    grad_head = dot_nt(grad_embed, proj.get()[...])
    yield
    head_unit, head_scale = standard(result)
    grad_result = norm_back(grad_head, head_unit, head_scale, head_gain.get()[...][None])
    grad_out = grad_result.astype(BF16)
    yield
    w_fc, w_fc_out = w_fc.get(), w_fc_out.get()
    grad_normed = 0.0
    for cols in chunks(w_fc.shape[2]):
        grad_active = dot_nt(grad_out, w_fc_out[0, cols, :])
        grad_hidden = (grad_active * gate_slope(hidden[:, cols])).astype(BF16)
        if keep_hidden is not None:
            keep_hidden[:, cols] = grad_hidden
        grad_normed = grad_normed + dot_nt(grad_hidden, w_fc[0, :, cols])
        yield
    unit, scale = standard(middle)
    grad_middle = grad_result + norm_back(grad_normed, unit, scale, gain.get()[...])
    yield
    grad_mixed = dot_nt(grad_middle.astype(BF16), w_out.get()[0]).astype(BF16)
    yield
    return grad_head, head_unit, grad_out, grad_normed, unit, grad_middle, grad_mixed


def own_steps(plan, tower, units, multiplier, own_at, ins, outs):
    mine, other = units[tower], units[1 - tower]
    own_out = outs[K.OWN, tower]
    caps, dim = own_out.ref.shape[1:]
    places, unused = pack_at(dim, plan.hidden, caps)
    other_total = log_sum(multiplier * dot_nt(mine, other), 0)
    yield
    pack = ins[K.PACK, tower].get()
    embed = pack[places[6], :]
    logits = multiplier * dot_nt(unit_rows_of(embed)[0].astype(BF16), other)
    matched = lax.broadcasted_iota(jnp.int32, logits.shape, 1) == own_at + lax.broadcasted_iota(
        jnp.int32, logits.shape, 0
    )
    grad_unit = unit_gradient(multiplier, logits, log_sum(logits, 1), other_total, matched, other)
    yield
    hidden_at = places[7].start
    hidden = jnp.concatenate(
        [pack[hidden_at + j * caps : hidden_at + (j + 1) * caps, :] for j in range(plan.hidden // dim)], 1
    )
    done = yield from tower_backward(
        embed_back(grad_unit, embed), pack[places[4], :], pack[places[5], :], hidden,
        weights_of(tower, ins), None,
    )
    grad_middle, grad_mixed = done[5], done[6].astype(F32)
    own_out.ref[0] = grad_mixed
    own_out.ref[1] = grad_middle
    own_out.push()
    w_ref = ins[K.W_QKV, tower].get()
    through_values = dot_nt(spread(grad_mixed).astype(BF16), w_ref[0, :, 2 * dim :])
    yield
    normed = ins[K.NORMED, tower].get()[...]
    grad_probs = dot_nt(through_values.astype(BF16), normed)
    yield
    probs = ins[K.PROBS, tower].get()[...]
    inner = jnp.sum(probs * grad_probs, -1, keepdims=True)
    grad_scores = (probs * (grad_probs - inner) * HEAD_DIM ** (-0.5)).astype(BF16)
    outs[K.SCORES, tower].ref[...] = grad_scores
    outs[K.SCORES, tower].push()
    yield
    spread_keys = dot(grad_scores, normed)
    yield
    grad_query = collect(dot(spread_keys.astype(BF16), w_ref[0, :, dim : 2 * dim]), caps).astype(BF16)
    outs[K.QUERY, tower].ref[...] = grad_query
    outs[K.QUERY, tower].push()
    yield
    units = pack[places[0], :] * dot(grad_scores, ins[K.UNIT, tower].get()[...])
    yield
    through_query = dot_nt(grad_query, w_ref[0, :, :dim])
    units = units + through_values * pack[places[1], :]
    gain_part = jnp.sum(units, 0, keepdims=True) + jnp.sum(
        through_query * pack[places[2], :], 0, keepdims=True
    )
    return spread_keys, grad_query, gain_part


def forward_pair(plan, rows, ins, kept, hidden, active):
    dim = plan.dim
    return run_together(
        [
            tower_forward(
                rows[:, 2 * tower * dim : (2 * tower + 1) * dim].astype(F32),
                rows[:, (2 * tower + 1) * dim : (2 * tower + 2) * dim],
                weights_of(tower, ins), kept[tower], hidden[tower], active[tower],
            )
            for tower in range(2)
        ]
    )


def middle_body(plan):
    def body(scalars, ins, outs, scratch):
        at_ref, scale_ref = scalars
        rows_ref, sems = scratch
        dim = plan.dim
        device = at_ref[0]
        caps, wide = rows_ref.shape[2:]
        copies = [
            pltpu.make_async_copy(ins[name].ref, rows_ref.at[:, core], sems.at[i])
            for i, (name, core) in enumerate(((K.MINE, device % 2), (K.OTHERS, 1 - device % 2)))
        ]
        for copy in copies:
            copy.start()
        for copy in copies:
            copy.wait()
        rows = rows_ref[...].reshape(plan.devices * caps, wide)
        outs[K.ROWS].ref[...] = rows
        outs[K.ROWS].push()
        units = forward_pair(plan, rows, ins, (None, None), (None, None), (None, None))
        multiplier = jnp.exp(jnp.full((1, 1), scale_ref[0], F32))
        own_at = device * caps
        parts = run_together(
            [own_steps(plan, tower, units, multiplier, own_at, ins, outs) for tower in range(2)]
        )
        (keys_t, query_t, gain_t), (keys_i, query_i, gain_i) = parts
        tiles = dim // LANES
        small = jnp.concatenate(
            [g[:, j * LANES : (j + 1) * LANES] for g in (gain_t, gain_i) for j in range(tiles)]
            + [jnp.zeros((caps - 2 * tiles, LANES), F32)],
            0,
        )
        common = [jnp.concatenate([query, small.astype(BF16)], 1) for query in (query_t, query_i)]
        pack_windows(plan, outs[K.SEND].ref, keys_t, keys_i, caps, common)

    return body


def tail_body(plan):
    def body(scalars, ins, outs, scratch):
        at_ref, scale_ref = scalars
        dim, hidden_dim = plan.dim, plan.hidden
        loss_ref, scale_grad_ref = outs[K.LOSS].ref, outs[K.SCALE].ref
        flat, flat_head, wide_t, wide_i, hidden_grad, small, hidden_t, hidden_i, active_t, active_i = scratch
        device = at_ref[0]
        eot = ins[K.EOT].get()
        caps = eot.shape[0]
        ends = [eot[b] for b in range(caps)]
        places, unused = pack_at(dim, hidden_dim, caps)
        multiplier = jnp.exp(jnp.full((1, 1), scale_ref[0], F32))

        def input_gradient(tower, picked, wide):
            names = K.X, K.GAIN, K.W_QKV, K.PROBS, K.PACK, K.OWN, K.SCORES, K.QUERY
            x, gain, w_ref, probs, pack, own, scores, query_grad = (
                ins[name, tower].get() for name in names
            )
            seq = x.shape[0]
            unit, scale = standard(x[...].reshape(seq * caps, dim).astype(F32))
            query = pack[places[3], :]
            grad_keys = dot_tn(scores[...], spread(query).astype(BF16)).astype(BF16)
            grad_values = dot_tn(probs[...].astype(BF16), spread(own[0]).astype(BF16)).astype(BF16)
            grad_normed = dot_nt(grad_keys, w_ref[0, :, dim : 2 * dim])
            grad_normed = grad_normed + dot_nt(grad_values, w_ref[0, :, 2 * dim :])
            through_query = dot_nt(query_grad[...], w_ref[0, :, :dim])
            wide[...] = grad_normed
            for b in range(caps):
                at = picked[b] * caps + b
                wide[pl.ds(at, 1), :] = wide[pl.ds(at, 1), :] + through_query[b : b + 1]
            wide[...] = norm_back(wide[...], unit, scale, gain[...])
            for b in range(caps):
                at = picked[b] * caps + b
                wide[pl.ds(at, 1), :] = wide[pl.ds(at, 1), :] + own[1][b : b + 1]
            outs[K.INPUT, tower].ref[...] = wide[...].reshape(seq, caps, dim)
            outs[K.INPUT, tower].push()

        input_gradient(0, ends, wide_t)
        input_gradient(1, [0] * caps, wide_i)

        rows = ins[K.ROWS].get()[...]
        count = rows.shape[0]
        kept = [], []
        hiddens, actives = (hidden_t, hidden_i), (active_t, active_i)
        units = forward_pair(plan, rows, ins, kept, hiddens, actives)
        embeds = [items[2] for items in kept]
        logits = multiplier * dot_nt(units[1], units[0])
        matched = lax.broadcasted_iota(jnp.int32, logits.shape, 1) == lax.broadcasted_iota(
            jnp.int32, logits.shape, 0
        )
        row_total, column_total = log_sum(logits, 1), log_sum(logits, 0)
        target = jnp.where(matched, 1.0, 0.0)
        by_row = 0.5 * (jnp.exp(logits - row_total) - target)
        by_column = 0.5 * (jnp.exp(logits - column_total) - target)
        total = jnp.sum(row_total) + jnp.sum(column_total) - 2.0 * jnp.sum(target * logits)
        loss_ref[0] = total / (2 * count)
        scale_grad_ref[0] = jnp.sum((by_row + by_column) * logits)
        by_row = (multiplier * by_row).astype(BF16)
        by_column = (multiplier * by_column).astype(BF16)
        grad_units = (
            dot_tn(by_row, units[1]) + dot_tn(by_column, units[1]),
            dot(by_row, units[0]) + dot(by_column, units[0]),
        )

        start, head_start = device * plan.share, device * plan.head_share
        front = plan.rows_out
        half = plan.head_total // 2
        for tower in range(2):
            weights = weights_of(tower, ins)
            gain, bias, head_gain, head_bias = (weights[j] for j in (1, 2, 5, 6))
            middle, result, unused = kept[tower]
            active = actives[tower]
            grad_embed = embed_back(grad_units[tower], embeds[tower])
            (done,) = run_together(
                [
                    tower_backward(
                        grad_embed, middle, result, hiddens[tower], weights, hidden_grad
                    )
                ]
            )
            grad_head, head_unit, grad_out, grad_normed, unit, grad_middle, grad_mixed = done
            outs[K.MIXED, tower].ref[...] = grad_mixed
            outs[K.MIXED, tower].push()
            middle_low = grad_middle.astype(BF16)
            normed = (unit * gain.get()[...] + bias.get()[...]).astype(BF16)
            head_in = head_unit * head_gain.get()[...][None] + head_bias.get()[...][None]
            head_in = head_in.astype(BF16)
            small[0:1, :] = jnp.sum(grad_normed * unit, 0, keepdims=True)
            small[1:2, :] = jnp.sum(grad_normed, 0, keepdims=True)
            small[2:3, :] = jnp.sum(grad_head * head_unit, 0, keepdims=True)
            small[3:4, :] = jnp.sum(grad_head, 0, keepdims=True)
            mixed = rows[:, (2 * tower + 1) * dim : (2 * tower + 2) * dim]

            def when_held(at, size, store):
                @pl.when((at < start + plan.share) & (at + size > start))
                def _():
                    store(front + (at - plan.out_at) // LANES)

            def when_kept(at, size, store):
                at = at + tower * half

                @pl.when((at < head_start + plan.head_share) & (at + size > head_start))
                def _():
                    store(at // LANES)

            def products(when, target, at, left, right):
                for t in range(left.shape[1] // LANES):
                    cols = slice(t * LANES, (t + 1) * LANES)
                    when(
                        at + t * LANES * right.shape[1],
                        LANES * right.shape[1],
                        lambda row: put_tile(target, row, dot_tn(left[:, cols], right[...])),
                    )

            def row_of(when, target, at, index):
                when(at, dim, lambda row: put_tile(target, row, small[index : index + 1, :]))

            products(when_held, flat, plan.out_at, mixed, middle_low)
            row_of(when_held, flat, plan.norm_at, 0)
            row_of(when_held, flat, plan.norm_at + dim, 1)
            products(when_held, flat, plan.fc_at, normed, hidden_grad)
            products(when_held, flat, plan.fc_out_at, active, grad_out)
            at = jnp.maximum(start - plan.out_at + front * LANES, 0)
            outs[K.PART, tower].ref[...] = take_rows(flat, at, plan.rows_out)
            outs[K.PART, tower].push()
            row_of(when_kept, flat_head, 0, 2)
            row_of(when_kept, flat_head, dim, 3)
            products(when_kept, flat_head, 2 * dim, head_in, grad_embed)

        outs[K.HEAD].ref[...] = take_rows(flat_head, head_start, plan.head_rows_out)
        outs[K.HEAD].push()

        for tower in range(2):
            bias = ins[K.BIAS, tower].get()

        @pl.when(device == 0)
        def _():
            for tower in range(2):
                w_ref = ins[K.W_QKV, tower].get()
                grads = dot_nt(outs[K.MIXED, tower].ref[...], w_ref[0, :, 2 * dim :])
                outs[K.BIAS].ref[tower : tower + 1, :] = jnp.sum(grads, 0, keepdims=True)

        @pl.when(device < plan.roots)
        def _():
            first = plan.column(device)
            lane = lax.broadcasted_iota(jnp.int32, (count, LANES), 1)
            picked_rows = []
            for tower in range(2):
                gain, bias, w_ref = (ins[name, tower].get() for name in (K.GAIN, K.BIAS, K.W_QKV))
                pooled = rows[:, 2 * tower * dim : (2 * tower + 1) * dim].astype(F32)
                unit, unused = standard(pooled)
                normed = unit * gain[...] + bias[...]
                outs[K.QUERIES].ref[:, tower * dim : (tower + 1) * dim] = dot(
                    normed.astype(BF16), w_ref[0, :, :dim]
                ).astype(BF16)
                shift = lax.rem(dim - first + tower * WINDOW, dim)
                picked_rows.append(pltpu.roll(normed, shift, 1)[:, :LANES])
            outs[K.WINDOWS].ref[...] = jnp.where(lane < WINDOW, picked_rows[0], picked_rows[1]).astype(BF16)

    return body


def last_body(plan):
    def body(scalars, ins, outs, scratch):
        (at_ref,) = scalars
        flat, wq, grad_query, sems = scratch
        dim = plan.dim
        heads = dim // HEAD_DIM
        tiles = dim // LANES
        device = at_ref[0]
        copies = [
            pltpu.make_async_copy(
                ins[K.W_QKV, tower].ref.at[0, :, pl.ds(0, dim)], wq.at[tower], sems.at[tower]
            )
            for tower in range(2)
        ]

        @pl.when(device == 0)
        def _():
            for copy in copies:
                copy.start()

        parts = [ins[K.PART, tower].get() for tower in range(2)]

        def store(tower, block):
            line = outs[K.SHARE, tower].ref
            line[...] = block.reshape(1, block.shape[0] * LANES)[:, : plan.share]

        @pl.when(device >= plan.roots)
        def _():
            for tower in range(2):
                store(tower, parts[tower][...])

        names = K.SENT, K.SWAPPED, K.VALUES, K.WINDOWS, K.QUERIES, K.BIAS, (K.MIXED, 0), (K.MIXED, 1)
        sent_ref, swapped, values_ref, windows, queries, bias, mixed_t, mixed_i = (
            ins[name].get() for name in names
        )

        @pl.when(device < plan.roots)
        def _():
            at_query = heads * LANES
            at_small = at_query + dim
            count = sent_ref.shape[0]
            for core in range(2):

                @pl.when(device % 2 == core)
                def _():
                    for tower, source in enumerate((sent_ref, swapped) if core == 0 else (swapped, sent_ref)):
                        grad_query[:, tower * dim : (tower + 1) * dim] = source[:, at_query:at_small]

            small = sent_ref[:, at_small:].astype(F32)
            small = jnp.sum(small.reshape(count // 8, 8, LANES), 0)
            query_part = dot_tn(windows[...], grad_query[...])
            lane = lax.broadcasted_iota(jnp.int32, (1, LANES), 1)
            halves = [(lane < HEAD_DIM).astype(F32), (lane >= HEAD_DIM).astype(F32)]
            for j in range(tiles):
                put = []
                cols = slice(j * LANES, (j + 1) * LANES)
                others = slice(dim + j * LANES, dim + (j + 1) * LANES)
                for source, factors in (
                    (sent_ref, (queries[:, cols], queries[:, others])),
                    (values_ref, (mixed_t[:, cols], mixed_i[:, cols])),
                ):
                    right = jnp.concatenate(factors, 1).astype(F32)
                    total = 0.0
                    for odd in range(2):
                        h = 2 * j + odd
                        left = source[:, h * LANES : (h + 1) * LANES]
                        mask = jnp.concatenate([halves[odd]] * 2, 1)
                        total = total + dot_tn(left, (right * mask).astype(BF16))
                    put.append(total)
                for tower in range(2):
                    rows = slice(tower * WINDOW, (tower + 1) * WINDOW)
                    own = slice(tower * LANES, (tower + 1) * LANES)
                    q_at = tower * dim + j * LANES
                    for part, block in enumerate(
                        (query_part[rows, q_at : q_at + LANES], put[0][rows, own], put[1][rows, own])
                    ):
                        flat[
                            tower,
                            pl.ds(2 * tiles + part * tiles + j, WINDOW, stride=3 * tiles),
                            :,
                        ] = block
            for tower in range(2):
                flat[tower, 0:tiles, :] = small[tower * tiles : (tower + 1) * tiles]

            @pl.when(device == 0)
            def _():
                for tower, copy in enumerate(copies):
                    copy.wait()
                    grads = grad_query[:, tower * dim : (tower + 1) * dim]
                    row = jnp.sum(dot_nt(grads, wq[tower]), 0, keepdims=True)
                    row = row + bias[tower : tower + 1, :]
                    for j in range(tiles):
                        flat[tower, tiles + j : tiles + j + 1, :] = row[
                            :, j * LANES : (j + 1) * LANES
                        ]

            start = device * plan.share
            at = start - plan.column(device) * plan.row
            shape = parts[0].shape
            index = (
                start
                + lax.broadcasted_iota(jnp.int32, shape, 0) * LANES
                + lax.broadcasted_iota(jnp.int32, shape, 1)
            )
            for tower in range(2):
                own = take_rows(flat.at[tower], at, plan.rows_out)
                store(tower, jnp.where(index < plan.out_at, own, parts[tower][...]))

    return body


class Fetch:
    def __init__(self, source, buf, sem, queue):
        self.ref, self.buf, self.queue, self.waited = source, buf, queue, False
        self.size = buf.dtype.itemsize
        for extent in buf.shape:
            self.size *= extent
        self.copy = pltpu.make_async_copy(source, buf, sem)

    def get(self):
        if not self.waited:
            self.queue.advance(self)
            self.copy.wait()
            self.waited = True
            self.queue.flying -= self.size
            self.queue.advance(None)
        return self.buf


class Queue:
    def __init__(self):
        self.waiting, self.flying = [], 0

    def advance(self, needed):
        while self.waiting and (
            needed in self.waiting or self.flying + self.waiting[0].size <= IN_FLIGHT
        ):
            fetch = self.waiting.pop(0)
            fetch.copy.start()
            self.flying += fetch.size


class Here:
    def __init__(self, ref):
        self.buf = self.ref = ref

    def get(self):
        return self.buf

    def push(self):
        pass


class Push:
    def __init__(self, ref, target, sem):
        self.ref, self.started = ref, False
        self.copy = pltpu.make_async_copy(ref, target, sem)

    def push(self):
        self.started = True
        self.copy.start()


def run(body, name, outs, scratch, scalars, arrays):
    smem = pl.BlockSpec(memory_space=pltpu.SMEM)
    hbm = pl.BlockSpec(memory_space=pltpu.HBM)
    vmem = pl.BlockSpec(memory_space=pltpu.VMEM)
    fetched = [(array, place) for array, place in arrays.values() if place in (Place.FAR, Place.FEW)]
    pushed = [(shape, kind) for shape, kind, place in outs.values() if place == Place.FAR]

    def kernel(*refs):
        at = 0

        def take(count):
            nonlocal at
            at += count
            return list(refs[at - count : at])

        scalar_refs, sources, targets = take(len(scalars)), take(len(arrays)), take(len(outs))
        in_bufs, out_bufs = take(len(fetched)), take(len(pushed))
        in_sems, out_sems = take(2)
        ins, results, fetches, pushes, queue = {}, {}, [], [], Queue()
        for source, (key, (unused, place)) in zip(sources, arrays.items()):
            if place in (Place.FAR, Place.FEW):
                sem = in_sems.at[len(fetches)]
                fetches.append(Fetch(source, in_bufs[len(fetches)], sem, queue))
                ins[key] = fetches[-1]
            else:
                ins[key] = Here(source)
        queue.waiting = list(fetches)
        queue.advance(None)
        for target, (key, (unused, unused, place)) in zip(targets, outs.items()):
            if place == Place.FAR:
                pushes.append(Push(out_bufs[len(pushes)], target, out_sems.at[len(pushes)]))
            results[key] = pushes[-1] if place == Place.FAR else Here(target)
        body(scalar_refs, ins, results, take(len(scratch)))
        for push in pushes:
            if not push.started:
                push.push()
        for fetch in fetches:
            fetch.get()
        for push in pushes:
            push.copy.wait()

    where = {Place.FAR: hbm, Place.FEW: hbm, Place.RAW: hbm, Place.AUTO: vmem, Place.SCALAR: smem}
    buffers = [
        (pltpu.SMEM if place == Place.FEW else pltpu.VMEM)(array.shape, array.dtype)
        for array, place in fetched
    ]
    buffers += [pltpu.VMEM(shape, kind) for shape, kind in pushed]
    buffers += [pltpu.SemaphoreType.DMA((max(len(group), 1),)) for group in (fetched, pushed)]
    pinned = [
        array if place == Place.AUTO else pltpu.with_memory_space_constraint(array, pltpu.HBM)
        for array, place in arrays.values()
    ]
    results = pl.pallas_call(
        kernel,
        name=name,
        out_shape=[
            (pltpu.HBM if place == Place.FAR else jax.ShapeDtypeStruct)(shape, kind)
            for shape, kind, place in outs.values()
        ],
        in_specs=[smem] * len(scalars) + [where[place] for unused, place in arrays.values()],
        out_specs=[where[place] for unused, unused, place in outs.values()],
        scratch_shapes=buffers + scratch,
        compiler_params=pltpu.CompilerParams(vmem_limit_bytes=LIMIT),
    )(*scalars, *pinned)
    return dict(zip(outs, results))


def exchange(array):
    return lax.all_to_all(array, "dp", split_axis=0, concat_axis=0, tiled=True)


def exchange_by_core(array, devices):
    groups = [list(range(core, devices, 2)) for core in range(2)]
    return lax.all_to_all(
        array, "dp", split_axis=0, concat_axis=0, tiled=True, axis_index_groups=groups
    )


def swap(array, devices):
    return lax.ppermute(array, "dp", [(i, i ^ 1) for i in range(devices)])


def compact(
    text_input, eot_index, image_input, ln1_gain, ln1_bias, w_qkv, w_attn_out, ln2_gain, ln2_bias,
    w_fc, w_fc_out, img_ln1_gain, img_ln1_bias, img_w_qkv, img_w_attn_out, img_ln2_gain,
    img_ln2_bias, img_w_fc, img_w_fc_out, final_gain, final_bias, text_proj, image_gain,
    image_bias, image_proj, logit_scale,
):
    caps, seq, dim = text_input.shape
    img_seq = image_input.shape[1]
    devices = lax.axis_size("dp")
    plan = Plan(dim, w_fc.shape[2], devices)
    heads = dim // HEAD_DIM
    count = devices * caps
    hidden = plan.hidden
    device = lax.axis_index("dp").astype(jnp.int32).reshape(1)
    text_input, image_input = text_input.swapaxes(0, 1), image_input.swapaxes(0, 1)
    totals = caps * seq, caps * img_seq
    chips = devices // 2
    width = heads * LANES

    first = {
        (K.X, 0): text_input, (K.X, 1): image_input,
        (K.GAIN, 0): ln1_gain, (K.BIAS, 0): ln1_bias,
        (K.GAIN, 1): img_ln1_gain, (K.BIAS, 1): img_ln1_bias,
        (K.W_QKV, 0): w_qkv, (K.W_QKV, 1): img_w_qkv,
    }
    second = {
        (K.W_OUT, 0): w_attn_out, (K.W_OUT, 1): img_w_attn_out,
        (K.GAIN2, 0): ln2_gain, (K.BIAS2, 0): ln2_bias,
        (K.GAIN2, 1): img_ln2_gain, (K.BIAS2, 1): img_ln2_bias,
        (K.W_FC, 0): w_fc, (K.W_FC_OUT, 0): w_fc_out,
        (K.W_FC, 1): img_w_fc, (K.W_FC_OUT, 1): img_w_fc_out,
        (K.HEAD_GAIN, 0): final_gain, (K.HEAD_BIAS, 0): final_bias,
        (K.HEAD_GAIN, 1): image_gain, (K.HEAD_BIAS, 1): image_bias,
        (K.PROJ, 0): text_proj, (K.PROJ, 1): image_proj,
    }

    def far(arrays):
        return {key: (array, Place.FAR) for key, array in arrays.items()}

    eot = {K.EOT: (eot_index, Place.FEW)}
    rows = run(
        front_body(plan),
        "front",
        {K.ROWS: ((chips, caps, 4 * dim), BF16, Place.AUTO)},
        [],
        [],
        eot | far(first),
    )[K.ROWS]
    mine = exchange_by_core(rows, devices)

    unused, pack_rows = pack_at(dim, hidden, caps)
    side_outs = {K.VALUES: ((devices, caps, width), BF16, Place.FAR)}
    middle_outs = {
        K.SEND: ((devices, caps, width + dim + LANES), BF16, Place.AUTO),
        K.ROWS: ((count, 4 * dim), BF16, Place.FAR),
    }
    for tower, total in enumerate(totals):
        side_outs |= {
            (K.NORMED, tower): ((total, dim), BF16, Place.FAR),
            (K.UNIT, tower): ((total, dim), BF16, Place.FAR),
            (K.PROBS, tower): ((heads * caps, total), F32, Place.FAR),
            (K.PACK, tower): ((pack_rows, dim), F32, Place.FAR),
        }
        middle_outs |= {
            (K.OWN, tower): ((2, caps, dim), F32, Place.FAR),
            (K.SCORES, tower): ((heads * caps, total), BF16, Place.FAR),
            (K.QUERY, tower): ((caps, dim), BF16, Place.FAR),
        }
    side = run(side_body(plan), "side", side_outs, [], [], eot | far(first) | far(second))
    values = exchange(side.pop(K.VALUES))
    mine, side[K.PACK, 0] = lax.optimization_barrier((mine, side[K.PACK, 0]))
    others = swap(mine, devices)

    late = {(K.W_QKV, 0): w_qkv, (K.W_QKV, 1): img_w_qkv}
    packs = {key: side[key] for key in ((K.PACK, 0), (K.PACK, 1))}
    middle = run(
        middle_body(plan),
        "middle",
        middle_outs,
        [pltpu.VMEM((chips, 2, caps, 4 * dim), BF16), pltpu.SemaphoreType.DMA((2,))],
        [device, logit_scale],
        {K.MINE: (mine, Place.AUTO), K.OTHERS: (others, Place.AUTO)}
        | far(second)
        | far(packs)
        | far(late)
        | far({(name, tower): side[name, tower] for name in (K.NORMED, K.PROBS, K.UNIT) for tower in (0, 1)}),
    )
    send, values = lax.optimization_barrier((middle[K.SEND], values))
    sent = exchange(send)

    share_rows = plan.rows_out
    region = (plan.total - plan.out_at) // LANES
    head_region = plan.head_total // LANES
    tail_ins = eot | far(first)
    tail_outs = {K.LOSS: ((1,), F32, Place.SCALAR), K.SCALE: ((1,), F32, Place.SCALAR)}
    for tower, length in enumerate((seq, img_seq)):
        for name, source in (
            (K.PROBS, side), (K.PACK, side), (K.OWN, middle), (K.SCORES, middle), (K.QUERY, middle)
        ):
            tail_ins |= far({(name, tower): source[name, tower]})
        tail_outs |= {
            (K.PART, tower): ((share_rows, LANES), F32, Place.FAR),
            (K.MIXED, tower): ((count, dim), BF16, Place.FAR),
            (K.INPUT, tower): ((length, caps, dim), F32, Place.FAR),
        }
    tail_outs |= {
        K.HEAD: ((plan.head_rows_out, LANES), F32, Place.FAR),
        K.WINDOWS: ((count, LANES), BF16, Place.FAR),
        K.QUERIES: ((count, 2 * dim), BF16, Place.FAR),
        K.BIAS: ((8, dim), F32, Place.FAR),
    }
    tail = run(
        tail_body(plan),
        "tail",
        tail_outs,
        [
            pltpu.VMEM((region + 2 * share_rows + 8, LANES), F32),
            pltpu.VMEM((head_region + plan.head_rows_out + 8, LANES), F32),
            pltpu.VMEM((totals[0], dim), F32),
            pltpu.VMEM((totals[1], dim), F32),
            pltpu.VMEM((count, hidden), BF16),
            pltpu.VMEM((8, dim), F32),
            pltpu.VMEM((count, hidden), F32),
            pltpu.VMEM((count, hidden), F32),
            pltpu.VMEM((count, hidden), BF16),
            pltpu.VMEM((count, hidden), BF16),
        ],
        [device, logit_scale],
        tail_ins | far({K.ROWS: middle[K.ROWS]} | second),
    )
    sent, tail[K.BIAS] = lax.optimization_barrier((sent, tail[K.BIAS]))
    swapped = swap(sent, devices)
    flat_rows = 2 * dim // LANES + max(WINDOW * plan.row, 2 * plan.row + share_rows * LANES) // LANES
    names = [(K.PART, 0), (K.PART, 1), K.WINDOWS, K.QUERIES, K.BIAS, (K.MIXED, 0), (K.MIXED, 1)]
    shares = run(
        last_body(plan),
        "last",
        {(K.SHARE, tower): ((1, plan.share), F32, Place.FAR) for tower in (0, 1)},
        [
            pltpu.VMEM((2, flat_rows // 8 * 8 + 16, LANES), F32),
            pltpu.VMEM((2, dim, dim), BF16),
            pltpu.VMEM((count, 2 * dim), BF16),
            pltpu.SemaphoreType.DMA((2,)),
        ],
        [device],
        far({name: tail[name] for name in names} | {K.VALUES: values.reshape(count, width)})
        | {key: (array.reshape(count, -1), Place.AUTO) for key, array in ((K.SENT, sent), (K.SWAPPED, swapped))}
        | {key: (array, Place.RAW) for key, array in late.items()},
    )

    def cut(array, size):
        return array.reshape(-1)[:size]

    return (
        tail[K.LOSS],
        tail[K.INPUT, 0].swapaxes(0, 1),
        tail[K.INPUT, 1].swapaxes(0, 1),
        shares[K.SHARE, 0],
        shares[K.SHARE, 1],
        cut(tail[K.HEAD], plan.head_share),
        tail[K.SCALE],
    )


def norm_apply(values, gain, bias):
    center = values - jnp.mean(values, -1, keepdims=True)
    spread = jnp.mean(center * center, -1, keepdims=True)
    return center * lax.rsqrt(spread + EPS) * gain + bias


def quick_gelu(values):
    return values * jax.nn.sigmoid(1.702 * values)


def unit_rows(values):
    return values * lax.rsqrt(jnp.sum(values * values, -1, keepdims=True) + UNIT_EPS)


def causal_mask(seq_len):
    row_pos = lax.broadcasted_iota(jnp.int32, (seq_len, seq_len), 0)
    col_pos = lax.broadcasted_iota(jnp.int32, (seq_len, seq_len), 1)
    return col_pos <= row_pos


def matmul(left, right):
    return jnp.dot(left, right, preferred_element_type=jnp.float32)


def inner_rows(left, right):
    return lax.dot_general(
        left, right, (((0,), (0,)), ((), ())), preferred_element_type=jnp.float32
    )


def outer_cols(left, right):
    return lax.dot_general(
        left, right, (((1,), (1,)), ((), ())), preferred_element_type=jnp.float32
    )


def layer_forward(stream, weights, causal):
    gain_one, bias_one, w_qkv, w_out, gain_two, bias_two, w_fc, w_fc_out = weights
    num_caps, seq_len, feat_dim = stream.shape
    num_heads = feat_dim // HEAD_DIM
    num_rows = num_caps * seq_len
    normed_one = (
        norm_apply(stream, gain_one, bias_one).astype(jnp.bfloat16).reshape(num_rows, feat_dim)
    )
    packed = (
        matmul(normed_one, w_qkv)
        .astype(jnp.bfloat16)
        .reshape(num_caps, seq_len, 3, num_heads, HEAD_DIM)
    )
    queries = packed[:, :, 0]
    key_rows = packed[:, :, 1]
    value_rows = packed[:, :, 2]
    raw_score = jnp.einsum("bqhd,bkhd->bhqk", queries, key_rows, preferred_element_type=jnp.float32)
    scores = raw_score * HEAD_DIM ** (-0.5)
    if causal:
        scores = jnp.where(causal_mask(seq_len), scores, MASKED)
    row_peak = jnp.max(scores, -1, keepdims=True)
    log_total = row_peak + jnp.log(jnp.sum(jnp.exp(scores - row_peak), -1, keepdims=True))
    attn_probs = jnp.exp(scores - log_total)
    probs_low = attn_probs.astype(jnp.bfloat16)
    mixed_rows = jnp.einsum(
        "bhqk,bkhd->bqhd", probs_low, value_rows, preferred_element_type=jnp.float32
    )
    mixed_rows = mixed_rows.astype(jnp.bfloat16).reshape(num_rows, feat_dim)
    middle = stream + matmul(mixed_rows, w_out).reshape(num_caps, seq_len, feat_dim)
    normed_two = (
        norm_apply(middle, gain_two, bias_two).astype(jnp.bfloat16).reshape(num_rows, feat_dim)
    )
    hidden = matmul(normed_two, w_fc)
    active = quick_gelu(hidden).astype(jnp.bfloat16)
    result = middle + matmul(active, w_fc_out).reshape(num_caps, seq_len, feat_dim)
    return (
        result,
        (normed_one, packed, attn_probs, probs_low, mixed_rows, middle, normed_two, hidden, active),
    )


def layer_backward(stream, weights, grad_out, causal):
    gain_one, bias_one, w_qkv, w_out, gain_two, bias_two, w_fc, w_fc_out = weights
    num_caps, seq_len, feat_dim = stream.shape
    num_heads = feat_dim // HEAD_DIM
    num_rows = num_caps * seq_len
    unused, kept = layer_forward(stream, weights, causal)
    normed_one, packed, attn_probs, probs_low, mixed_rows, middle, normed_two, hidden, active = kept
    grad_low = grad_out.reshape(num_rows, feat_dim).astype(jnp.bfloat16)
    grad_fc_out = inner_rows(active, grad_low)
    grad_active = outer_cols(grad_low, w_fc_out)
    unused_gelu, gelu_back = jax.vjp(quick_gelu, hidden)
    grad_hidden = gelu_back(grad_active)[0].astype(jnp.bfloat16)
    grad_fc = inner_rows(normed_two, grad_hidden)
    grad_normed_two = outer_cols(grad_hidden, w_fc)
    unused_two, norm_back_two = jax.vjp(norm_apply, middle, gain_two, bias_two)
    grad_mid_norm, grad_gain_two, grad_bias_two = norm_back_two(
        grad_normed_two.reshape(num_caps, seq_len, feat_dim)
    )
    grad_middle = grad_out + grad_mid_norm
    middle_low = grad_middle.reshape(num_rows, feat_dim).astype(jnp.bfloat16)
    grad_w_out = inner_rows(mixed_rows, middle_low)
    grad_mixed = (
        outer_cols(middle_low, w_out)
        .astype(jnp.bfloat16)
        .reshape(num_caps, seq_len, num_heads, HEAD_DIM)
    )
    queries = packed[:, :, 0]
    key_rows = packed[:, :, 1]
    value_rows = packed[:, :, 2]
    grad_values = jnp.einsum(
        "bhqk,bqhd->bkhd", probs_low, grad_mixed, preferred_element_type=jnp.float32
    )
    grad_probs = jnp.einsum(
        "bqhd,bkhd->bhqk", grad_mixed, value_rows, preferred_element_type=jnp.float32
    )
    row_inner = jnp.sum(attn_probs * grad_probs, -1, keepdims=True)
    grad_raw = (attn_probs * (grad_probs - row_inner) * HEAD_DIM ** (-0.5)).astype(jnp.bfloat16)
    grad_queries = jnp.einsum(
        "bhqk,bkhd->bqhd", grad_raw, key_rows, preferred_element_type=jnp.float32
    )
    grad_keys = jnp.einsum("bhqk,bqhd->bkhd", grad_raw, queries, preferred_element_type=jnp.float32)
    grad_packed = (
        jnp.stack([grad_queries, grad_keys, grad_values], 2)
        .astype(jnp.bfloat16)
        .reshape(num_rows, 3 * feat_dim)
    )
    grad_qkv = inner_rows(normed_one, grad_packed)
    grad_normed_one = outer_cols(grad_packed, w_qkv)
    unused_one, norm_back_one = jax.vjp(norm_apply, stream, gain_one, bias_one)
    grad_in_norm, grad_gain_one, grad_bias_one = norm_back_one(
        grad_normed_one.reshape(num_caps, seq_len, feat_dim)
    )
    grads_here = [
        grad_gain_one,
        grad_bias_one,
        grad_qkv,
        grad_w_out,
        grad_gain_two,
        grad_bias_two,
        grad_fc,
        grad_fc_out,
    ]
    return (grad_middle + grad_in_norm, grads_here)


def head_forward(features, gain, bias, proj):
    normed = norm_apply(features, gain, bias).astype(jnp.bfloat16)
    embedded = matmul(normed, proj)
    return (unit_rows(embedded), (normed, embedded))


def head_backward(features, gain, bias, proj, kept, grad_unit):
    normed, embedded = kept
    unused_unit, unit_back = jax.vjp(unit_rows, embedded)
    grad_embed = unit_back(grad_unit)[0].astype(jnp.bfloat16)
    grad_proj = inner_rows(normed, grad_embed)
    grad_normed = outer_cols(grad_embed, proj)
    unused_norm, norm_back = jax.vjp(norm_apply, features, gain, bias)
    grad_feat, grad_gain, grad_bias = norm_back(grad_normed)
    return (grad_feat, [grad_gain, grad_bias, grad_proj])


def plain_contrast(own_rows, other_rows, multiplier, start):
    logits = multiplier * outer_cols(own_rows, other_rows)
    row_peak = jnp.max(logits, -1, keepdims=True)
    log_total = row_peak + jnp.log(jnp.sum(jnp.exp(logits - row_peak), -1, keepdims=True))
    col_pos = lax.broadcasted_iota(jnp.int32, logits.shape, 1)
    target_pos = lax.broadcasted_iota(jnp.int32, logits.shape, 0) + start
    matched = (col_pos == target_pos).astype(jnp.float32)
    loss_sum = jnp.sum(log_total) - jnp.sum(matched * logits)
    grad_logits = 0.5 * (jnp.exp(logits - log_total) - matched)
    scale_part = jnp.sum(grad_logits * logits)
    return (loss_sum, scale_part, (multiplier * grad_logits).astype(jnp.bfloat16), log_total[:, 0])


def pack_flat(arrays, devices):
    flat = jnp.concatenate([array.reshape(-1) for array in arrays])
    padding = -flat.shape[0] % devices
    return jnp.concatenate([flat, jnp.zeros((padding,), jnp.float32)])


def plain(
    text_input,
    eot_index,
    image_input,
    ln1_gain,
    ln1_bias,
    w_qkv,
    w_attn_out,
    ln2_gain,
    ln2_bias,
    w_fc,
    w_fc_out,
    img_ln1_gain,
    img_ln1_bias,
    img_w_qkv,
    img_w_attn_out,
    img_ln2_gain,
    img_ln2_bias,
    img_w_fc,
    img_w_fc_out,
    final_gain,
    final_bias,
    text_proj,
    image_gain,
    image_bias,
    image_proj,
    logit_scale,
):
    num_caps, seq_len, feat_dim = text_input.shape
    devices = lax.axis_size("dp")
    all_caps = num_caps * devices
    start = lax.axis_index("dp") * num_caps
    depth = ln1_gain.shape[0]
    text_stack = (ln1_gain, ln1_bias, w_qkv, w_attn_out, ln2_gain, ln2_bias, w_fc, w_fc_out)
    image_stack = (
        img_ln1_gain,
        img_ln1_bias,
        img_w_qkv,
        img_w_attn_out,
        img_ln2_gain,
        img_ln2_bias,
        img_w_fc,
        img_w_fc_out,
    )

    def text_weights(layer_num):
        return tuple((array[layer_num] for array in text_stack))

    def image_weights(layer_num):
        return tuple((array[layer_num] for array in image_stack))

    stream = text_input.astype(jnp.float32)
    layer_num = 0
    text_saved = [stream]
    stream, unused = layer_forward(stream, text_weights(layer_num), True)
    pooled = jnp.take_along_axis(stream, eot_index[:, None, None], axis=1)[:, 0]
    picture = image_input.astype(jnp.float32)
    layer_num = 0
    image_saved = [picture]
    picture, unused = layer_forward(picture, image_weights(layer_num), False)
    image_pooled = picture[:, 0]
    text_unit, text_kept = head_forward(pooled, final_gain, final_bias, text_proj)
    image_unit, image_kept = head_forward(image_pooled, image_gain, image_bias, image_proj)
    image_low = image_unit.astype(jnp.bfloat16)
    text_low = text_unit.astype(jnp.bfloat16)
    image_all, text_all = (
        lax.all_gather(image_low, "dp", axis=0, tiled=True),
        lax.all_gather(text_low, "dp", axis=0, tiled=True),
    )
    multiplier = jnp.exp(logit_scale[0])
    loss_image, scale_image, grad_raw_it, unused_it = plain_contrast(
        image_low, text_all, multiplier, start
    )
    loss_text, scale_text, grad_raw_ti, unused_ti = plain_contrast(text_low, image_all, multiplier, start)
    spread_text = inner_rows(grad_raw_it, image_low)
    spread_image = inner_rows(grad_raw_ti, text_low)
    back_text, back_image = (
        lax.psum_scatter(spread_text, "dp", scatter_dimension=0, tiled=True),
        lax.psum_scatter(spread_image, "dp", scatter_dimension=0, tiled=True),
    )
    total, grad_scale = lax.psum((loss_image + loss_text, scale_image + scale_text), "dp")
    grad_image_unit = matmul(grad_raw_it, text_all) + back_image
    grad_text_unit = matmul(grad_raw_ti, image_all) + back_text
    grad_pooled, text_head_grads = head_backward(
        pooled, final_gain, final_bias, text_proj, text_kept, grad_text_unit
    )
    grad_image_pooled, image_head_grads = head_backward(
        image_pooled, image_gain, image_bias, image_proj, image_kept, grad_image_unit
    )
    head_flat = pack_flat(text_head_grads + image_head_grads, devices)
    image_flat = [None] * depth
    img_seq = image_input.shape[1]
    img_dim = image_input.shape[2]
    grad_picture = jnp.concatenate(
        [grad_image_pooled[:, None, :], jnp.zeros((num_caps, img_seq - 1, img_dim), jnp.float32)], 1
    )
    for layer_num in reversed(range(depth)):
        grad_picture, grads_here = layer_backward(
            image_saved[layer_num], image_weights(layer_num), grad_picture, False
        )
        image_flat[layer_num] = pack_flat(grads_here, devices)
    text_flat = [None] * depth
    selected = (
        lax.broadcasted_iota(jnp.int32, (num_caps, seq_len), 1) == eot_index[:, None]
    ).astype(jnp.float32)
    grad_stream = selected[:, :, None] * grad_pooled[:, None, :]
    for layer_num in reversed(range(depth)):
        grad_stream, grads_here = layer_backward(
            text_saved[layer_num], text_weights(layer_num), grad_stream, True
        )
        text_flat[layer_num] = pack_flat(grads_here, devices)
    text_share, image_share, head_share = (
        lax.psum_scatter(jnp.stack(text_flat), "dp", scatter_dimension=1, tiled=True),
        lax.psum_scatter(jnp.stack(image_flat), "dp", scatter_dimension=1, tiled=True),
        lax.psum_scatter(head_flat, "dp", scatter_dimension=0, tiled=True),
    )
    loss = (total / (2 * all_caps)).reshape(1)
    return (
        loss,
        grad_stream,
        grad_picture,
        text_share,
        image_share,
        head_share,
        grad_scale.reshape(1),
    )


def shards(*args):
    caps = args[0].shape[0] * lax.axis_size("dp")
    return compact(*args) if caps <= 512 else plain(*args)


def solution(mesh):
    return jax.shard_map(
        shards,
        mesh=mesh,
        in_specs=(
            P("dp", None, None),
            P("dp"),
            P("dp", None, None),
            P(),
            P(),
            P(),
            P(),
            P(),
            P(),
            P(),
            P(),
            P(),
            P(),
            P(),
            P(),
            P(),
            P(),
            P(),
            P(),
            P(),
            P(),
            P(),
            P(),
            P(),
            P(),
            P(),
        ),
        out_specs=(
            P(),
            P("dp", None, None),
            P("dp", None, None),
            P(None, "dp"),
            P(None, "dp"),
            P("dp"),
            P(),
        ),
        check_vma=False,
    )
```

profile of v0, /device:TPU:0, one launch (start us, length us, event | category | flops | bytes accessed | tf_op | source)
XLA Modules:
  0.0 72.6 jit_solution(15055021816905311573)
XLA Ops:
  0.6 4.2 %front.1 = bf16[16,8,1536]{2,1,0:T(8,128)(2,1)} custom-call(s32[8]{0:T(128)} %refs_2_.1, bf16[77,8,384]{2,1,0:T(8,128)(2,1)} %bitcast.12, bf16[50,8,384]{2,1,0:T(8,128)(2,1)} %bitcast.15, f32[1,384]{1,0:T(1,128)} %refs_5_.7, f32[1,384]{1,0:T(1,128)} %refs_6_.7, f32[1,384]{1,0:T(1,128)} %refs_7_.7, f32[1,384]{1,0:T(1,128)} %refs_8_.7, ...), custom_call_target="tpu_custom_call" | custom-call | tf_op jit(solution)/shard_map/front/pallas_call | solution.py:901
  4.8 8.3 %all-to-all-start = ((bf16[16,8,1536]{2,1,0:T(8,128)(2,1)}), bf16[16,8,1536]{2,1,0:T(8,128)(2,1)S(1)}, u32[]{:S(2)}, u32[]{:S(2)}) async-start(bf16[16,8,1536]{2,1,0:T(8,128)(2,1)} %front.1), calls=%async_computation | async-start | bytes 786432 | tf_op jit(solution)/shard_map/all_to_all | solution.py:922
  13.2 7.2 %side.1 = (bf16[32,8,768]{2,1,0:T(8,128)(2,1)}, bf16[616,384]{1,0:T(8,128)(2,1)}, bf16[616,384]{1,0:T(8,128)(2,1)}, f32[48,616]{1,0:T(8,128)}, f32[168,384]{1,0:...) custom-call(s32[8]{0:T(128)} %refs_2_.1, ...), custom_call_target="tpu_custom_call" | custom-call | tf_op jit(solution)/shard_map/side/pallas_call | solution.py:901
  20.4 5.4 %all-to-all-done.refs_2_ = bf16[16,8,1536]{2,1,0:T(8,128)(2,1)S(1)} async-done(((bf16[16,8,1536]{2,1,0:T(8,128)(2,1)}), bf16[16,8,1536]{2,1,0:T(8,128)(2,1)S(1)}, u32[]{:S(2)}, u32[]{:S(2)}) %all-to-all-start) | async-done | bytes 393248 | tf_op jit(solution)/shard_map/all_to_all | solution.py:922
  25.8 2.6 %all-to-all-start.1 = ((bf16[32,8,768]{2,1,0:T(8,128)(2,1)}), bf16[32,8,768]{2,1,0:T(8,128)(2,1)S(1)}, u32[]{:S(2)}, u32[]{:S(2)}) async-start(bf16[32,8,768]{2,1,0:T(8,128)(2,1)} %get-tuple-element.69), calls=%async_computation.1 | async-start | bytes 786432 | tf_op jit(solution)/shard_map/all_to_all | solution.py:917
  28.4 0.3 collective-permute-start
  29.3 0.8 %collective-permute-done.refs_3_ = bf16[16,8,1536]{2,1,0:T(8,128)(2,1)S(1)} collective-permute-done((bf16[16,8,1536]{2,1,0:T(8,128)(2,1)S(1)}, bf16[16,8,1536]{2,1,0:T(8,128)(2,1)S(1)}, u32[]{:S(2)}, u32[]{:S(2)}) %collective-permute-start) | collective-permute-done | bytes 393248 | tf_op jit(solution)/shard_map/ppermute | solution.py:928
  30.2 12.5 %middle.1 = (bf16[32,8,1280]{2,1,0:T(8,128)(2,1)}, bf16[256,1536]{1,0:T(8,128)(2,1)}, f32[2,8,384]{2,1,0:T(8,128)}, bf16[48,616]{1,0:T(8,128)(2,1)}, bf16[8,384]...) custom-call(s32[1]{0:T(128)} %bitcast.refs_0_, f32[1]{0:T(128)S(6)} %copy.33.refs_1_, ...), custom_call_target="tpu_custom_call" | custom-call | tf_op jit(solution)/shard_map/middle/pallas_call | solution.py:901
  42.7 0.0 all-to-all-done.1
  42.7 0.0 copy-start
  42.8 6.0 %all-to-all-start.2 = ((bf16[32,8,1280]{2,1,0:T(8,128)(2,1)}), bf16[32,8,1280]{2,1,0:T(8,128)(2,1)S(1)}, u32[]{:S(2)}, u32[]{:S(2)}) async-start(bf16[32,8,1280]{2,1,0:T(8,128)(2,1)} %get-tuple-element.70), calls=%async_computation.2 | async-start | bytes 1310720 | tf_op jit(solution)/shard_map/all_to_all | solution.py:917
  48.8 17.6 %tail.1 = (f32[1]{0:T(128)}, f32[1]{0:T(128)}, f32[440,128]{1,0:T(8,128)}, bf16[256,384]{1,0:T(8,128)(2,1)}, f32[77,8,384]{2,1,0:T(8,128)}, /*index=5*/f32[440,1...) custom-call(s32[1]{0:T(128)} %bitcast.refs_0_, ...), custom_call_target="tpu_custom_call" | custom-call | tf_op jit(solution)/shard_map/tail/pallas_call | solution.py:901
  66.4 0.0 copy-done
  66.4 0.1 all-to-all-done.2
  66.5 0.1 collective-permute-start.1
  66.6 2.0 %collective-permute-done.1 = bf16[32,8,1280]{2,1,0:T(8,128)(2,1)S(1)} collective-permute-done((bf16[32,8,1280]{2,1,0:T(8,128)(2,1)S(1)}, bf16[32,8,1280]{2,1,0:T(8,128)(2,1)S(1)}, u32[]{:S(2)}, u32[]{:S(2)}) %collective-permute-start.1) | collective-permute-done | bytes 655392 | tf_op jit(solution)/shard_map/ppermute | solution.py:928
  68.6 3.9 %last.1 = (f32[1,55344]{1,0:T(1,128)}, f32[1,55344]{1,0:T(1,128)}) custom-call(s32[1]{0:T(128)} %bitcast.refs_0_, f32[440,128]{1,0:T(8,128)} %get-tuple-element.64.refs_1_, f32[440,128]{1,0:T(8,128)} %get-tuple-element.65.refs_2_, bf16[256,128]{1,0:T(8,128)(2,1)} %get-tuple-element.66.refs_3_, bf16[256,768]{1,0:T(8,128)(2,1)} %get-tuple-element.67.refs_4_, ...), custom_call_target="tpu_custom_call" | custom-call | tf_op jit(solution)/shard_map/last/pallas_call | solution.py:901
Async XLA Ops:
  4.8 21.0 %all-to-all-start = ((bf16[16,8,1536]{2,1,0:T(8,128)(2,1)}), bf16[16,8,1536]{2,1,0:T(8,128)(2,1)S(1)}, u32[]{:S(2)}, u32[]{:S(2)}) async-start(bf16[16,8,1536]{2,1,0:T(8,128)(2,1)} %front.1), calls=%async_computation | async-start | bytes 786432 | tf_op jit(solution)/shard_map/all_to_all | solution.py:922
  25.8 16.9 %all-to-all-start.1 = ((bf16[32,8,768]{2,1,0:T(8,128)(2,1)}), bf16[32,8,768]{2,1,0:T(8,128)(2,1)S(1)}, u32[]{:S(2)}, u32[]{:S(2)}) async-start(bf16[32,8,768]{2,1,0:T(8,128)(2,1)} %get-tuple-element.69), calls=%async_computation.1 | async-start | bytes 786432 | tf_op jit(solution)/shard_map/all_to_all | solution.py:917
  28.4 1.8 %collective-permute-start = (bf16[16,8,1536]{2,1,0:T(8,128)(2,1)S(1)}, bf16[16,8,1536]{2,1,0:T(8,128)(2,1)S(1)}, u32[]{:S(2)}, u32[]{:S(2)}) collective-permute-start(bf16[16,8,1536]{2,1,0:T(8,128)(2,1)S(1)} %all-to-all-done.refs_2_), channel_id=1, source_target_pairs={{0,1},{1,0},{2,3},{3,2},{4,5},{5,4},{6,7},{7,6},{8,9},{9,8},{10,11... | collective-permute-start | bytes 1179656 | tf_op jit(solution)/shard_map/ppermute | solution.py:928
  42.7 23.7 %copy-start = (bf16[32,8,768]{2,1,0:T(8,128)(2,1)}, bf16[32,8,768]{2,1,0:T(8,128)(2,1)S(1)}, u32[]{:S(2)}) copy-start(bf16[32,8,768]{2,1,0:T(8,128)(2,1)S(1)} %all-to-all-done.1) | copy-start | bytes 1179652
  42.8 23.8 %all-to-all-start.2 = ((bf16[32,8,1280]{2,1,0:T(8,128)(2,1)}), bf16[32,8,1280]{2,1,0:T(8,128)(2,1)S(1)}, u32[]{:S(2)}, u32[]{:S(2)}) async-start(bf16[32,8,1280]{2,1,0:T(8,128)(2,1)} %get-tuple-element.70), calls=%async_computation.2 | async-start | bytes 1310720 | tf_op jit(solution)/shard_map/all_to_all | solution.py:917
  66.5 2.1 %collective-permute-start.1 = (bf16[32,8,1280]{2,1,0:T(8,128)(2,1)S(1)}, bf16[32,8,1280]{2,1,0:T(8,128)(2,1)S(1)}, u32[]{:S(2)}, u32[]{:S(2)}) collective-permute-start(bf16[32,8,1280]{2,1,0:T(8,128)(2,1)S(1)} %all-to-all-done.2), channel_id=1, source_target_pairs={{0,1},{1,0},{2,3},{3,2},{4,5},{5,4},{6,7},{7,6},{8,9},{9,8},{10,11... | collective-permute-start | bytes 1966088 | tf_op jit(solution)/shard_map/ppermute | solution.py:928
where the time goes:
time: 73.1 us; the launch traced here: 72.6 us
  Pallas kernels  45.4 us (62%)
  starting transfers between devices  17.3 us (24%)
  waiting for transfers between devices  8.4 us (11%)
  between operations  1.55 us (2%)
    pallas_call x5, Pallas kernels, run(): pl.pallas_call(kernel, name=name, out_shape=[(pltpu.HBM if place == Place...  45.4 us
    all_to_all x2, starting transfers between devices, exchange(): return lax.all_to_all(array, 'dp', split_axis=0, concat_axis=0, tiled=True)  8.61 us
    all_to_all x1, starting transfers between devices, exchange_by_core(): lax.all_to_all(array, 'dp', split_axis=0, concat_axis=0, tiled=True, axis...  8.32 us
    all_to_all x1, waiting for transfers between devices, exchange_by_core(): lax.all_to_all(array, 'dp', split_axis=0, concat_axis=0, tiled=True, axis...  5.42 us
    ppermute x2, waiting for transfers between devices, swap(): return lax.ppermute(array, 'dp', [(i, i ^ 1) for i in range(devices)])  2.87 us
  transfers between devices with their start and end apart: 5, of which 4 were waited for; matrix products, arithmetic and copies ran while one was open for 0% of the time, Pallas kernels for 51%

commit v1 on v0

--- a/solution.py
+++ b/solution.py
@@ -9,13 +9,11 @@
 
 HEAD_DIM = 64
 LANES = 128
-WINDOW = 64
 
 EPS = 1e-05
 UNIT_EPS = 1e-06
 MASKED = -1000000000.0
 LIMIT = 44 * 2**20
-IN_FLIGHT = 64 * 2**20
 F32 = jnp.float32
 BF16 = jnp.bfloat16
 
@@ -49,7 +47,6 @@
     PROBS = enum.auto()
     PROJ = enum.auto()
     QUERIES = enum.auto()
-    QUERY = enum.auto()
     ROWS = enum.auto()
     SCALE = enum.auto()
     SCORES = enum.auto()
@@ -137,7 +134,11 @@
         self.roots = -(-self.out_at // self.share)
         self.rows_out = -(-(self.share // LANES + 2) // 8) * 8
         self.head_rows_out = -(-(self.head_share // LANES + 2) // 8) * 8
-        assert self.share // self.row + 2 <= WINDOW
+        self.window = self.share // self.row + 2
+        self.pad = -(-self.window // 8) * 8
+        self.used = self.pad + self.window
+        self.piece = LANES - self.used
+        assert self.piece > 0 and -(-self.used // self.piece) < dim // HEAD_DIM
         assert self.total % devices == 0 and self.head_total % devices == 0
 
     def column(self, device):
@@ -151,14 +152,29 @@
     first = plan.column(device)
     lane = lax.broadcasted_iota(jnp.int32, (text.shape[0], LANES), 1)
     left = pltpu.roll(text, (dim - first) % dim, 1)[:, :LANES]
-    right = pltpu.roll(image, (dim - first + WINDOW) % dim, 1)[:, :LANES]
-    both = jnp.where(lane < WINDOW, left, right).astype(BF16)
+    right = pltpu.roll(image, (dim - first + plan.pad) % dim, 1)[:, :LANES]
+    both = jnp.where(lane < plan.pad, left, right)
     heads = text.shape[0] // caps
-    return jnp.concatenate([both[h * caps : (h + 1) * caps] for h in range(heads)], 1)
+    lane, last = lane[:caps], both[(heads - 1) * caps :]
+    tiles = []
+    for h in range(heads - 1):
+        moved = pltpu.roll(last, (plan.used - h * plan.piece) % LANES, 1)
+        tiles.append(jnp.where(lane < plan.used, both[h * caps : (h + 1) * caps], moved).astype(BF16))
+    return jnp.concatenate(tiles, 1)
+
+
+def last_head(plan, source, heads):
+    lane = lax.broadcasted_iota(jnp.int32, (source.shape[0], LANES), 1)
+    whole = jnp.zeros(lane.shape, F32)
+    for h in range(-(-plan.used // plan.piece)):
+        tile = source[:, h * LANES : (h + 1) * LANES].astype(F32)
+        moved = pltpu.roll(tile, (LANES + h * plan.piece - plan.used) % LANES, 1)
+        whole = jnp.where(lane >= h * plan.piece, moved, whole)
+    return whole.astype(BF16)
 
 
 def pack_windows(plan, target, text, image, caps, common):
-    width = text.shape[0] // caps * LANES
+    width = (text.shape[0] // caps - 1) * LANES
     held = plan.roots + plan.roots % 2
 
     def fill(device, core):
@@ -176,9 +192,15 @@
             for core in range(2):
                 fill(2 * chip + core, core)
 
+
+def clear_windows(plan, target):
+    held = plan.roots + plan.roots % 2
+
     @pl.loop(held, target.shape[0])
     def _(device):
         target[device] = jnp.zeros(target.shape[1:], BF16)
+
+    return slice(0, held), slice(held, target.shape[0])
 
 
 def take_rows(source, at, count):
@@ -284,6 +306,7 @@
         caps = ins[K.EOT].buf.shape[0]
         places, unused = pack_at(dim, hidden, caps)
         towers = attended_towers(ins)
+        clear_windows(plan, outs[K.VALUES].ref)
         pack_windows(plan, outs[K.VALUES].ref, towers[0][2][5], towers[1][2][5], caps, None)
         outs[K.VALUES].push()
         kept = [], []
@@ -350,7 +373,7 @@
     normed = (unit * gain.get()[...] + bias.get()[...]).astype(BF16)
     yield
     result = middle
-    w_fc, w_fc_out = w_fc.get(), w_fc_out.get()
+    w_fc = w_fc.get()
     every = []
     for cols in chunks(w_fc.shape[2]):
         hidden = dot(normed, w_fc[0, :, cols])
@@ -359,7 +382,7 @@
         if hidden_ref is not None:
             hidden_ref[:, cols] = hidden
             active_ref[:, cols] = active
-        result = result + dot(active, w_fc_out[0, cols, :])
+        result = result + dot(active, w_fc_out.get()[0, cols, :])
         yield
     head_unit, unused = standard(result)
     head_in = (head_unit * head_gain.get()[...][None] + head_bias.get()[...][None]).astype(BF16)
@@ -417,8 +440,9 @@
 
 def own_steps(plan, tower, units, multiplier, own_at, ins, outs):
     mine, other = units[tower], units[1 - tower]
-    own_out = outs[K.OWN, tower]
-    caps, dim = own_out.ref.shape[1:]
+    own_out, scores_out = outs[K.OWN, tower], outs[K.SCORES, tower]
+    dim = plan.dim
+    caps = scores_out.ref.shape[0] * HEAD_DIM // dim
     places, unused = pack_at(dim, plan.hidden, caps)
     other_total = log_sum(multiplier * dot_nt(mine, other), 0)
     yield
@@ -439,11 +463,10 @@
         weights_of(tower, ins), None,
     )
     grad_middle, grad_mixed = done[5], done[6].astype(F32)
-    own_out.ref[0] = grad_mixed
-    own_out.ref[1] = grad_middle
-    own_out.push()
+    own_out.ref[:caps, :] = grad_middle
     w_ref = ins[K.W_QKV, tower].get()
     through_values = dot_nt(spread(grad_mixed).astype(BF16), w_ref[0, :, 2 * dim :])
+    own_out.ref[2 * caps :, :] = through_values
     yield
     normed = ins[K.NORMED, tower].get()[...]
     grad_probs = dot_nt(through_values.astype(BF16), normed)
@@ -451,23 +474,24 @@
     probs = ins[K.PROBS, tower].get()[...]
     inner = jnp.sum(probs * grad_probs, -1, keepdims=True)
     grad_scores = (probs * (grad_probs - inner) * HEAD_DIM ** (-0.5)).astype(BF16)
-    outs[K.SCORES, tower].ref[...] = grad_scores
-    outs[K.SCORES, tower].push()
+    scores_out.ref[...] = grad_scores
+    scores_out.push()
     yield
     spread_keys = dot(grad_scores, normed)
     yield
     grad_query = collect(dot(spread_keys.astype(BF16), w_ref[0, :, dim : 2 * dim]), caps).astype(BF16)
-    outs[K.QUERY, tower].ref[...] = grad_query
-    outs[K.QUERY, tower].push()
     yield
     units = pack[places[0], :] * dot(grad_scores, ins[K.UNIT, tower].get()[...])
     yield
     through_query = dot_nt(grad_query, w_ref[0, :, :dim])
+    own_out.ref[caps : 2 * caps, :] = through_query
+    own_out.push()
     units = units + through_values * pack[places[1], :]
     gain_part = jnp.sum(units, 0, keepdims=True) + jnp.sum(
         through_query * pack[places[2], :], 0, keepdims=True
     )
-    return spread_keys, grad_query, gain_part
+    bias_part = jnp.sum(through_values, 0, keepdims=True) + jnp.sum(through_query, 0, keepdims=True)
+    return spread_keys, grad_query, (gain_part, bias_part)
 
 
 def forward_pair(plan, rows, ins, kept, hidden, active):
@@ -484,6 +508,19 @@
     )
 
 
+def row_copies(scalars, ins, scratch):
+    core = scalars[0][0] % 2
+    return [
+        pltpu.make_async_copy(ins[name].ref, scratch[0].at[:, at], scratch[1].at[i])
+        for i, (name, at) in enumerate(((K.MINE, core), (K.OTHERS, 1 - core)))
+    ]
+
+
+def join_rows(scalars, ins, scratch):
+    for copy in row_copies(scalars, ins, scratch):
+        copy.start()
+
+
 def middle_body(plan):
     def body(scalars, ins, outs, scratch):
         at_ref, scale_ref = scalars
@@ -491,13 +528,9 @@
         dim = plan.dim
         device = at_ref[0]
         caps, wide = rows_ref.shape[2:]
-        copies = [
-            pltpu.make_async_copy(ins[name].ref, rows_ref.at[:, core], sems.at[i])
-            for i, (name, core) in enumerate(((K.MINE, device % 2), (K.OTHERS, 1 - device % 2)))
-        ]
-        for copy in copies:
-            copy.start()
-        for copy in copies:
+        held, others = clear_windows(plan, outs[K.SEND].ref)
+        outs[K.SEND].push_part(others)
+        for copy in row_copies(scalars, ins, scratch):
             copy.wait()
         rows = rows_ref[...].reshape(plan.devices * caps, wide)
         outs[K.ROWS].ref[...] = rows
@@ -508,17 +541,38 @@
         parts = run_together(
             [own_steps(plan, tower, units, multiplier, own_at, ins, outs) for tower in range(2)]
         )
-        (keys_t, query_t, gain_t), (keys_i, query_i, gain_i) = parts
         tiles = dim // LANES
-        small = jnp.concatenate(
-            [g[:, j * LANES : (j + 1) * LANES] for g in (gain_t, gain_i) for j in range(tiles)]
-            + [jnp.zeros((caps - 2 * tiles, LANES), F32)],
-            0,
+        common = []
+        for unused, query, sums in parts:
+            small = [row[:, j * LANES : (j + 1) * LANES] for row in sums for j in range(tiles)]
+            small.append(jnp.zeros((caps - 2 * tiles, LANES), F32))
+            common.append(jnp.concatenate([query, jnp.concatenate(small, 0).astype(BF16)], 1))
+        keys_t, keys_i = parts[0][0], parts[1][0]
+        pack_windows(plan, outs[K.SEND].ref, keys_t, keys_i, caps, common)
+        outs[K.SEND].push_part(held)
+
+    return body
+
+
+def late_weights(ins, scratch):
+    parts, sems = scratch[-2:]
+    dim = parts.shape[1]
+    return [
+        pltpu.make_async_copy(
+            ins[K.W_QKV, tower].ref.at[0, :, pl.ds(0, dim)], parts.at[tower], sems.at[tower]
         )
-        common = [jnp.concatenate([query, small.astype(BF16)], 1) for query in (query_t, query_i)]
-        pack_windows(plan, outs[K.SEND].ref, keys_t, keys_i, caps, common)
-
-    return body
+        for tower in range(2)
+    ]
+
+
+def tail_ahead(plan):
+    def ahead(scalars, ins, scratch):
+        @pl.when(scalars[0][0] < plan.roots)
+        def _():
+            for copy in late_weights(ins, scratch):
+                copy.start()
+
+    return ahead
 
 
 def tail_body(plan):
@@ -526,7 +580,7 @@
         at_ref, scale_ref = scalars
         dim, hidden_dim = plan.dim, plan.hidden
         loss_ref, scale_grad_ref = outs[K.LOSS].ref, outs[K.SCALE].ref
-        flat, flat_head, wide_t, wide_i, hidden_grad, small, hidden_t, hidden_i, active_t, active_i = scratch
+        flat, flat_head, wide_t, wide_i, small, hiddens, actives, hidden_grads, late, unused = scratch
         device = at_ref[0]
         eot = ins[K.EOT].get()
         caps = eot.shape[0]
@@ -535,36 +589,33 @@
         multiplier = jnp.exp(jnp.full((1, 1), scale_ref[0], F32))
 
         def input_gradient(tower, picked, wide):
-            names = K.X, K.GAIN, K.W_QKV, K.PROBS, K.PACK, K.OWN, K.SCORES, K.QUERY
-            x, gain, w_ref, probs, pack, own, scores, query_grad = (
-                ins[name, tower].get() for name in names
-            )
+            x, gain = ins[K.X, tower].get(), ins[K.GAIN, tower].get()
             seq = x.shape[0]
             unit, scale = standard(x[...].reshape(seq * caps, dim).astype(F32))
-            query = pack[places[3], :]
-            grad_keys = dot_tn(scores[...], spread(query).astype(BF16)).astype(BF16)
-            grad_values = dot_tn(probs[...].astype(BF16), spread(own[0]).astype(BF16)).astype(BF16)
-            grad_normed = dot_nt(grad_keys, w_ref[0, :, dim : 2 * dim])
-            grad_normed = grad_normed + dot_nt(grad_values, w_ref[0, :, 2 * dim :])
-            through_query = dot_nt(query_grad[...], w_ref[0, :, :dim])
-            wide[...] = grad_normed
+            yield
+            probs, pack, own, scores = (
+                ins[name, tower].get() for name in (K.PROBS, K.PACK, K.OWN, K.SCORES)
+            )
+            left = jnp.concatenate([scores[...], probs[...].astype(BF16)], 0)
+            right = jnp.concatenate([pack[places[0], :], own[2 * caps :, :]], 0).astype(BF16)
+            wide[...] = dot_tn(left, right)
+            yield
             for b in range(caps):
                 at = picked[b] * caps + b
-                wide[pl.ds(at, 1), :] = wide[pl.ds(at, 1), :] + through_query[b : b + 1]
+                wide[pl.ds(at, 1), :] = wide[pl.ds(at, 1), :] + own[caps + b : caps + b + 1, :]
             wide[...] = norm_back(wide[...], unit, scale, gain[...])
+            yield
             for b in range(caps):
                 at = picked[b] * caps + b
-                wide[pl.ds(at, 1), :] = wide[pl.ds(at, 1), :] + own[1][b : b + 1]
+                wide[pl.ds(at, 1), :] = wide[pl.ds(at, 1), :] + own[b : b + 1, :]
             outs[K.INPUT, tower].ref[...] = wide[...].reshape(seq, caps, dim)
             outs[K.INPUT, tower].push()
 
-        input_gradient(0, ends, wide_t)
-        input_gradient(1, [0] * caps, wide_i)
+        run_together([input_gradient(0, ends, wide_t), input_gradient(1, [0] * caps, wide_i)])
 
         rows = ins[K.ROWS].get()[...]
         count = rows.shape[0]
         kept = [], []
-        hiddens, actives = (hidden_t, hidden_i), (active_t, active_i)
         units = forward_pair(plan, rows, ins, kept, hiddens, actives)
         embeds = [items[2] for items in kept]
         logits = multiplier * dot_nt(units[1], units[0])
@@ -585,25 +636,28 @@
             dot(by_row, units[0]) + dot(by_column, units[0]),
         )
 
+        grad_embeds = [embed_back(grad_units[tower], embeds[tower]) for tower in range(2)]
+        backs = run_together(
+            [
+                tower_backward(
+                    grad_embeds[tower], kept[tower][0], kept[tower][1], hiddens[tower],
+                    weights_of(tower, ins), hidden_grads[tower],
+                )
+                for tower in range(2)
+            ]
+        )
+
+        mixed_grads = []
         start, head_start = device * plan.share, device * plan.head_share
         front = plan.rows_out
         half = plan.head_total // 2
         for tower in range(2):
             weights = weights_of(tower, ins)
             gain, bias, head_gain, head_bias = (weights[j] for j in (1, 2, 5, 6))
-            middle, result, unused = kept[tower]
-            active = actives[tower]
-            grad_embed = embed_back(grad_units[tower], embeds[tower])
-            (done,) = run_together(
-                [
-                    tower_backward(
-                        grad_embed, middle, result, hiddens[tower], weights, hidden_grad
-                    )
-                ]
-            )
+            active, hidden_grad = actives[tower], hidden_grads[tower]
+            grad_embed, done = grad_embeds[tower], backs[tower]
             grad_head, head_unit, grad_out, grad_normed, unit, grad_middle, grad_mixed = done
-            outs[K.MIXED, tower].ref[...] = grad_mixed
-            outs[K.MIXED, tower].push()
+            mixed_grads.append(grad_mixed)
             middle_low = grad_middle.astype(BF16)
             normed = (unit * gain.get()[...] + bias.get()[...]).astype(BF16)
             head_in = head_unit * head_gain.get()[...][None] + head_bias.get()[...][None]
@@ -653,56 +707,60 @@
         outs[K.HEAD].ref[...] = take_rows(flat_head, head_start, plan.head_rows_out)
         outs[K.HEAD].push()
 
-        for tower in range(2):
-            bias = ins[K.BIAS, tower].get()
-
-        @pl.when(device == 0)
-        def _():
-            for tower in range(2):
-                w_ref = ins[K.W_QKV, tower].get()
-                grads = dot_nt(outs[K.MIXED, tower].ref[...], w_ref[0, :, 2 * dim :])
-                outs[K.BIAS].ref[tower : tower + 1, :] = jnp.sum(grads, 0, keepdims=True)
+        query_t, query_i = late_weights(ins, scratch)
+        values = ins[K.VALUES].get()
 
         @pl.when(device < plan.roots)
         def _():
+            query_t.wait()
+            query_i.wait()
             first = plan.column(device)
             lane = lax.broadcasted_iota(jnp.int32, (count, LANES), 1)
             picked_rows = []
             for tower in range(2):
-                gain, bias, w_ref = (ins[name, tower].get() for name in (K.GAIN, K.BIAS, K.W_QKV))
+                gain, bias = ins[K.GAIN, tower].get(), ins[K.BIAS, tower].get()
                 pooled = rows[:, 2 * tower * dim : (2 * tower + 1) * dim].astype(F32)
                 unit, unused = standard(pooled)
                 normed = unit * gain[...] + bias[...]
                 outs[K.QUERIES].ref[:, tower * dim : (tower + 1) * dim] = dot(
-                    normed.astype(BF16), w_ref[0, :, :dim]
+                    normed.astype(BF16), late[tower]
                 ).astype(BF16)
-                shift = lax.rem(dim - first + tower * WINDOW, dim)
+                shift = lax.rem(dim - first + tower * plan.pad, dim)
                 picked_rows.append(pltpu.roll(normed, shift, 1)[:, :LANES])
-            outs[K.WINDOWS].ref[...] = jnp.where(lane < WINDOW, picked_rows[0], picked_rows[1]).astype(BF16)
+            end = last_head(plan, values, dim // HEAD_DIM)
+            for j in range(dim // LANES):
+                cols = slice(j * LANES, (j + 1) * LANES)
+                block = window_product(plan, values, end, mixed_grads, (0, 0), j)
+                for tower in range(2):
+                    at = tower * plan.pad
+                    outs[K.VALUES].ref[tower, :, cols] = block[
+                        at : at + plan.pad, tower * LANES : (tower + 1) * LANES
+                    ]
+            outs[K.WINDOWS].ref[...] = jnp.where(lane < plan.pad, picked_rows[0], picked_rows[1]).astype(BF16)
 
     return body
+
+
+def window_product(plan, source, end, factors, offsets, j):
+    lane = lax.broadcasted_iota(jnp.int32, (1, 2 * LANES), 1) % LANES
+    right = [factor[:, at + j * LANES : at + (j + 1) * LANES] for factor, at in zip(factors, offsets)]
+    right = jnp.concatenate(right, 1).astype(F32)
+    total = 0.0
+    for h in (2 * j, 2 * j + 1):
+        left = end if (h + 1) * HEAD_DIM == plan.dim else source[:, h * LANES : (h + 1) * LANES]
+        mine = (lane // HEAD_DIM == h % 2).astype(F32)
+        total = total + dot_tn(left, (right * mine).astype(BF16))
+    return total
 
 
 def last_body(plan):
     def body(scalars, ins, outs, scratch):
         (at_ref,) = scalars
-        flat, wq, grad_query, sems = scratch
+        flat, grad_query = scratch
         dim = plan.dim
         heads = dim // HEAD_DIM
         tiles = dim // LANES
         device = at_ref[0]
-        copies = [
-            pltpu.make_async_copy(
-                ins[K.W_QKV, tower].ref.at[0, :, pl.ds(0, dim)], wq.at[tower], sems.at[tower]
-            )
-            for tower in range(2)
-        ]
-
-        @pl.when(device == 0)
-        def _():
-            for copy in copies:
-                copy.start()
-
         parts = [ins[K.PART, tower].get() for tower in range(2)]
 
         def store(tower, block):
@@ -714,71 +772,46 @@
             for tower in range(2):
                 store(tower, parts[tower][...])
 
-        names = K.SENT, K.SWAPPED, K.VALUES, K.WINDOWS, K.QUERIES, K.BIAS, (K.MIXED, 0), (K.MIXED, 1)
-        sent_ref, swapped, values_ref, windows, queries, bias, mixed_t, mixed_i = (
+        names = K.SENT, K.SWAPPED, K.WINDOWS, K.QUERIES, K.VALUES
+        sent_ref, swapped, windows, queries, value_part = (
             ins[name].get() for name in names
         )
 
         @pl.when(device < plan.roots)
         def _():
-            at_query = heads * LANES
-            at_small = at_query + dim
+            at_query = (heads - 1) * LANES
             count = sent_ref.shape[0]
+            caps = count // plan.devices
             for core in range(2):
 
                 @pl.when(device % 2 == core)
                 def _():
-                    for tower, source in enumerate((sent_ref, swapped) if core == 0 else (swapped, sent_ref)):
-                        grad_query[:, tower * dim : (tower + 1) * dim] = source[:, at_query:at_small]
-
-            small = sent_ref[:, at_small:].astype(F32)
-            small = jnp.sum(small.reshape(count // 8, 8, LANES), 0)
+                    received = sent_ref[:, at_query:], swapped[...]
+                    for tower, values in enumerate(received if core == 0 else received[::-1]):
+                        grad_query[:, tower * dim : (tower + 1) * dim] = values[:, :dim]
+                        small = values[:, dim:].astype(F32).reshape(plan.devices, caps, LANES)
+                        flat[tower, : 2 * tiles, :] = jnp.sum(small, 0)[: 2 * tiles]
+
             query_part = dot_tn(windows[...], grad_query[...])
-            lane = lax.broadcasted_iota(jnp.int32, (1, LANES), 1)
-            halves = [(lane < HEAD_DIM).astype(F32), (lane >= HEAD_DIM).astype(F32)]
+            end = last_head(plan, sent_ref, heads)
             for j in range(tiles):
-                put = []
-                cols = slice(j * LANES, (j + 1) * LANES)
-                others = slice(dim + j * LANES, dim + (j + 1) * LANES)
-                for source, factors in (
-                    (sent_ref, (queries[:, cols], queries[:, others])),
-                    (values_ref, (mixed_t[:, cols], mixed_i[:, cols])),
-                ):
-                    right = jnp.concatenate(factors, 1).astype(F32)
-                    total = 0.0
-                    for odd in range(2):
-                        h = 2 * j + odd
-                        left = source[:, h * LANES : (h + 1) * LANES]
-                        mask = jnp.concatenate([halves[odd]] * 2, 1)
-                        total = total + dot_tn(left, (right * mask).astype(BF16))
-                    put.append(total)
+                put = window_product(plan, sent_ref, end, (queries, queries), (0, dim), j)
                 for tower in range(2):
-                    rows = slice(tower * WINDOW, (tower + 1) * WINDOW)
+                    rows = slice(tower * plan.pad, (tower + 1) * plan.pad)
                     own = slice(tower * LANES, (tower + 1) * LANES)
                     q_at = tower * dim + j * LANES
                     for part, block in enumerate(
-                        (query_part[rows, q_at : q_at + LANES], put[0][rows, own], put[1][rows, own])
+                        (
+                            query_part[rows, q_at : q_at + LANES],
+                            put[rows, own],
+                            value_part[tower, :, j * LANES : (j + 1) * LANES],
+                        )
                     ):
                         flat[
                             tower,
-                            pl.ds(2 * tiles + part * tiles + j, WINDOW, stride=3 * tiles),
+                            pl.ds(2 * tiles + part * tiles + j, plan.pad, stride=3 * tiles),
                             :,
                         ] = block
-            for tower in range(2):
-                flat[tower, 0:tiles, :] = small[tower * tiles : (tower + 1) * tiles]
-
-            @pl.when(device == 0)
-            def _():
-                for tower, copy in enumerate(copies):
-                    copy.wait()
-                    grads = grad_query[:, tower * dim : (tower + 1) * dim]
-                    row = jnp.sum(dot_nt(grads, wq[tower]), 0, keepdims=True)
-                    row = row + bias[tower : tower + 1, :]
-                    for j in range(tiles):
-                        flat[tower, tiles + j : tiles + j + 1, :] = row[
-                            :, j * LANES : (j + 1) * LANES
-                        ]
-
             start = device * plan.share
             at = start - plan.column(device) * plan.row
             shape = parts[0].shape
@@ -795,34 +828,25 @@
 
 
 class Fetch:
-    def __init__(self, source, buf, sem, queue):
-        self.ref, self.buf, self.queue, self.waited = source, buf, queue, False
-        self.size = buf.dtype.itemsize
-        for extent in buf.shape:
-            self.size *= extent
+    def __init__(self, source, buf, sem, group):
+        self.ref, self.buf, self.group = source, buf, group
         self.copy = pltpu.make_async_copy(source, buf, sem)
+        group.members.append(self)
 
     def get(self):
+        self.group.wait()
+        return self.buf
+
+
+class Group:
+    def __init__(self):
+        self.members, self.waited = [], False
+
+    def wait(self):
         if not self.waited:
-            self.queue.advance(self)
-            self.copy.wait()
             self.waited = True
-            self.queue.flying -= self.size
-            self.queue.advance(None)
-        return self.buf
-
-
-class Queue:
-    def __init__(self):
-        self.waiting, self.flying = [], 0
-
-    def advance(self, needed):
-        while self.waiting and (
-            needed in self.waiting or self.flying + self.waiting[0].size <= IN_FLIGHT
-        ):
-            fetch = self.waiting.pop(0)
-            fetch.copy.start()
-            self.flying += fetch.size
+            for fetch in self.members:
+                fetch.copy.wait()
 
 
 class Here:
@@ -838,18 +862,24 @@
 
 class Push:
     def __init__(self, ref, target, sem):
-        self.ref, self.started = ref, False
+        self.ref, self.target, self.sem, self.started = ref, target, sem, False
         self.copy = pltpu.make_async_copy(ref, target, sem)
 
     def push(self):
         self.started = True
         self.copy.start()
 
-
-def run(body, name, outs, scratch, scalars, arrays):
+    def push_part(self, part):
+        self.started = True
+        pltpu.make_async_copy(self.ref.at[part], self.target.at[part], self.sem).start()
+
+
+def run(body, name, outs, scratch, scalars, arrays, ahead=None):
     smem = pl.BlockSpec(memory_space=pltpu.SMEM)
     hbm = pl.BlockSpec(memory_space=pltpu.HBM)
     vmem = pl.BlockSpec(memory_space=pltpu.VMEM)
+    groups = arrays
+    arrays = {key: value for group in groups for key, value in group.items()}
     fetched = [(array, place) for array, place in arrays.values() if place in (Place.FAR, Place.FEW)]
     pushed = [(shape, kind) for shape, kind, place in outs.values() if place == Place.FAR]
 
@@ -864,21 +894,27 @@
         scalar_refs, sources, targets = take(len(scalars)), take(len(arrays)), take(len(outs))
         in_bufs, out_bufs = take(len(fetched)), take(len(pushed))
         in_sems, out_sems = take(2)
-        ins, results, fetches, pushes, queue = {}, {}, [], [], Queue()
-        for source, (key, (unused, place)) in zip(sources, arrays.items()):
-            if place in (Place.FAR, Place.FEW):
-                sem = in_sems.at[len(fetches)]
-                fetches.append(Fetch(source, in_bufs[len(fetches)], sem, queue))
-                ins[key] = fetches[-1]
-            else:
-                ins[key] = Here(source)
-        queue.waiting = list(fetches)
-        queue.advance(None)
+        ins, results, fetches, pushes = {}, {}, [], []
+        sources = iter(sources)
+        chain = [Group() for unused in groups]
+        for group, together in zip(groups, chain):
+            for (key, (unused, place)), source in zip(group.items(), sources):
+                if place in (Place.FAR, Place.FEW):
+                    sem = in_sems.at[len(fetches)]
+                    fetches.append(Fetch(source, in_bufs[len(fetches)], sem, together))
+                    ins[key] = fetches[-1]
+                else:
+                    ins[key] = Here(source)
         for target, (key, (unused, unused, place)) in zip(targets, outs.items()):
             if place == Place.FAR:
                 pushes.append(Push(out_bufs[len(pushes)], target, out_sems.at[len(pushes)]))
             results[key] = pushes[-1] if place == Place.FAR else Here(target)
-        body(scalar_refs, ins, results, take(len(scratch)))
+        own_scratch = take(len(scratch))
+        if ahead is not None:
+            ahead(scalar_refs, ins, own_scratch)
+        for fetch in fetches:
+            fetch.copy.start()
+        body(scalar_refs, ins, results, own_scratch)
         for push in pushes:
             if not push.started:
                 push.push()
@@ -907,7 +943,7 @@
         ],
         in_specs=[smem] * len(scalars) + [where[place] for unused, place in arrays.values()],
         out_specs=[where[place] for unused, unused, place in outs.values()],
-        scratch_shapes=buffers + scratch,
+        scratch_shapes=buffers + list(scratch),
         compiler_params=pltpu.CompilerParams(vmem_limit_bytes=LIMIT),
     )(*scalars, *pinned)
     return dict(zip(outs, results))
@@ -945,20 +981,22 @@
     text_input, image_input = text_input.swapaxes(0, 1), image_input.swapaxes(0, 1)
     totals = caps * seq, caps * img_seq
     chips = devices // 2
-    width = heads * LANES
+    width = (heads - 1) * LANES
 
     first = {
         (K.X, 0): text_input, (K.X, 1): image_input,
         (K.GAIN, 0): ln1_gain, (K.BIAS, 0): ln1_bias,
         (K.GAIN, 1): img_ln1_gain, (K.BIAS, 1): img_ln1_bias,
-        (K.W_QKV, 0): w_qkv, (K.W_QKV, 1): img_w_qkv,
     }
+    late = {(K.W_QKV, 0): w_qkv, (K.W_QKV, 1): img_w_qkv}
     second = {
         (K.W_OUT, 0): w_attn_out, (K.W_OUT, 1): img_w_attn_out,
         (K.GAIN2, 0): ln2_gain, (K.BIAS2, 0): ln2_bias,
         (K.GAIN2, 1): img_ln2_gain, (K.BIAS2, 1): img_ln2_bias,
-        (K.W_FC, 0): w_fc, (K.W_FC_OUT, 0): w_fc_out,
-        (K.W_FC, 1): img_w_fc, (K.W_FC_OUT, 1): img_w_fc_out,
+    }
+    hidden_in = {(K.W_FC, 0): w_fc, (K.W_FC, 1): img_w_fc}
+    third = {
+        (K.W_FC_OUT, 0): w_fc_out, (K.W_FC_OUT, 1): img_w_fc_out,
         (K.HEAD_GAIN, 0): final_gain, (K.HEAD_BIAS, 0): final_bias,
         (K.HEAD_GAIN, 1): image_gain, (K.HEAD_BIAS, 1): image_bias,
         (K.PROJ, 0): text_proj, (K.PROJ, 1): image_proj,
@@ -974,14 +1012,14 @@
         {K.ROWS: ((chips, caps, 4 * dim), BF16, Place.AUTO)},
         [],
         [],
-        eot | far(first),
+        [eot | far(first), far(late)],
     )[K.ROWS]
     mine = exchange_by_core(rows, devices)
 
     unused, pack_rows = pack_at(dim, hidden, caps)
     side_outs = {K.VALUES: ((devices, caps, width), BF16, Place.FAR)}
     middle_outs = {
-        K.SEND: ((devices, caps, width + dim + LANES), BF16, Place.AUTO),
+        K.SEND: ((devices, caps, width + dim + LANES), BF16, Place.FAR),
         K.ROWS: ((count, 4 * dim), BF16, Place.FAR),
     }
     for tower, total in enumerate(totals):
@@ -992,16 +1030,14 @@
             (K.PACK, tower): ((pack_rows, dim), F32, Place.FAR),
         }
         middle_outs |= {
-            (K.OWN, tower): ((2, caps, dim), F32, Place.FAR),
+            (K.OWN, tower): (((2 + heads) * caps, dim), F32, Place.FAR),
             (K.SCORES, tower): ((heads * caps, total), BF16, Place.FAR),
-            (K.QUERY, tower): ((caps, dim), BF16, Place.FAR),
         }
-    side = run(side_body(plan), "side", side_outs, [], [], eot | far(first) | far(second))
+    side = run(side_body(plan), "side", side_outs, [], [], [eot | far(first), far(late), far(second | hidden_in | third)])
     values = exchange(side.pop(K.VALUES))
     mine, side[K.PACK, 0] = lax.optimization_barrier((mine, side[K.PACK, 0]))
     others = swap(mine, devices)
 
-    late = {(K.W_QKV, 0): w_qkv, (K.W_QKV, 1): img_w_qkv}
     packs = {key: side[key] for key in ((K.PACK, 0), (K.PACK, 1))}
     middle = run(
         middle_body(plan),
@@ -1009,11 +1045,14 @@
         middle_outs,
         [pltpu.VMEM((chips, 2, caps, 4 * dim), BF16), pltpu.SemaphoreType.DMA((2,))],
         [device, logit_scale],
-        {K.MINE: (mine, Place.AUTO), K.OTHERS: (others, Place.AUTO)}
-        | far(second)
-        | far(packs)
-        | far(late)
-        | far({(name, tower): side[name, tower] for name in (K.NORMED, K.PROBS, K.UNIT) for tower in (0, 1)}),
+        [
+            {K.MINE: (mine, Place.AUTO), K.OTHERS: (others, Place.AUTO)} | far(second),
+            far(hidden_in),
+            far(third | packs),
+            far(late)
+            | far({(name, tower): side[name, tower] for name in (K.NORMED, K.PROBS, K.UNIT) for tower in (0, 1)}),
+        ],
+        join_rows,
     )
     send, values = lax.optimization_barrier((middle[K.SEND], values))
     sent = exchange(send)
@@ -1021,23 +1060,20 @@
     share_rows = plan.rows_out
     region = (plan.total - plan.out_at) // LANES
     head_region = plan.head_total // LANES
-    tail_ins = eot | far(first)
+    attended = {}
     tail_outs = {K.LOSS: ((1,), F32, Place.SCALAR), K.SCALE: ((1,), F32, Place.SCALAR)}
     for tower, length in enumerate((seq, img_seq)):
-        for name, source in (
-            (K.PROBS, side), (K.PACK, side), (K.OWN, middle), (K.SCORES, middle), (K.QUERY, middle)
-        ):
-            tail_ins |= far({(name, tower): source[name, tower]})
+        for name, source in ((K.PROBS, side), (K.PACK, side), (K.OWN, middle), (K.SCORES, middle)):
+            attended[name, tower] = source[name, tower]
         tail_outs |= {
             (K.PART, tower): ((share_rows, LANES), F32, Place.FAR),
-            (K.MIXED, tower): ((count, dim), BF16, Place.FAR),
             (K.INPUT, tower): ((length, caps, dim), F32, Place.FAR),
         }
     tail_outs |= {
         K.HEAD: ((plan.head_rows_out, LANES), F32, Place.FAR),
         K.WINDOWS: ((count, LANES), BF16, Place.FAR),
         K.QUERIES: ((count, 2 * dim), BF16, Place.FAR),
-        K.BIAS: ((8, dim), F32, Place.FAR),
+        K.VALUES: ((2, plan.pad, dim), F32, Place.FAR),
     }
     tail = run(
         tail_body(plan),
@@ -1048,34 +1084,42 @@
             pltpu.VMEM((head_region + plan.head_rows_out + 8, LANES), F32),
             pltpu.VMEM((totals[0], dim), F32),
             pltpu.VMEM((totals[1], dim), F32),
-            pltpu.VMEM((count, hidden), BF16),
             pltpu.VMEM((8, dim), F32),
-            pltpu.VMEM((count, hidden), F32),
-            pltpu.VMEM((count, hidden), F32),
-            pltpu.VMEM((count, hidden), BF16),
-            pltpu.VMEM((count, hidden), BF16),
+            [pltpu.VMEM((count, hidden), F32)] * 2,
+            [pltpu.VMEM((count, hidden), BF16)] * 2,
+            [pltpu.VMEM((count, hidden), BF16)] * 2,
+            pltpu.VMEM((2, dim, dim), BF16),
+            pltpu.SemaphoreType.DMA((2,)),
         ],
         [device, logit_scale],
-        tail_ins | far({K.ROWS: middle[K.ROWS]} | second),
-    )
-    sent, tail[K.BIAS] = lax.optimization_barrier((sent, tail[K.BIAS]))
-    swapped = swap(sent, devices)
-    flat_rows = 2 * dim // LANES + max(WINDOW * plan.row, 2 * plan.row + share_rows * LANES) // LANES
-    names = [(K.PART, 0), (K.PART, 1), K.WINDOWS, K.QUERIES, K.BIAS, (K.MIXED, 0), (K.MIXED, 1)]
+        [
+            eot | far(first),
+            far(attended),
+            far({K.ROWS: middle[K.ROWS]} | second | hidden_in),
+            far(third),
+            far({K.VALUES: values.reshape(count, width)})
+            | {key: (array, Place.RAW) for key, array in late.items()},
+        ],
+        tail_ahead(plan),
+    )
+    sent, tail[K.WINDOWS] = lax.optimization_barrier((sent, tail[K.WINDOWS]))
+    swapped = swap(sent[:, :, width:], devices)
+    flat_rows = max(2 * dim + plan.pad * plan.row, 2 * dim + 2 * plan.row + share_rows * LANES) // LANES
+    names = [(K.PART, 0), (K.PART, 1), K.WINDOWS, K.QUERIES, K.VALUES]
     shares = run(
         last_body(plan),
         "last",
         {(K.SHARE, tower): ((1, plan.share), F32, Place.FAR) for tower in (0, 1)},
         [
             pltpu.VMEM((2, flat_rows // 8 * 8 + 16, LANES), F32),
-            pltpu.VMEM((2, dim, dim), BF16),
             pltpu.VMEM((count, 2 * dim), BF16),
-            pltpu.SemaphoreType.DMA((2,)),
         ],
         [device],
-        far({name: tail[name] for name in names} | {K.VALUES: values.reshape(count, width)})
-        | {key: (array.reshape(count, -1), Place.AUTO) for key, array in ((K.SENT, sent), (K.SWAPPED, swapped))}
-        | {key: (array, Place.RAW) for key, array in late.items()},
+        [
+            far({name: tail[name] for name in names})
+            | {K.SENT: (sent.reshape(count, -1), Place.AUTO)}
+            | {K.SWAPPED: (swapped.reshape(count, -1), Place.AUTO)},
+        ],
     )
 
     def cut(array, size):

time: 73.1 us -> 69 us (0.944)
  Pallas kernels: 45.4 us -> 39.4 us
  waiting for transfers between devices: 8.4 us -> 10.2 us
    pallas_call x5, Pallas kernels: 45.4 us -> 39.4 us  [run(): pl.pallas_call(kernel, name=name, out_shape=[(pltpu.HBM if place == Place...]
    all_to_all x2, waiting for transfers between devices: 0.11 us -> 2 us  [exchange(): return lax.all_to_all(array, 'dp', split_axis=0, concat_axis=0, tiled=True)]
  transfers between devices with their start and end apart: 5 -> 5, of which waited for: 4 -> 4; matrix products, arithmetic and copies ran while one was open for 0% -> 0% of each run, Pallas kernels for 51% -> 48%
where the time goes in v1:
time: 69 us; the launch traced here: 68.5 us
  Pallas kernels  39.4 us (57%)
  starting transfers between devices  17.3 us (25%)
  waiting for transfers between devices  10.2 us (15%)
  between operations  1.54 us (2%)
    pallas_call x5, Pallas kernels, run(): pl.pallas_call(kernel, name=name, out_shape=[(pltpu.HBM if place == Place...  39.4 us
    all_to_all x2, starting transfers between devices, exchange(): return lax.all_to_all(array, 'dp', split_axis=0, concat_axis=0, tiled=True)  8.61 us
    all_to_all x1, starting transfers between devices, exchange_by_core(): lax.all_to_all(array, 'dp', split_axis=0, concat_axis=0, tiled=True, axis...  8.33 us
    all_to_all x1, waiting for transfers between devices, exchange_by_core(): lax.all_to_all(array, 'dp', split_axis=0, concat_axis=0, tiled=True, axis...  5.86 us
    ppermute x2, waiting for transfers between devices, swap(): return lax.ppermute(array, 'dp', [(i, i ^ 1) for i in range(devices)])  2.37 us
    all_to_all x2, waiting for transfers between devices, exchange(): return lax.all_to_all(array, 'dp', split_axis=0, concat_axis=0, tiled=True)  2 us
  transfers between devices with their start and end apart: 5, of which 4 were waited for; matrix products, arithmetic and copies ran while one was open for 0% of the time, Pallas kernels for 48%

profile of v1, /device:TPU:0, one launch (start us, length us, event | category | flops | bytes accessed | tf_op | source)
XLA Modules:
  0.0 68.5 jit_solution(11453313932855081618)
XLA Ops:
  0.6 4.0 %front.1 = bf16[16,8,1536]{2,1,0:T(8,128)(2,1)} custom-call(s32[8]{0:T(128)} %refs_2_.1, bf16[77,8,384]{2,1,0:T(8,128)(2,1)} %bitcast.12, bf16[50,8,384]{2,1,0:T(8,128)(2,1)} %bitcast.15, f32[1,384]{1,0:T(1,128)} %refs_5_.7, f32[1,384]{1,0:T(1,128)} %refs_6_.7, f32[1,384]{1,0:T(1,128)} %refs_7_.7, f32[1,384]{1,0:T(1,128)} %refs_8_.7, ...), custom_call_target="tpu_custom_call" | custom-call | tf_op jit(solution)/shard_map/front/pallas_call | solution.py:937
  4.6 8.3 %all-to-all-start = ((bf16[16,8,1536]{2,1,0:T(8,128)(2,1)}), bf16[16,8,1536]{2,1,0:T(8,128)(2,1)S(1)}, u32[]{:S(2)}, u32[]{:S(2)}) async-start(bf16[16,8,1536]{2,1,0:T(8,128)(2,1)} %front.1), calls=%async_computation | async-start | bytes 786432 | tf_op jit(solution)/shard_map/all_to_all | solution.py:958
  13.0 6.8 %side.1 = (bf16[32,8,640]{2,1,0:T(8,128)(2,1)}, bf16[616,384]{1,0:T(8,128)(2,1)}, bf16[616,384]{1,0:T(8,128)(2,1)}, f32[48,616]{1,0:T(8,128)}, f32[168,384]{1,0:...) custom-call(s32[8]{0:T(128)} %refs_2_.1, ...), custom_call_target="tpu_custom_call" | custom-call | tf_op jit(solution)/shard_map/side/pallas_call | solution.py:937
  19.7 5.9 %all-to-all-done.refs_2_ = bf16[16,8,1536]{2,1,0:T(8,128)(2,1)S(1)} async-done(((bf16[16,8,1536]{2,1,0:T(8,128)(2,1)}), bf16[16,8,1536]{2,1,0:T(8,128)(2,1)S(1)}, u32[]{:S(2)}, u32[]{:S(2)}) %all-to-all-start) | async-done | bytes 393248 | tf_op jit(solution)/shard_map/all_to_all | solution.py:958
  25.6 2.6 %all-to-all-start.1 = ((bf16[32,8,640]{2,1,0:T(8,128)(2,1)}), bf16[32,8,640]{2,1,0:T(8,128)(2,1)S(1)}, u32[]{:S(2)}, u32[]{:S(2)}) async-start(bf16[32,8,640]{2,1,0:T(8,128)(2,1)} %get-tuple-element.56), calls=%async_computation.1 | async-start | bytes 655360 | tf_op jit(solution)/shard_map/all_to_all | solution.py:953
  28.2 0.3 collective-permute-start
  29.1 0.8 %collective-permute-done.refs_3_ = bf16[16,8,1536]{2,1,0:T(8,128)(2,1)S(1)} collective-permute-done((bf16[16,8,1536]{2,1,0:T(8,128)(2,1)S(1)}, bf16[16,8,1536]{2,1,0:T(8,128)(2,1)S(1)}, u32[]{:S(2)}, u32[]{:S(2)}) %collective-permute-start) | collective-permute-done | bytes 393248 | tf_op jit(solution)/shard_map/ppermute | solution.py:964
  30.0 11.4 %middle.1 = (bf16[32,8,1152]{2,1,0:T(8,128)(2,1)}, bf16[256,1536]{1,0:T(8,128)(2,1)}, f32[64,384]{1,0:T(8,128)}, bf16[48,616]{1,0:T(8,128)(2,1)}, f32[64,384]{1,0:T(8,128)}, /*index=5*/bf16[48,400]{1,0:T(8,128)(2,1)}) custom-call(s32[1]{0:T(128)} %bitcast.refs_0_, f32[1]{0:T(128)S(6)} %copy.33.refs_1_, bf16[16,8,1536]{2,1,0:T(8,128)(2,1)S(1)} %all-to-all-done.refs_2_, ...), custom_call_target="tpu_custom_call" | custom-call | tf_op jit(solution)/shard_map/middle/pallas_call | solution.py:937
  41.4 0.0 all-to-all-done.1
  41.4 0.0 copy-start
  41.4 6.0 %all-to-all-start.2 = ((bf16[32,8,1152]{2,1,0:T(8,128)(2,1)}), bf16[32,8,1152]{2,1,0:T(8,128)(2,1)S(1)}, u32[]{:S(2)}, u32[]{:S(2)}) async-start(bf16[32,8,1152]{2,1,0:T(8,128)(2,1)} %get-tuple-element.63), calls=%async_computation.2 | async-start | bytes 1179648 | tf_op jit(solution)/shard_map/all_to_all | solution.py:953
  47.4 0.0 copy-done
  47.4 14.5 %tail.1 = (f32[1]{0:T(128)}, f32[1]{0:T(128)}, f32[440,128]{1,0:T(8,128)}, f32[77,8,384]{2,1,0:T(8,128)}, f32[440,128]{1,0:T(8,128)}, /*index=5*/f32[50,8,384]{2...) custom-call(s32[1]{0:T(128)} %bitcast.refs_0_, ...), custom_call_target="tpu_custom_call" | custom-call | tf_op jit(solution)/shard_map/tail/pallas_call | solution.py:937
  62.0 2.0 %all-to-all-done.2 = bf16[32,8,1152]{2,1,0:T(8,128)(2,1)S(1)} async-done(((bf16[32,8,1152]{2,1,0:T(8,128)(2,1)}), bf16[32,8,1152]{2,1,0:T(8,128)(2,1)S(1)}, u32[]{:S(2)}, u32[]{:S(2)}) %all-to-all-start.2) | async-done | bytes 589856 | tf_op jit(solution)/shard_map/all_to_all | solution.py:953
  64.0 0.1 collective-permute-start.1
  64.1 1.5 %collective-permute-done.1 = bf16[32,8,512]{2,1,0:T(8,128)(2,1)S(1)} collective-permute-done((bf16[32,8,512]{2,1,0:T(8,128)(2,1)S(1)}, bf16[32,8,512]{2,1,0:T(8,128)(2,1)S(1)}, u32[]{:S(2)}, u32[]{:S(2)}) %collective-permute-start.1) | collective-permute-done | bytes 262176 | tf_op jit(solution)/shard_map/ppermute | solution.py:964
  65.6 2.8 %last.1 = (f32[1,55344]{1,0:T(1,128)}, f32[1,55344]{1,0:T(1,128)}) custom-call(s32[1]{0:T(128)} %bitcast.refs_0_, f32[440,128]{1,0:T(8,128)} %get-tuple-element.61.refs_1_, f32[440,128]{1,0:T(8,128)} %get-tuple-element.62.refs_2_, bf16[256,128]{1,0:T(8,128)(2,1)} %get-tuple-element.65.refs_3_, bf16[256,768]{1,0:T(8,128)(2,1)} %get-tuple-element.66.refs_4_, ...), custom_call_target="tpu_custom_call" | custom-call | tf_op jit(solution)/shard_map/last/pallas_call | solution.py:937
  (1 shorter events, 0.0 us)
Async XLA Ops:
  4.6 21.0 %all-to-all-start = ((bf16[16,8,1536]{2,1,0:T(8,128)(2,1)}), bf16[16,8,1536]{2,1,0:T(8,128)(2,1)S(1)}, u32[]{:S(2)}, u32[]{:S(2)}) async-start(bf16[16,8,1536]{2,1,0:T(8,128)(2,1)} %front.1), calls=%async_computation | async-start | bytes 786432 | tf_op jit(solution)/shard_map/all_to_all | solution.py:958
  25.6 15.8 %all-to-all-start.1 = ((bf16[32,8,640]{2,1,0:T(8,128)(2,1)}), bf16[32,8,640]{2,1,0:T(8,128)(2,1)S(1)}, u32[]{:S(2)}, u32[]{:S(2)}) async-start(bf16[32,8,640]{2,1,0:T(8,128)(2,1)} %get-tuple-element.56), calls=%async_computation.1 | async-start | bytes 655360 | tf_op jit(solution)/shard_map/all_to_all | solution.py:953
  28.2 1.8 %collective-permute-start = (bf16[16,8,1536]{2,1,0:T(8,128)(2,1)S(1)}, bf16[16,8,1536]{2,1,0:T(8,128)(2,1)S(1)}, u32[]{:S(2)}, u32[]{:S(2)}) collective-permute-start(bf16[16,8,1536]{2,1,0:T(8,128)(2,1)S(1)} %all-to-all-done.refs_2_), channel_id=1, source_target_pairs={{0,1},{1,0},{2,3},{3,2},{4,5},{5,4},{6,7},{7,6},{8,9},{9,8},{10,11... | collective-permute-start | bytes 1179656 | tf_op jit(solution)/shard_map/ppermute | solution.py:964
  41.4 6.0 %copy-start = (bf16[32,8,640]{2,1,0:T(8,128)(2,1)}, bf16[32,8,640]{2,1,0:T(8,128)(2,1)S(1)}, u32[]{:S(2)}) copy-start(bf16[32,8,640]{2,1,0:T(8,128)(2,1)S(1)} %all-to-all-done.1) | copy-start | bytes 983044
  41.4 22.6 %all-to-all-start.2 = ((bf16[32,8,1152]{2,1,0:T(8,128)(2,1)}), bf16[32,8,1152]{2,1,0:T(8,128)(2,1)S(1)}, u32[]{:S(2)}, u32[]{:S(2)}) async-start(bf16[32,8,1152]{2,1,0:T(8,128)(2,1)} %get-tuple-element.63), calls=%async_computation.2 | async-start | bytes 1179648 | tf_op jit(solution)/shard_map/all_to_all | solution.py:953
  64.0 1.6 %collective-permute-start.1 = (bf16[32,8,512]{2,1,0:T(8,128)(2,1)S(1)}, bf16[32,8,512]{2,1,0:T(8,128)(2,1)S(1)}, u32[]{:S(2)}, u32[]{:S(2)}) collective-permute-start(bf16[32,8,512]{2,1,0:T(8,128)(2,1)S(1)} %slice.6), channel_id=1, source_target_pairs={{0,1},{1,0},{2,3},{3,2},{4,5},{5,4},{6,7},{7,6},{8,9},{9,8},{10,11... | collective-permute-start | bytes 786440 | tf_op jit(solution)/shard_map/ppermute | solution.py:964

commit v2 on v1

--- a/solution.py
+++ b/solution.py
@@ -23,6 +23,7 @@
     FEW = enum.auto()
     RAW = enum.auto()
     AUTO = enum.auto()
+    NEAR = enum.auto()
     SCALAR = enum.auto()
 
 
@@ -287,7 +288,7 @@
 
 def pack_at(dim, hidden, caps):
     heads = dim // HEAD_DIM
-    sizes = [heads * caps, heads * caps, caps, caps, caps, caps, caps, caps * hidden // dim]
+    sizes = [heads * caps] * 2 + [caps] * 8 + [caps * hidden // dim]
     places, at = [], 0
     for size in sizes:
         places.append(slice(at, at + size))
@@ -309,7 +310,7 @@
         clear_windows(plan, outs[K.VALUES].ref)
         pack_windows(plan, outs[K.VALUES].ref, towers[0][2][5], towers[1][2][5], caps, None)
         outs[K.VALUES].push()
-        kept = [], []
+        kept, hiddens = ([], []), scratch[0]
         for tower, (pooled, mixed, saved) in enumerate(towers):
             normed, unit, probs, query, through_keys, values, chosen = saved
             unit = unit.astype(BF16)
@@ -321,17 +322,19 @@
                 outs[K.PACK, tower].ref[place, :] = value
         run_together(
             [
-                tower_forward(pooled, mixed, weights_of(tower, ins), kept[tower], None, None)
+                tower_forward(
+                    pooled, mixed, weights_of(tower, ins), kept[tower], hiddens[tower], None
+                )
                 for tower, (pooled, mixed, unused) in enumerate(towers)
             ]
         )
         for tower in range(2):
             pack = outs[K.PACK, tower]
-            for place, value in zip(places[4:], kept[tower][:3]):
-                pack.ref[place, :] = value
+            for place, value in zip(places[4:10], kept[tower]):
+                pack.ref[place, :] = jnp.broadcast_to(value, (caps, dim))
             for j in range(hidden // dim):
-                at = places[7].start + j * caps
-                pack.ref[at : at + caps, :] = kept[tower][3][:, j * dim : (j + 1) * dim]
+                at = places[10].start + j * caps
+                pack.ref[at : at + caps, :] = gate_slope(hiddens[tower][:, j * dim : (j + 1) * dim])
             pack.push()
 
     return body
@@ -369,30 +372,28 @@
     w_out, gain, bias, w_fc, w_fc_out, head_gain, head_bias, proj = weights
     middle = pooled + dot(mixed, w_out.get()[0])
     yield
-    unit, unused = standard(middle)
+    unit, scale = standard(middle)
     normed = (unit * gain.get()[...] + bias.get()[...]).astype(BF16)
     yield
     result = middle
     w_fc = w_fc.get()
-    every = []
     for cols in chunks(w_fc.shape[2]):
         hidden = dot(normed, w_fc[0, :, cols])
         active = (hidden * jax.nn.sigmoid(1.702 * hidden)).astype(BF16)
-        every.append(hidden)
         if hidden_ref is not None:
             hidden_ref[:, cols] = hidden
+        if active_ref is not None:
             active_ref[:, cols] = active
         result = result + dot(active, w_fc_out.get()[0, cols, :])
         yield
-    head_unit, unused = standard(result)
+    head_unit, head_scale = standard(result)
     head_in = (head_unit * head_gain.get()[...][None] + head_bias.get()[...][None]).astype(BF16)
     embed = dot(head_in, proj.get()[...])
     yield
+    unit_embed, length = unit_rows_of(embed)
     if kept is not None:
-        kept += [middle, result, embed]
-        if hidden_ref is None:
-            kept.append(jnp.concatenate(every, 1))
-    return unit_rows_of(embed)[0].astype(BF16)
+        kept += [unit, scale, head_unit, head_scale, unit_embed, length]
+    return unit_embed.astype(BF16)
 
 
 def log_sum(logits, axis):
@@ -407,17 +408,16 @@
     return dot(own.astype(BF16), other) + dot(cross.astype(BF16), other)
 
 
-def embed_back(grad_unit, embed):
-    unit_embed, length = unit_rows_of(embed)
+def embed_back(grad_unit, unit_embed, length):
     along = jnp.sum(unit_embed * grad_unit, -1, keepdims=True)
     return (length * (grad_unit - unit_embed * along)).astype(BF16)
 
 
-def tower_backward(grad_embed, middle, result, hidden, weights, keep_hidden):
+def tower_backward(grad_embed, kept, slope, weights, keep_hidden):
+    unit, scale, head_unit, head_scale = kept
     w_out, gain, bias, w_fc, w_fc_out, head_gain, head_bias, proj = weights
     grad_head = dot_nt(grad_embed, proj.get()[...])
     yield
-    head_unit, head_scale = standard(result)
     grad_result = norm_back(grad_head, head_unit, head_scale, head_gain.get()[...][None])
     grad_out = grad_result.astype(BF16)
     yield
@@ -425,17 +425,16 @@
     grad_normed = 0.0
     for cols in chunks(w_fc.shape[2]):
         grad_active = dot_nt(grad_out, w_fc_out[0, cols, :])
-        grad_hidden = (grad_active * gate_slope(hidden[:, cols])).astype(BF16)
+        grad_hidden = (grad_active * slope(cols)).astype(BF16)
         if keep_hidden is not None:
             keep_hidden[:, cols] = grad_hidden
         grad_normed = grad_normed + dot_nt(grad_hidden, w_fc[0, :, cols])
         yield
-    unit, scale = standard(middle)
     grad_middle = grad_result + norm_back(grad_normed, unit, scale, gain.get()[...])
     yield
     grad_mixed = dot_nt(grad_middle.astype(BF16), w_out.get()[0]).astype(BF16)
     yield
-    return grad_head, head_unit, grad_out, grad_normed, unit, grad_middle, grad_mixed
+    return grad_head, grad_out, grad_normed, grad_middle, grad_mixed
 
 
 def own_steps(plan, tower, units, multiplier, own_at, ins, outs):
@@ -447,22 +446,21 @@
     other_total = log_sum(multiplier * dot_nt(mine, other), 0)
     yield
     pack = ins[K.PACK, tower].get()
-    embed = pack[places[6], :]
-    logits = multiplier * dot_nt(unit_rows_of(embed)[0].astype(BF16), other)
+    unit, scale, head_unit, head_scale, unit_embed, length = (pack[places[j], :] for j in range(4, 10))
+    logits = multiplier * dot_nt(unit_embed.astype(BF16), other)
     matched = lax.broadcasted_iota(jnp.int32, logits.shape, 1) == own_at + lax.broadcasted_iota(
         jnp.int32, logits.shape, 0
     )
     grad_unit = unit_gradient(multiplier, logits, log_sum(logits, 1), other_total, matched, other)
     yield
-    hidden_at = places[7].start
-    hidden = jnp.concatenate(
-        [pack[hidden_at + j * caps : hidden_at + (j + 1) * caps, :] for j in range(plan.hidden // dim)], 1
-    )
+    slope_at = places[10].start
+    slopes = [pack[slope_at + j * caps : slope_at + (j + 1) * caps, :] for j in range(plan.hidden // dim)]
+    slopes = jnp.concatenate(slopes, 1)
     done = yield from tower_backward(
-        embed_back(grad_unit, embed), pack[places[4], :], pack[places[5], :], hidden,
-        weights_of(tower, ins), None,
-    )
-    grad_middle, grad_mixed = done[5], done[6].astype(F32)
+        embed_back(grad_unit, unit_embed, length), (unit, scale, head_unit, head_scale),
+        lambda cols: slopes[:, cols], weights_of(tower, ins), None,
+    )
+    grad_middle, grad_mixed = done[3], done[4].astype(F32)
     own_out.ref[:caps, :] = grad_middle
     w_ref = ins[K.W_QKV, tower].get()
     through_values = dot_nt(spread(grad_mixed).astype(BF16), w_ref[0, :, 2 * dim :])
@@ -617,7 +615,6 @@
         count = rows.shape[0]
         kept = [], []
         units = forward_pair(plan, rows, ins, kept, hiddens, actives)
-        embeds = [items[2] for items in kept]
         logits = multiplier * dot_nt(units[1], units[0])
         matched = lax.broadcasted_iota(jnp.int32, logits.shape, 1) == lax.broadcasted_iota(
             jnp.int32, logits.shape, 0
@@ -636,11 +633,12 @@
             dot(by_row, units[0]) + dot(by_column, units[0]),
         )
 
-        grad_embeds = [embed_back(grad_units[tower], embeds[tower]) for tower in range(2)]
+        grad_embeds = [embed_back(grad_units[tower], *kept[tower][4:]) for tower in range(2)]
         backs = run_together(
             [
                 tower_backward(
-                    grad_embeds[tower], kept[tower][0], kept[tower][1], hiddens[tower],
+                    grad_embeds[tower], kept[tower][:4],
+                    lambda cols, hidden=hiddens[tower]: gate_slope(hidden[:, cols]),
                     weights_of(tower, ins), hidden_grads[tower],
                 )
                 for tower in range(2)
@@ -656,7 +654,8 @@
             gain, bias, head_gain, head_bias = (weights[j] for j in (1, 2, 5, 6))
             active, hidden_grad = actives[tower], hidden_grads[tower]
             grad_embed, done = grad_embeds[tower], backs[tower]
-            grad_head, head_unit, grad_out, grad_normed, unit, grad_middle, grad_mixed = done
+            grad_head, grad_out, grad_normed, grad_middle, grad_mixed = done
+            unit, unused, head_unit = kept[tower][:3]
             mixed_grads.append(grad_mixed)
             middle_low = grad_middle.astype(BF16)
             normed = (unit * gain.get()[...] + bias.get()[...]).astype(BF16)
@@ -923,7 +922,7 @@
         for push in pushes:
             push.copy.wait()
 
-    where = {Place.FAR: hbm, Place.FEW: hbm, Place.RAW: hbm, Place.AUTO: vmem, Place.SCALAR: smem}
+    where = {Place.FAR: hbm, Place.FEW: hbm, Place.RAW: hbm, Place.AUTO: vmem, Place.NEAR: vmem, Place.SCALAR: smem}
     buffers = [
         (pltpu.SMEM if place == Place.FEW else pltpu.VMEM)(array.shape, array.dtype)
         for array, place in fetched
@@ -938,7 +937,7 @@
         kernel,
         name=name,
         out_shape=[
-            (pltpu.HBM if place == Place.FAR else jax.ShapeDtypeStruct)(shape, kind)
+            {Place.FAR: pltpu.HBM, Place.NEAR: pltpu.VMEM}.get(place, jax.ShapeDtypeStruct)(shape, kind)
             for shape, kind, place in outs.values()
         ],
         in_specs=[smem] * len(scalars) + [where[place] for unused, place in arrays.values()],
@@ -989,8 +988,8 @@
         (K.GAIN, 1): img_ln1_gain, (K.BIAS, 1): img_ln1_bias,
     }
     late = {(K.W_QKV, 0): w_qkv, (K.W_QKV, 1): img_w_qkv}
+    outputs_in = {(K.W_OUT, 0): w_attn_out, (K.W_OUT, 1): img_w_attn_out}
     second = {
-        (K.W_OUT, 0): w_attn_out, (K.W_OUT, 1): img_w_attn_out,
         (K.GAIN2, 0): ln2_gain, (K.BIAS2, 0): ln2_bias,
         (K.GAIN2, 1): img_ln2_gain, (K.BIAS2, 1): img_ln2_bias,
     }
@@ -1009,7 +1008,7 @@
     rows = run(
         front_body(plan),
         "front",
-        {K.ROWS: ((chips, caps, 4 * dim), BF16, Place.AUTO)},
+        {K.ROWS: ((chips, caps, 4 * dim), BF16, Place.NEAR)},
         [],
         [],
         [eot | far(first), far(late)],
@@ -1033,7 +1032,7 @@
             (K.OWN, tower): (((2 + heads) * caps, dim), F32, Place.FAR),
             (K.SCORES, tower): ((heads * caps, total), BF16, Place.FAR),
         }
-    side = run(side_body(plan), "side", side_outs, [], [], [eot | far(first), far(late), far(second | hidden_in | third)])
+    side = run(side_body(plan), "side", side_outs, [[pltpu.VMEM((caps, hidden), F32)] * 2], [], [eot | far(first), far(late), far(outputs_in | second | hidden_in | third)])
     values = exchange(side.pop(K.VALUES))
     mine, side[K.PACK, 0] = lax.optimization_barrier((mine, side[K.PACK, 0]))
     others = swap(mine, devices)
@@ -1046,8 +1045,9 @@
         [pltpu.VMEM((chips, 2, caps, 4 * dim), BF16), pltpu.SemaphoreType.DMA((2,))],
         [device, logit_scale],
         [
-            {K.MINE: (mine, Place.AUTO), K.OTHERS: (others, Place.AUTO)} | far(second),
-            far(hidden_in),
+            {K.MINE: (mine, Place.AUTO), K.OTHERS: (others, Place.AUTO)}
+            | {key: (array, Place.AUTO) for key, array in hidden_in.items()}
+            | far(outputs_in | second),
             far(third | packs),
             far(late)
             | far({(name, tower): side[name, tower] for name in (K.NORMED, K.PROBS, K.UNIT) for tower in (0, 1)}),
@@ -1066,14 +1066,14 @@
         for name, source in ((K.PROBS, side), (K.PACK, side), (K.OWN, middle), (K.SCORES, middle)):
             attended[name, tower] = source[name, tower]
         tail_outs |= {
-            (K.PART, tower): ((share_rows, LANES), F32, Place.FAR),
+            (K.PART, tower): ((share_rows, LANES), F32, Place.NEAR),
             (K.INPUT, tower): ((length, caps, dim), F32, Place.FAR),
         }
     tail_outs |= {
         K.HEAD: ((plan.head_rows_out, LANES), F32, Place.FAR),
-        K.WINDOWS: ((count, LANES), BF16, Place.FAR),
-        K.QUERIES: ((count, 2 * dim), BF16, Place.FAR),
-        K.VALUES: ((2, plan.pad, dim), F32, Place.FAR),
+        K.WINDOWS: ((count, LANES), BF16, Place.NEAR),
+        K.QUERIES: ((count, 2 * dim), BF16, Place.NEAR),
+        K.VALUES: ((2, plan.pad, dim), F32, Place.NEAR),
     }
     tail = run(
         tail_body(plan),
@@ -1095,7 +1095,7 @@
         [
             eot | far(first),
             far(attended),
-            far({K.ROWS: middle[K.ROWS]} | second | hidden_in),
+            far({K.ROWS: middle[K.ROWS]} | outputs_in | second | hidden_in),
             far(third),
             far({K.VALUES: values.reshape(count, width)})
             | {key: (array, Place.RAW) for key, array in late.items()},
@@ -1116,7 +1116,7 @@
         ],
         [device],
         [
-            far({name: tail[name] for name in names})
+            {name: (tail[name], Place.AUTO) for name in names}
             | {K.SENT: (sent.reshape(count, -1), Place.AUTO)}
             | {K.SWAPPED: (swapped.reshape(count, -1), Place.AUTO)},
         ],

time: 69 us -> 66.9 us (0.970)
  Pallas kernels: 39.4 us -> 36.9 us
    pallas_call x5, Pallas kernels: 39.4 us -> 36.9 us  [run(): pl.pallas_call(kernel, name=name, out_shape=[{Place.FAR: pltpu.HBM, Place...]
    all_to_all x2, waiting for transfers between devices: 2 us -> 2.8 us  [exchange(): return lax.all_to_all(array, 'dp', split_axis=0, concat_axis=0, tiled=True)]
  transfers between devices with their start and end apart: 5 -> 5, of which waited for: 4 -> 4; matrix products, arithmetic and copies ran while one was open for 0% -> 0% of each run, Pallas kernels for 48% -> 47%
where the time goes in v2:
time: 66.9 us; the launch traced here: 66.5 us
  Pallas kernels  36.9 us (55%)
  starting transfers between devices  17.3 us (26%)
  waiting for transfers between devices  10.7 us (16%)
  between operations  1.55 us (2%)
    pallas_call x5, Pallas kernels, run(): pl.pallas_call(kernel, name=name, out_shape=[{Place.FAR: pltpu.HBM, Place...  36.9 us
    all_to_all x2, starting transfers between devices, exchange(): return lax.all_to_all(array, 'dp', split_axis=0, concat_axis=0, tiled=True)  8.61 us
    all_to_all x1, starting transfers between devices, exchange_by_core(): lax.all_to_all(array, 'dp', split_axis=0, concat_axis=0, tiled=True, axis...  8.33 us
    all_to_all x1, waiting for transfers between devices, exchange_by_core(): lax.all_to_all(array, 'dp', split_axis=0, concat_axis=0, tiled=True, axis...  5.58 us
    all_to_all x2, waiting for transfers between devices, exchange(): return lax.all_to_all(array, 'dp', split_axis=0, concat_axis=0, tiled=True)  2.8 us
    ppermute x2, waiting for transfers between devices, swap(): return lax.ppermute(array, 'dp', [(i, i ^ 1) for i in range(devices)])  2.37 us
  transfers between devices with their start and end apart: 5, of which 4 were waited for; matrix products, arithmetic and copies ran while one was open for 0% of the time, Pallas kernels for 47%

profile of v2, /device:TPU:0, one launch (start us, length us, event | category | flops | bytes accessed | tf_op | source)
XLA Modules:
  0.0 66.5 jit_solution(9901199263896408224)
XLA Ops:
  0.6 4.0 %front.1 = bf16[16,8,1536]{2,1,0:T(8,128)(2,1)} custom-call(s32[8]{0:T(128)} %refs_2_.1, bf16[77,8,384]{2,1,0:T(8,128)(2,1)} %bitcast.12, bf16[50,8,384]{2,1,0:T(8,128)(2,1)} %bitcast.15, f32[1,384]{1,0:T(1,128)} %refs_5_.7, f32[1,384]{1,0:T(1,128)} %refs_6_.7, f32[1,384]{1,0:T(1,128)} %refs_7_.7, f32[1,384]{1,0:T(1,128)} %refs_8_.7, ...), custom_call_target="tpu_custom_call" | custom-call | tf_op jit(solution)/shard_map/front/pallas_call | solution.py:936
  4.6 8.3 %all-to-all-start = ((bf16[16,8,1536]{2,1,0:T(8,128)(2,1)}), bf16[16,8,1536]{2,1,0:T(8,128)(2,1)S(1)}, u32[]{:S(2)}, u32[]{:S(2)}) async-start(bf16[16,8,1536]{2,1,0:T(8,128)(2,1)} %front.1), calls=%async_computation | async-start | bytes 786432 | tf_op jit(solution)/shard_map/all_to_all | solution.py:957
  13.0 0.0 copy-start
  13.0 0.0 copy-start.1
  13.0 7.0 %side.1 = (bf16[32,8,640]{2,1,0:T(8,128)(2,1)}, bf16[616,384]{1,0:T(8,128)(2,1)}, bf16[616,384]{1,0:T(8,128)(2,1)}, f32[48,616]{1,0:T(8,128)}, f32[192,384]{1,0:...) custom-call(s32[8]{0:T(128)} %refs_2_.1, ...), custom_call_target="tpu_custom_call" | custom-call | tf_op jit(solution)/shard_map/side/pallas_call | solution.py:936
  20.0 5.6 %all-to-all-done.refs_2_ = bf16[16,8,1536]{2,1,0:T(8,128)(2,1)S(1)} async-done(((bf16[16,8,1536]{2,1,0:T(8,128)(2,1)}), bf16[16,8,1536]{2,1,0:T(8,128)(2,1)S(1)}, u32[]{:S(2)}, u32[]{:S(2)}) %all-to-all-start) | async-done | bytes 393248 | tf_op jit(solution)/shard_map/all_to_all | solution.py:957
  25.6 2.6 %all-to-all-start.1 = ((bf16[32,8,640]{2,1,0:T(8,128)(2,1)}), bf16[32,8,640]{2,1,0:T(8,128)(2,1)S(1)}, u32[]{:S(2)}, u32[]{:S(2)}) async-start(bf16[32,8,640]{2,1,0:T(8,128)(2,1)} %get-tuple-element.56), calls=%async_computation.1 | async-start | bytes 655360 | tf_op jit(solution)/shard_map/all_to_all | solution.py:952
  28.2 0.3 collective-permute-start
  29.1 0.8 %collective-permute-done.refs_3_ = bf16[16,8,1536]{2,1,0:T(8,128)(2,1)S(1)} collective-permute-done((bf16[16,8,1536]{2,1,0:T(8,128)(2,1)S(1)}, bf16[16,8,1536]{2,1,0:T(8,128)(2,1)S(1)}, u32[]{:S(2)}, u32[]{:S(2)}) %collective-permute-start) | collective-permute-done | bytes 393248 | tf_op jit(solution)/shard_map/ppermute | solution.py:963
  30.0 0.0 copy-done
  30.0 0.0 copy-done.1
  30.0 10.7 %middle.1 = (bf16[32,8,1152]{2,1,0:T(8,128)(2,1)}, bf16[256,1536]{1,0:T(8,128)(2,1)}, f32[64,384]{1,0:T(8,128)}, bf16[48,616]{1,0:T(8,128)(2,1)}, f32[64,384]{1,0:T(8,128)}, /*index=5*/bf16[48,400]{1,0:T(8,128)(2,1)}) custom-call(s32[1]{0:T(128)} %bitcast.refs_0_, f32[1]{0:T(128)S(6)} %copy.33.refs_1_, bf16[16,8,1536]{2,1,0:T(8,128)(2,1)S(1)} %all-to-all-done.refs_2_, ...), custom_call_target="tpu_custom_call" | custom-call | tf_op jit(solution)/shard_map/middle/pallas_call | solution.py:936
  40.6 0.0 all-to-all-done.1
  40.7 0.0 copy-start.2
  40.7 6.0 %all-to-all-start.2 = ((bf16[32,8,1152]{2,1,0:T(8,128)(2,1)}), bf16[32,8,1152]{2,1,0:T(8,128)(2,1)S(1)}, u32[]{:S(2)}, u32[]{:S(2)}) async-start(bf16[32,8,1152]{2,1,0:T(8,128)(2,1)} %get-tuple-element.63), calls=%async_computation.2 | async-start | bytes 1179648 | tf_op jit(solution)/shard_map/all_to_all | solution.py:952
  46.7 0.0 copy-done.2
  46.7 13.7 %tail.1 = (f32[1]{0:T(128)}, f32[1]{0:T(128)}, f32[440,128]{1,0:T(8,128)S(1)}, f32[77,8,384]{2,1,0:T(8,128)}, f32[440,128]{1,0:T(8,128)S(1)}, /*index=5*/f32[50,...) custom-call(s32[1]{0:T(128)} %bitcast.refs_0_, ...), custom_call_target="tpu_custom_call" | custom-call | tf_op jit(solution)/shard_map/tail/pallas_call | solution.py:936
  60.4 2.8 %all-to-all-done.2 = bf16[32,8,1152]{2,1,0:T(8,128)(2,1)S(1)} async-done(((bf16[32,8,1152]{2,1,0:T(8,128)(2,1)}), bf16[32,8,1152]{2,1,0:T(8,128)(2,1)S(1)}, u32[]{:S(2)}, u32[]{:S(2)}) %all-to-all-start.2) | async-done | bytes 589856 | tf_op jit(solution)/shard_map/all_to_all | solution.py:952
  63.3 0.1 collective-permute-start.1
  63.3 1.5 %collective-permute-done.1 = bf16[32,8,512]{2,1,0:T(8,128)(2,1)S(1)} collective-permute-done((bf16[32,8,512]{2,1,0:T(8,128)(2,1)S(1)}, bf16[32,8,512]{2,1,0:T(8,128)(2,1)S(1)}, u32[]{:S(2)}, u32[]{:S(2)}) %collective-permute-start.1) | collective-permute-done | bytes 262176 | tf_op jit(solution)/shard_map/ppermute | solution.py:963
  64.9 1.5 %last.1 = (f32[1,55344]{1,0:T(1,128)}, f32[1,55344]{1,0:T(1,128)}) custom-call(s32[1]{0:T(128)} %bitcast.refs_0_, f32[440,128]{1,0:T(8,128)S(1)} %get-tuple-element.61.refs_1_, f32[440,128]{1,0:T(8,128)S(1)} %get-tuple-element.62.refs_2_, bf16[256,128]{1,0:T(8,128)(2,1)S(1)} %get-tuple-element.65.refs_3_, bf16[256,768]{1,0:T(8,128)(2,1)S(1)} %get-tuple-element.66.refs_4_, ...), custom_call_target="tpu_custom_call" | custom-call | tf_op jit(solution)/shard_map/last/pallas_call | solution.py:936
  (1 shorter events, 0.0 us)
Async XLA Ops:
  4.6 21.0 %all-to-all-start = ((bf16[16,8,1536]{2,1,0:T(8,128)(2,1)}), bf16[16,8,1536]{2,1,0:T(8,128)(2,1)S(1)}, u32[]{:S(2)}, u32[]{:S(2)}) async-start(bf16[16,8,1536]{2,1,0:T(8,128)(2,1)} %front.1), calls=%async_computation | async-start | bytes 786432 | tf_op jit(solution)/shard_map/all_to_all | solution.py:957
  13.0 17.0 %copy-start = (bf16[1,384,1536]{2,1,0:T(8,128)(2,1)S(1)}, bf16[1,384,1536]{2,1,0:T(8,128)(2,1)}, u32[]{:S(2)}) copy-start(bf16[1,384,1536]{2,1,0:T(8,128)(2,1)} %refs_24_.3) | copy-start | bytes 3538948
  13.0 17.0 %copy-start.1 = (bf16[1,384,1536]{2,1,0:T(8,128)(2,1)S(1)}, bf16[1,384,1536]{2,1,0:T(8,128)(2,1)}, u32[]{:S(2)}) copy-start(bf16[1,384,1536]{2,1,0:T(8,128)(2,1)} %refs_25_.1) | copy-start | bytes 3538948
  25.6 15.1 %all-to-all-start.1 = ((bf16[32,8,640]{2,1,0:T(8,128)(2,1)}), bf16[32,8,640]{2,1,0:T(8,128)(2,1)S(1)}, u32[]{:S(2)}, u32[]{:S(2)}) async-start(bf16[32,8,640]{2,1,0:T(8,128)(2,1)} %get-tuple-element.56), calls=%async_computation.1 | async-start | bytes 655360 | tf_op jit(solution)/shard_map/all_to_all | solution.py:952
  28.2 1.8 %collective-permute-start = (bf16[16,8,1536]{2,1,0:T(8,128)(2,1)S(1)}, bf16[16,8,1536]{2,1,0:T(8,128)(2,1)S(1)}, u32[]{:S(2)}, u32[]{:S(2)}) collective-permute-start(bf16[16,8,1536]{2,1,0:T(8,128)(2,1)S(1)} %all-to-all-done.refs_2_), channel_id=1, source_target_pairs={{0,1},{1,0},{2,3},{3,2},{4,5},{5,4},{6,7},{7,6},{8,9},{9,8},{10,11... | collective-permute-start | bytes 1179656 | tf_op jit(solution)/shard_map/ppermute | solution.py:963
  40.7 6.0 %copy-start.2 = (bf16[32,8,640]{2,1,0:T(8,128)(2,1)}, bf16[32,8,640]{2,1,0:T(8,128)(2,1)S(1)}, u32[]{:S(2)}) copy-start(bf16[32,8,640]{2,1,0:T(8,128)(2,1)S(1)} %all-to-all-done.1) | copy-start | bytes 983044
  40.7 22.6 %all-to-all-start.2 = ((bf16[32,8,1152]{2,1,0:T(8,128)(2,1)}), bf16[32,8,1152]{2,1,0:T(8,128)(2,1)S(1)}, u32[]{:S(2)}, u32[]{:S(2)}) async-start(bf16[32,8,1152]{2,1,0:T(8,128)(2,1)} %get-tuple-element.63), calls=%async_computation.2 | async-start | bytes 1179648 | tf_op jit(solution)/shard_map/all_to_all | solution.py:952
  63.3 1.6 %collective-permute-start.1 = (bf16[32,8,512]{2,1,0:T(8,128)(2,1)S(1)}, bf16[32,8,512]{2,1,0:T(8,128)(2,1)S(1)}, u32[]{:S(2)}, u32[]{:S(2)}) collective-permute-start(bf16[32,8,512]{2,1,0:T(8,128)(2,1)S(1)} %slice.6), channel_id=1, source_target_pairs={{0,1},{1,0},{2,3},{3,2},{4,5},{5,4},{6,7},{7,6},{8,9},{9,8},{10,11... | collective-permute-start | bytes 786440 | tf_op jit(solution)/shard_map/ppermute | solution.py:963

commit v3 on v2

--- a/solution.py
+++ b/solution.py
@@ -61,6 +61,7 @@
     W_FC_OUT = enum.auto()
     W_OUT = enum.auto()
     W_QKV = enum.auto()
+    W_QUERY = enum.auto()
     WINDOWS = enum.auto()
     X = enum.auto()
 
@@ -75,6 +76,14 @@
 
 def dot_tn(left, right):
     return lax.dot_general(left, right, (((0,), (0,)), ((), ())), preferred_element_type=F32)
+
+
+def summed_through(rows, weights):
+    total = dot(jnp.ones((8, rows.shape[0]), BF16), rows)
+    high = total.astype(BF16)
+    low = (total - high.astype(F32)).astype(BF16)
+    both = dot_nt(jnp.concatenate([high, low], 0), weights)
+    return both[:1] + both[8:9]
 
 
 def standard(values):
@@ -120,7 +129,7 @@
 
 
 class Plan:
-    def __init__(self, dim, hidden, devices):
+    def __init__(self, dim, hidden, devices, caps):
         self.dim, self.hidden, self.devices = dim, hidden, devices
         self.row = 3 * dim
         self.qkv_at = 2 * dim
@@ -135,12 +144,20 @@
         self.roots = -(-self.out_at // self.share)
         self.rows_out = -(-(self.share // LANES + 2) // 8) * 8
         self.head_rows_out = -(-(self.head_share // LANES + 2) // 8) * 8
-        self.window = self.share // self.row + 2
-        self.pad = -(-self.window // 8) * 8
-        self.used = self.pad + self.window
+        ends = [min((d + 1) * self.share - self.qkv_at, dim * self.row) for d in range(self.roots)]
+        self.window = max((end - 1) // self.row + 1 - self.column(d) for d, end in enumerate(ends))
+        self.used = 2 * self.window
         self.piece = LANES - self.used
+        self.extra = dim // caps
+        self.spare, at = [], 0
+        for h in reversed(range(dim // HEAD_DIM - 1)):
+            start = self.used + min(max(self.used - h * self.piece, 0), self.piece)
+            size = min(LANES - start, self.extra - at)
+            self.spare.append((h, start, size, at))
+            at += size
         assert self.piece > 0 and -(-self.used // self.piece) < dim // HEAD_DIM
-        assert self.total % devices == 0 and self.head_total % devices == 0
+        assert at == self.extra <= LANES
+        self.spare_from = min(h for h, unused, size, unused in self.spare if size > 0)
 
     def column(self, device):
         if isinstance(device, int):
@@ -148,19 +165,24 @@
         return jnp.minimum(jnp.maximum(device * self.share - self.qkv_at, 0) // self.row, self.dim - 1)
 
 
-def window_tiles(plan, text, image, device, caps):
+def window_tiles(plan, text, image, device, caps, extra):
     dim = text.shape[1]
     first = plan.column(device)
     lane = lax.broadcasted_iota(jnp.int32, (text.shape[0], LANES), 1)
     left = pltpu.roll(text, (dim - first) % dim, 1)[:, :LANES]
-    right = pltpu.roll(image, (dim - first + plan.pad) % dim, 1)[:, :LANES]
-    both = jnp.where(lane < plan.pad, left, right)
+    right = pltpu.roll(image, (dim - first + plan.window) % dim, 1)[:, :LANES]
+    both = jnp.where(lane < plan.window, left, right)
     heads = text.shape[0] // caps
     lane, last = lane[:caps], both[(heads - 1) * caps :]
     tiles = []
     for h in range(heads - 1):
         moved = pltpu.roll(last, (plan.used - h * plan.piece) % LANES, 1)
-        tiles.append(jnp.where(lane < plan.used, both[h * caps : (h + 1) * caps], moved).astype(BF16))
+        tile = jnp.where(lane < plan.used, both[h * caps : (h + 1) * caps], moved)
+        for at, start, size, taken in plan.spare if extra is not None else ():
+            if at == h and size > 0:
+                moved = pltpu.roll(extra, (start - taken) % LANES, 1)
+                tile = jnp.where((lane >= start) & (lane < start + size), moved, tile)
+        tiles.append(tile.astype(BF16))
     return jnp.concatenate(tiles, 1)
 
 
@@ -174,14 +196,40 @@
     return whole.astype(BF16)
 
 
+def fold_row(row, caps):
+    dim = row.shape[1]
+    step = dim // caps
+    rows = [pltpu.roll(row, (dim - i * step) % dim, 1)[:, :LANES] for i in range(caps)]
+    return jnp.concatenate(rows, 0)
+
+
+def spare_row(plan, sums, first, dim):
+    caps = sums.shape[0]
+    lane = lax.broadcasted_iota(jnp.int32, (caps, LANES), 1)
+    folded = jnp.zeros((caps, LANES), F32)
+    for h, start, size, taken in plan.spare:
+        if size > 0:
+            tile = sums[:, (h - first) * LANES : (h - first + 1) * LANES]
+            moved = pltpu.roll(tile, (taken - start) % LANES, 1)
+            folded = jnp.where((lane >= taken) & (lane < taken + size), moved, folded)
+    wide = jnp.concatenate([folded, jnp.zeros((caps, dim - LANES), F32)], 1)
+    lane = lax.broadcasted_iota(jnp.int32, (1, dim), 1)
+    row = jnp.zeros((1, dim), F32)
+    for i in range(caps):
+        moved = pltpu.roll(wide[i : i + 1], i * plan.extra, 1) if i else wide[:1]
+        row = jnp.where((lane >= i * plan.extra) & (lane < (i + 1) * plan.extra), moved, row)
+    return row
+
+
 def pack_windows(plan, target, text, image, caps, common):
     width = (text.shape[0] // caps - 1) * LANES
     held = plan.roots + plan.roots % 2
 
     def fill(device, core):
-        target[device, :, :width] = window_tiles(plan, text, image, device, caps)
+        extra = None if common is None else common[core][1]
+        target[device, :, :width] = window_tiles(plan, text, image, device, caps, extra)
         if common is not None:
-            target[device, :, width:] = common[core]
+            target[device, :, width:] = common[core][0]
 
     if held <= 16:
         for device in range(held):
@@ -230,18 +278,18 @@
     total = seq * caps
     heads = dim // HEAD_DIM
     source = x.reshape(total, dim)
-    unit, unused = standard(source.astype(F32))
-    yield
-    gain, bias = ins[K.GAIN, tower].get()[...], ins[K.BIAS, tower].get()[...]
-    normed = (unit * gain + bias).astype(BF16)
     chosen, column, pick_at = picked_columns(caps, total, picked)
     last_at = pick_at
     if last is not picked:
         unused, unused, last_at = picked_columns(caps, total, last)
     pooled = dot(chosen, source)
+    unit, unused = standard(source.astype(F32))
     yield
     pooled_unit, unused = standard(pooled)
+    gain, bias = ins[K.GAIN, tower].get()[...], ins[K.BIAS, tower].get()[...]
     pooled_normed = (pooled_unit * gain + bias).astype(BF16)
+    normed = (unit * gain + bias).astype(BF16)
+    yield
     w_ref = ins[K.W_QKV, tower].get()
     query = dot(pooled_normed, w_ref[0, :, :dim]).astype(BF16).astype(F32)
     yield
@@ -488,8 +536,7 @@
     gain_part = jnp.sum(units, 0, keepdims=True) + jnp.sum(
         through_query * pack[places[2], :], 0, keepdims=True
     )
-    bias_part = jnp.sum(through_values, 0, keepdims=True) + jnp.sum(through_query, 0, keepdims=True)
-    return spread_keys, grad_query, (gain_part, bias_part)
+    return spread_keys, grad_query, gain_part
 
 
 def forward_pair(plan, rows, ins, kept, hidden, active):
@@ -514,7 +561,7 @@
     ]
 
 
-def join_rows(scalars, ins, scratch):
+def join_rows(scalars, ins, outs, scratch):
     for copy in row_copies(scalars, ins, scratch):
         copy.start()
 
@@ -539,12 +586,7 @@
         parts = run_together(
             [own_steps(plan, tower, units, multiplier, own_at, ins, outs) for tower in range(2)]
         )
-        tiles = dim // LANES
-        common = []
-        for unused, query, sums in parts:
-            small = [row[:, j * LANES : (j + 1) * LANES] for row in sums for j in range(tiles)]
-            small.append(jnp.zeros((caps - 2 * tiles, LANES), F32))
-            common.append(jnp.concatenate([query, jnp.concatenate(small, 0).astype(BF16)], 1))
+        common = [(query, fold_row(gain_part, caps)) for unused, query, gain_part in parts]
         keys_t, keys_i = parts[0][0], parts[1][0]
         pack_windows(plan, outs[K.SEND].ref, keys_t, keys_i, caps, common)
         outs[K.SEND].push_part(held)
@@ -552,22 +594,30 @@
     return body
 
 
-def late_weights(ins, scratch):
-    parts, sems = scratch[-2:]
-    dim = parts.shape[1]
+def late_weights(ins, outs, scratch):
+    value, sems = scratch[-2:]
+    dim = value.shape[1]
     return [
         pltpu.make_async_copy(
-            ins[K.W_QKV, tower].ref.at[0, :, pl.ds(0, dim)], parts.at[tower], sems.at[tower]
+            ins[K.W_QKV, tower].ref.at[0, :, pl.ds(at, dim)], target.at[tower], sems.at[2 * part + tower]
         )
+        for part, (at, target) in enumerate(((0, outs[K.W_QUERY].ref), (2 * dim, value)))
         for tower in range(2)
     ]
 
 
 def tail_ahead(plan):
-    def ahead(scalars, ins, scratch):
+    def ahead(scalars, ins, outs, scratch):
+        copies = late_weights(ins, outs, scratch)
+
         @pl.when(scalars[0][0] < plan.roots)
         def _():
-            for copy in late_weights(ins, scratch):
+            for copy in copies[:2]:
+                copy.start()
+
+        @pl.when(scalars[0][0] == 0)
+        def _():
+            for copy in copies[2:]:
                 copy.start()
 
     return ahead
@@ -706,13 +756,20 @@
         outs[K.HEAD].ref[...] = take_rows(flat_head, head_start, plan.head_rows_out)
         outs[K.HEAD].push()
 
-        query_t, query_i = late_weights(ins, scratch)
+        copies = late_weights(ins, outs, scratch)
+
+        @pl.when(device == 0)
+        def _():
+            for tower in range(2):
+                copies[2 + tower].wait()
+                outs[K.BIAS].ref[tower : tower + 1, :] = summed_through(mixed_grads[tower], late[tower])
+
         values = ins[K.VALUES].get()
 
         @pl.when(device < plan.roots)
         def _():
-            query_t.wait()
-            query_i.wait()
+            for copy in copies[:2]:
+                copy.wait()
             first = plan.column(device)
             lane = lax.broadcasted_iota(jnp.int32, (count, LANES), 1)
             picked_rows = []
@@ -722,20 +779,20 @@
                 unit, unused = standard(pooled)
                 normed = unit * gain[...] + bias[...]
                 outs[K.QUERIES].ref[:, tower * dim : (tower + 1) * dim] = dot(
-                    normed.astype(BF16), late[tower]
+                    normed.astype(BF16), outs[K.W_QUERY].ref[tower]
                 ).astype(BF16)
-                shift = lax.rem(dim - first + tower * plan.pad, dim)
+                shift = lax.rem(dim - first + tower * plan.window, dim)
                 picked_rows.append(pltpu.roll(normed, shift, 1)[:, :LANES])
             end = last_head(plan, values, dim // HEAD_DIM)
             for j in range(dim // LANES):
                 cols = slice(j * LANES, (j + 1) * LANES)
                 block = window_product(plan, values, end, mixed_grads, (0, 0), j)
                 for tower in range(2):
-                    at = tower * plan.pad
+                    at = tower * plan.window
                     outs[K.VALUES].ref[tower, :, cols] = block[
-                        at : at + plan.pad, tower * LANES : (tower + 1) * LANES
+                        at : at + plan.window, tower * LANES : (tower + 1) * LANES
                     ]
-            outs[K.WINDOWS].ref[...] = jnp.where(lane < plan.pad, picked_rows[0], picked_rows[1]).astype(BF16)
+            outs[K.WINDOWS].ref[...] = jnp.where(lane < plan.window, picked_rows[0], picked_rows[1]).astype(BF16)
 
     return body
 
@@ -771,32 +828,39 @@
             for tower in range(2):
                 store(tower, parts[tower][...])
 
-        names = K.SENT, K.SWAPPED, K.WINDOWS, K.QUERIES, K.VALUES
-        sent_ref, swapped, windows, queries, value_part = (
+        names = K.SENT, K.SWAPPED, K.WINDOWS, K.QUERIES, K.VALUES, K.W_QUERY, K.BIAS
+        sent_ref, swapped, windows, queries, value_part, w_query, bias = (
             ins[name].get() for name in names
         )
 
         @pl.when(device < plan.roots)
         def _():
-            at_query = (heads - 1) * LANES
             count = sent_ref.shape[0]
             caps = count // plan.devices
+            first = plan.spare_from
             for core in range(2):
 
                 @pl.when(device % 2 == core)
                 def _():
-                    received = sent_ref[:, at_query:], swapped[...]
+                    received = sent_ref[:, first * LANES :], swapped[...]
                     for tower, values in enumerate(received if core == 0 else received[::-1]):
-                        grad_query[:, tower * dim : (tower + 1) * dim] = values[:, :dim]
-                        small = values[:, dim:].astype(F32).reshape(plan.devices, caps, LANES)
-                        flat[tower, : 2 * tiles, :] = jnp.sum(small, 0)[: 2 * tiles]
+                        grad_query[:, tower * dim : (tower + 1) * dim] = values[:, -dim:]
+
+            @pl.when(device == 0)
+            def _():
+                for tower, values in enumerate((sent_ref[:, first * LANES :], swapped[...])):
+                    sums = values[:, :-dim].astype(F32).reshape(plan.devices, caps, -1)
+                    put_tile(flat.at[tower], 0, spare_row(plan, jnp.sum(sums, 0), first, dim))
+                    grads = grad_query[:, tower * dim : (tower + 1) * dim]
+                    row = summed_through(grads, w_query[tower])
+                    put_tile(flat.at[tower], tiles, row + bias[tower : tower + 1, :])
 
             query_part = dot_tn(windows[...], grad_query[...])
             end = last_head(plan, sent_ref, heads)
             for j in range(tiles):
                 put = window_product(plan, sent_ref, end, (queries, queries), (0, dim), j)
                 for tower in range(2):
-                    rows = slice(tower * plan.pad, (tower + 1) * plan.pad)
+                    rows = slice(tower * plan.window, (tower + 1) * plan.window)
                     own = slice(tower * LANES, (tower + 1) * LANES)
                     q_at = tower * dim + j * LANES
                     for part, block in enumerate(
@@ -808,7 +872,7 @@
                     ):
                         flat[
                             tower,
-                            pl.ds(2 * tiles + part * tiles + j, plan.pad, stride=3 * tiles),
+                            pl.ds(2 * tiles + part * tiles + j, plan.window, stride=3 * tiles),
                             :,
                         ] = block
             start = device * plan.share
@@ -910,7 +974,7 @@
             results[key] = pushes[-1] if place == Place.FAR else Here(target)
         own_scratch = take(len(scratch))
         if ahead is not None:
-            ahead(scalar_refs, ins, own_scratch)
+            ahead(scalar_refs, ins, results, own_scratch)
         for fetch in fetches:
             fetch.copy.start()
         body(scalar_refs, ins, results, own_scratch)
@@ -972,7 +1036,7 @@
     caps, seq, dim = text_input.shape
     img_seq = image_input.shape[1]
     devices = lax.axis_size("dp")
-    plan = Plan(dim, w_fc.shape[2], devices)
+    plan = Plan(dim, w_fc.shape[2], devices, caps)
     heads = dim // HEAD_DIM
     count = devices * caps
     hidden = plan.hidden
@@ -1018,7 +1082,7 @@
     unused, pack_rows = pack_at(dim, hidden, caps)
     side_outs = {K.VALUES: ((devices, caps, width), BF16, Place.FAR)}
     middle_outs = {
-        K.SEND: ((devices, caps, width + dim + LANES), BF16, Place.FAR),
+        K.SEND: ((devices, caps, width + dim), BF16, Place.FAR),
         K.ROWS: ((count, 4 * dim), BF16, Place.FAR),
     }
     for tower, total in enumerate(totals):
@@ -1073,7 +1137,9 @@
         K.HEAD: ((plan.head_rows_out, LANES), F32, Place.FAR),
         K.WINDOWS: ((count, LANES), BF16, Place.NEAR),
         K.QUERIES: ((count, 2 * dim), BF16, Place.NEAR),
-        K.VALUES: ((2, plan.pad, dim), F32, Place.NEAR),
+        K.VALUES: ((2, plan.window, dim), F32, Place.NEAR),
+        K.W_QUERY: ((2, dim, dim), BF16, Place.NEAR),
+        K.BIAS: ((8, dim), F32, Place.NEAR),
     }
     tail = run(
         tail_body(plan),
@@ -1089,7 +1155,7 @@
             [pltpu.VMEM((count, hidden), BF16)] * 2,
             [pltpu.VMEM((count, hidden), BF16)] * 2,
             pltpu.VMEM((2, dim, dim), BF16),
-            pltpu.SemaphoreType.DMA((2,)),
+            pltpu.SemaphoreType.DMA((4,)),
         ],
         [device, logit_scale],
         [
@@ -1103,9 +1169,9 @@
         tail_ahead(plan),
     )
     sent, tail[K.WINDOWS] = lax.optimization_barrier((sent, tail[K.WINDOWS]))
-    swapped = swap(sent[:, :, width:], devices)
-    flat_rows = max(2 * dim + plan.pad * plan.row, 2 * dim + 2 * plan.row + share_rows * LANES) // LANES
-    names = [(K.PART, 0), (K.PART, 1), K.WINDOWS, K.QUERIES, K.VALUES]
+    swapped = swap(sent[:, :, plan.spare_from * LANES :], devices)
+    flat_rows = max(2 * dim + plan.window * plan.row, 2 * dim + 2 * plan.row + share_rows * LANES) // LANES
+    names = [(K.PART, 0), (K.PART, 1), K.WINDOWS, K.QUERIES, K.VALUES, K.W_QUERY, K.BIAS]
     shares = run(
         last_body(plan),
         "last",

time: 66.9 us -> 66.3 us (level)
  waiting for transfers between devices: 10.7 us -> 8.75 us
  Pallas kernels: 36.9 us -> 38.3 us
    all_to_all x2, waiting for transfers between devices: 2.8 us -> 0.69 us  [exchange(): return lax.all_to_all(array, 'dp', split_axis=0, concat_axis=0, tiled=True)]
    pallas_call x5, Pallas kernels: 36.9 us -> 38.3 us  [run(): pl.pallas_call(kernel, name=name, out_shape=[{Place.FAR: pltpu.HBM, Place...]
  transfers between devices with their start and end apart: 5 -> 5, of which waited for: 4 -> 4; matrix products, arithmetic and copies ran while one was open for 0% -> 0% of each run, Pallas kernels for 47% -> 49%
where the time goes in v3:
time: 66.3 us; the launch traced here: 65.9 us
  Pallas kernels  38.3 us (58%)
  starting transfers between devices  17.3 us (26%)
  waiting for transfers between devices  8.75 us (13%)
  between operations  1.55 us (2%)
    pallas_call x5, Pallas kernels, run(): pl.pallas_call(kernel, name=name, out_shape=[{Place.FAR: pltpu.HBM, Place...  38.3 us
    all_to_all x2, starting transfers between devices, exchange(): return lax.all_to_all(array, 'dp', split_axis=0, concat_axis=0, tiled=True)  8.61 us
    all_to_all x1, starting transfers between devices, exchange_by_core(): lax.all_to_all(array, 'dp', split_axis=0, concat_axis=0, tiled=True, axis...  8.33 us
    all_to_all x1, waiting for transfers between devices, exchange_by_core(): lax.all_to_all(array, 'dp', split_axis=0, concat_axis=0, tiled=True, axis...  5.6 us
    ppermute x2, waiting for transfers between devices, swap(): return lax.ppermute(array, 'dp', [(i, i ^ 1) for i in range(devices)])  2.46 us
  transfers between devices with their start and end apart: 5, of which 4 were waited for; matrix products, arithmetic and copies ran while one was open for 0% of the time, Pallas kernels for 49%

profile of v3, /device:TPU:0, one launch (start us, length us, event | category | flops | bytes accessed | tf_op | source)
XLA Modules:
  0.0 65.9 jit_solution(17146316213558872398)
XLA Ops:
  0.6 3.9 %front.1 = bf16[16,8,1536]{2,1,0:T(8,128)(2,1)} custom-call(s32[8]{0:T(128)} %refs_2_.1, bf16[77,8,384]{2,1,0:T(8,128)(2,1)} %bitcast.12, bf16[50,8,384]{2,1,0:T(8,128)(2,1)} %bitcast.15, f32[1,384]{1,0:T(1,128)} %refs_5_.7, f32[1,384]{1,0:T(1,128)} %refs_6_.7, f32[1,384]{1,0:T(1,128)} %refs_7_.7, f32[1,384]{1,0:T(1,128)} %refs_8_.7, ...), custom_call_target="tpu_custom_call" | custom-call | tf_op jit(solution)/shard_map/front/pallas_call | solution.py:1000
  4.5 8.3 %all-to-all-start = ((bf16[16,8,1536]{2,1,0:T(8,128)(2,1)}), bf16[16,8,1536]{2,1,0:T(8,128)(2,1)S(1)}, u32[]{:S(2)}, u32[]{:S(2)}) async-start(bf16[16,8,1536]{2,1,0:T(8,128)(2,1)} %front.1), calls=%async_computation | async-start | bytes 786432 | tf_op jit(solution)/shard_map/all_to_all | solution.py:1021
  12.9 0.0 copy-start
  12.9 0.0 copy-start.1
  12.9 7.0 %side.1 = (bf16[32,8,640]{2,1,0:T(8,128)(2,1)}, bf16[616,384]{1,0:T(8,128)(2,1)}, bf16[616,384]{1,0:T(8,128)(2,1)}, f32[48,616]{1,0:T(8,128)}, f32[192,384]{1,0:...) custom-call(s32[8]{0:T(128)} %refs_2_.1, ...), custom_call_target="tpu_custom_call" | custom-call | tf_op jit(solution)/shard_map/side/pallas_call | solution.py:1000
  19.9 5.6 %all-to-all-done.refs_2_ = bf16[16,8,1536]{2,1,0:T(8,128)(2,1)S(1)} async-done(((bf16[16,8,1536]{2,1,0:T(8,128)(2,1)}), bf16[16,8,1536]{2,1,0:T(8,128)(2,1)S(1)}, u32[]{:S(2)}, u32[]{:S(2)}) %all-to-all-start) | async-done | bytes 393248 | tf_op jit(solution)/shard_map/all_to_all | solution.py:1021
  25.5 2.6 %all-to-all-start.1 = ((bf16[32,8,640]{2,1,0:T(8,128)(2,1)}), bf16[32,8,640]{2,1,0:T(8,128)(2,1)S(1)}, u32[]{:S(2)}, u32[]{:S(2)}) async-start(bf16[32,8,640]{2,1,0:T(8,128)(2,1)} %get-tuple-element.58), calls=%async_computation.1 | async-start | bytes 655360 | tf_op jit(solution)/shard_map/all_to_all | solution.py:1016
  28.1 0.3 collective-permute-start
  29.0 0.8 %collective-permute-done.refs_3_ = bf16[16,8,1536]{2,1,0:T(8,128)(2,1)S(1)} collective-permute-done((bf16[16,8,1536]{2,1,0:T(8,128)(2,1)S(1)}, bf16[16,8,1536]{2,1,0:T(8,128)(2,1)S(1)}, u32[]{:S(2)}, u32[]{:S(2)}) %collective-permute-start) | collective-permute-done | bytes 393248 | tf_op jit(solution)/shard_map/ppermute | solution.py:1027
  29.9 0.0 copy-done
  29.9 0.0 copy-done.1
  29.9 10.8 %middle.1 = (bf16[32,8,1024]{2,1,0:T(8,128)(2,1)}, bf16[256,1536]{1,0:T(8,128)(2,1)}, f32[64,384]{1,0:T(8,128)}, bf16[48,616]{1,0:T(8,128)(2,1)}, f32[64,384]{1,0:T(8,128)}, /*index=5*/bf16[48,400]{1,0:T(8,128)(2,1)}) custom-call(s32[1]{0:T(128)} %bitcast.refs_0_, f32[1]{0:T(128)S(6)} %copy.33.refs_1_, bf16[16,8,1536]{2,1,0:T(8,128)(2,1)S(1)} %all-to-all-done.refs_2_, ...), custom_call_target="tpu_custom_call" | custom-call | tf_op jit(solution)/shard_map/middle/pallas_call | solution.py:1000
  40.7 0.0 all-to-all-done.1
  40.7 0.0 copy-start.2
  40.7 6.0 %all-to-all-start.2 = ((bf16[32,8,1024]{2,1,0:T(8,128)(2,1)}), bf16[32,8,1024]{2,1,0:T(8,128)(2,1)S(1)}, u32[]{:S(2)}, u32[]{:S(2)}) async-start(bf16[32,8,1024]{2,1,0:T(8,128)(2,1)} %get-tuple-element.65), calls=%async_computation.2 | async-start | bytes 1048576 | tf_op jit(solution)/shard_map/all_to_all | solution.py:1016
  46.7 0.0 copy-done.2
  46.7 14.7 %tail.1 = (f32[1]{0:T(128)}, f32[1]{0:T(128)}, f32[440,128]{1,0:T(8,128)S(1)}, f32[77,8,384]{2,1,0:T(8,128)}, f32[440,128]{1,0:T(8,128)S(1)}, /*index=5*/f32[50,...) custom-call(s32[1]{0:T(128)} %bitcast.refs_0_, ...), custom_call_target="tpu_custom_call" | custom-call | tf_op jit(solution)/shard_map/tail/pallas_call | solution.py:1000
  61.4 0.7 %all-to-all-done.2 = bf16[32,8,1024]{2,1,0:T(8,128)(2,1)S(1)} async-done(((bf16[32,8,1024]{2,1,0:T(8,128)(2,1)}), bf16[32,8,1024]{2,1,0:T(8,128)(2,1)S(1)}, u32[]{:S(2)}, u32[]{:S(2)}) %all-to-all-start.2) | async-done | bytes 524320 | tf_op jit(solution)/shard_map/all_to_all | solution.py:1016
  62.1 0.1 collective-permute-start.1
  62.2 1.6 %collective-permute-done.1 = bf16[32,8,640]{2,1,0:T(8,128)(2,1)S(1)} collective-permute-done((bf16[32,8,640]{2,1,0:T(8,128)(2,1)S(1)}, bf16[32,8,640]{2,1,0:T(8,128)(2,1)S(1)}, u32[]{:S(2)}, u32[]{:S(2)}) %collective-permute-start.1) | collective-permute-done | bytes 327712 | tf_op jit(solution)/shard_map/ppermute | solution.py:1027
  63.8 2.0 %last.1 = (f32[1,55344]{1,0:T(1,128)}, f32[1,55344]{1,0:T(1,128)}) custom-call(s32[1]{0:T(128)} %bitcast.refs_0_, f32[440,128]{1,0:T(8,128)S(1)} %get-tuple-element.63.refs_1_, f32[440,128]{1,0:T(8,128)S(1)} %get-tuple-element.64.refs_2_, bf16[256,128]{1,0:T(8,128)(2,1)S(1)} %get-tuple-element.67.refs_3_, bf16[256,768]{1,0:T(8,128)(2,1)S(1)} %get-tuple-element.68.refs_4_, ...), custom_call_target="tpu_custom_call" | custom-call | tf_op jit(solution)/shard_map/last/pallas_call | solution.py:1000
  (1 shorter events, 0.0 us)
Async XLA Ops:
  4.5 21.0 %all-to-all-start = ((bf16[16,8,1536]{2,1,0:T(8,128)(2,1)}), bf16[16,8,1536]{2,1,0:T(8,128)(2,1)S(1)}, u32[]{:S(2)}, u32[]{:S(2)}) async-start(bf16[16,8,1536]{2,1,0:T(8,128)(2,1)} %front.1), calls=%async_computation | async-start | bytes 786432 | tf_op jit(solution)/shard_map/all_to_all | solution.py:1021
  12.9 17.0 %copy-start = (bf16[1,384,1536]{2,1,0:T(8,128)(2,1)S(1)}, bf16[1,384,1536]{2,1,0:T(8,128)(2,1)}, u32[]{:S(2)}) copy-start(bf16[1,384,1536]{2,1,0:T(8,128)(2,1)} %refs_24_.3) | copy-start | bytes 3538948
  12.9 17.0 %copy-start.1 = (bf16[1,384,1536]{2,1,0:T(8,128)(2,1)S(1)}, bf16[1,384,1536]{2,1,0:T(8,128)(2,1)}, u32[]{:S(2)}) copy-start(bf16[1,384,1536]{2,1,0:T(8,128)(2,1)} %refs_25_.1) | copy-start | bytes 3538948
  25.5 15.2 %all-to-all-start.1 = ((bf16[32,8,640]{2,1,0:T(8,128)(2,1)}), bf16[32,8,640]{2,1,0:T(8,128)(2,1)S(1)}, u32[]{:S(2)}, u32[]{:S(2)}) async-start(bf16[32,8,640]{2,1,0:T(8,128)(2,1)} %get-tuple-element.58), calls=%async_computation.1 | async-start | bytes 655360 | tf_op jit(solution)/shard_map/all_to_all | solution.py:1016
  28.1 1.8 %collective-permute-start = (bf16[16,8,1536]{2,1,0:T(8,128)(2,1)S(1)}, bf16[16,8,1536]{2,1,0:T(8,128)(2,1)S(1)}, u32[]{:S(2)}, u32[]{:S(2)}) collective-permute-start(bf16[16,8,1536]{2,1,0:T(8,128)(2,1)S(1)} %all-to-all-done.refs_2_), channel_id=1, source_target_pairs={{0,1},{1,0},{2,3},{3,2},{4,5},{5,4},{6,7},{7,6},{8,9},{9,8},{10,11... | collective-permute-start | bytes 1179656 | tf_op jit(solution)/shard_map/ppermute | solution.py:1027
  40.7 6.0 %copy-start.2 = (bf16[32,8,640]{2,1,0:T(8,128)(2,1)}, bf16[32,8,640]{2,1,0:T(8,128)(2,1)S(1)}, u32[]{:S(2)}) copy-start(bf16[32,8,640]{2,1,0:T(8,128)(2,1)S(1)} %all-to-all-done.1) | copy-start | bytes 983044
  40.7 21.4 %all-to-all-start.2 = ((bf16[32,8,1024]{2,1,0:T(8,128)(2,1)}), bf16[32,8,1024]{2,1,0:T(8,128)(2,1)S(1)}, u32[]{:S(2)}, u32[]{:S(2)}) async-start(bf16[32,8,1024]{2,1,0:T(8,128)(2,1)} %get-tuple-element.65), calls=%async_computation.2 | async-start | bytes 1048576 | tf_op jit(solution)/shard_map/all_to_all | solution.py:1016
  62.1 1.7 %collective-permute-start.1 = (bf16[32,8,640]{2,1,0:T(8,128)(2,1)S(1)}, bf16[32,8,640]{2,1,0:T(8,128)(2,1)S(1)}, u32[]{:S(2)}, u32[]{:S(2)}) collective-permute-start(bf16[32,8,640]{2,1,0:T(8,128)(2,1)S(1)} %slice.6), channel_id=1, source_target_pairs={{0,1},{1,0},{2,3},{3,2},{4,5},{5,4},{6,7},{7,6},{8,9},{9,8},{10,11... | collective-permute-start | bytes 983048 | tf_op jit(solution)/shard_map/ppermute | solution.py:1027

commit v4 on v3

--- a/solution.py
+++ b/solution.py
@@ -321,15 +321,16 @@
 
 def front_body(plan):
     def body(scalars, ins, outs, scratch):
-        payload = []
-        for pooled, mixed, unused in attended_towers(ins):
-            payload += [pooled.astype(BF16), mixed]
-        payload = jnp.concatenate(payload, 1)
+        payload = [
+            jnp.concatenate([pooled.astype(BF16), mixed], 1)
+            for pooled, mixed, unused in attended_towers(ins)
+        ]
         rows = outs[K.ROWS].ref
 
-        @pl.loop(0, rows.shape[0])
+        @pl.loop(0, rows.shape[0] // 2)
         def _(chip):
-            rows[chip] = payload
+            for core in range(2):
+                rows[2 * chip + core] = payload[core]
 
     return body
 
@@ -555,9 +556,14 @@
 
 def row_copies(scalars, ins, scratch):
     core = scalars[0][0] % 2
+    wide = scratch[0].shape[1] // 2
     return [
-        pltpu.make_async_copy(ins[name].ref, scratch[0].at[:, at], scratch[1].at[i])
-        for i, (name, at) in enumerate(((K.MINE, core), (K.OTHERS, 1 - core)))
+        pltpu.make_async_copy(
+            ins[name].ref,
+            scratch[0].at[:, pl.ds(pl.multiple_of(tower * wide, LANES), wide)],
+            scratch[1].at[i],
+        )
+        for i, (name, tower) in enumerate(((K.MINE, core), (K.OTHERS, 1 - core)))
     ]
 
 
@@ -572,12 +578,12 @@
         rows_ref, sems = scratch
         dim = plan.dim
         device = at_ref[0]
-        caps, wide = rows_ref.shape[2:]
+        caps = rows_ref.shape[0] // plan.devices
         held, others = clear_windows(plan, outs[K.SEND].ref)
         outs[K.SEND].push_part(others)
         for copy in row_copies(scalars, ins, scratch):
             copy.wait()
-        rows = rows_ref[...].reshape(plan.devices * caps, wide)
+        rows = rows_ref[...]
         outs[K.ROWS].ref[...] = rows
         outs[K.ROWS].push()
         units = forward_pair(plan, rows, ins, (None, None), (None, None), (None, None))
@@ -1016,13 +1022,6 @@
     return lax.all_to_all(array, "dp", split_axis=0, concat_axis=0, tiled=True)
 
 
-def exchange_by_core(array, devices):
-    groups = [list(range(core, devices, 2)) for core in range(2)]
-    return lax.all_to_all(
-        array, "dp", split_axis=0, concat_axis=0, tiled=True, axis_index_groups=groups
-    )
-
-
 def swap(array, devices):
     return lax.ppermute(array, "dp", [(i, i ^ 1) for i in range(devices)])
 
@@ -1043,7 +1042,6 @@
     device = lax.axis_index("dp").astype(jnp.int32).reshape(1)
     text_input, image_input = text_input.swapaxes(0, 1), image_input.swapaxes(0, 1)
     totals = caps * seq, caps * img_seq
-    chips = devices // 2
     width = (heads - 1) * LANES
 
     first = {
@@ -1072,12 +1070,12 @@
     rows = run(
         front_body(plan),
         "front",
-        {K.ROWS: ((chips, caps, 4 * dim), BF16, Place.NEAR)},
+        {K.ROWS: ((devices, caps, 2 * dim), BF16, Place.NEAR)},
         [],
         [],
         [eot | far(first), far(late)],
     )[K.ROWS]
-    mine = exchange_by_core(rows, devices)
+    mine = exchange(rows).reshape(count, 2 * dim)
 
     unused, pack_rows = pack_at(dim, hidden, caps)
     side_outs = {K.VALUES: ((devices, caps, width), BF16, Place.FAR)}
@@ -1106,7 +1104,7 @@
         middle_body(plan),
         "middle",
         middle_outs,
-        [pltpu.VMEM((chips, 2, caps, 4 * dim), BF16), pltpu.SemaphoreType.DMA((2,))],
+        [pltpu.VMEM((count, 4 * dim), BF16), pltpu.SemaphoreType.DMA((2,))],
         [device, logit_scale],
         [
             {K.MINE: (mine, Place.AUTO), K.OTHERS: (others, Place.AUTO)}

time: 66.3 us -> 66 us (level)
  starting transfers between devices: 17.3 us -> 16.3 us
    all_to_all x1 -> x0, starting transfers between devices: 8.33 us -> none  [exchange_by_core(): lax.all_to_all(array, 'dp', split_axis=0, concat_axis=0, tiled=True, axis...]
    all_to_all x2 -> x3, starting transfers between devices: 8.61 us -> 16 us  [exchange(): return lax.all_to_all(array, 'dp', split_axis=0, concat_axis=0, tiled=True)]
    all_to_all x2 -> x3, waiting for transfers between devices: 0.69 us -> 6.83 us  [exchange(): return lax.all_to_all(array, 'dp', split_axis=0, concat_axis=0, tiled=True)]
    all_to_all x1 -> x0, waiting for transfers between devices: 5.6 us -> none  [exchange_by_core(): lax.all_to_all(array, 'dp', split_axis=0, concat_axis=0, tiled=True, axis...]
where the time goes in v4:
time: 66 us; the launch traced here: 65.5 us
  Pallas kernels  38.3 us (58%)
  starting transfers between devices  16.3 us (25%)
  waiting for transfers between devices  9.26 us (14%)
  between operations  1.55 us (2%)
    pallas_call x5, Pallas kernels, run(): pl.pallas_call(kernel, name=name, out_shape=[{Place.FAR: pltpu.HBM, Place...  38.3 us
    all_to_all x3, starting transfers between devices, exchange(): return lax.all_to_all(array, 'dp', split_axis=0, concat_axis=0, tiled=True)  16 us
    all_to_all x3, waiting for transfers between devices, exchange(): return lax.all_to_all(array, 'dp', split_axis=0, concat_axis=0, tiled=True)  6.83 us
    ppermute x2, waiting for transfers between devices, swap(): return lax.ppermute(array, 'dp', [(i, i ^ 1) for i in range(devices)])  2.44 us
  transfers between devices with their start and end apart: 5, of which 4 were waited for; matrix products, arithmetic and copies ran while one was open for 0% of the time, Pallas kernels for 49%

profile of v4, /device:TPU:0, one launch (start us, length us, event | category | flops | bytes accessed | tf_op | source)
XLA Modules:
  0.0 65.5 jit_solution(18409898706317964783)
XLA Ops:
  0.6 3.9 %front.1 = bf16[32,8,768]{2,1,0:T(8,128)(2,1)} custom-call(s32[8]{0:T(128)} %refs_2_.1, bf16[77,8,384]{2,1,0:T(8,128)(2,1)} %bitcast.15, bf16[50,8,384]{2,1,0:T(8,128)(2,1)} %bitcast.18, f32[1,384]{1,0:T(1,128)} %refs_5_.7, f32[1,384]{1,0:T(1,128)} %refs_6_.7, f32[1,384]{1,0:T(1,128)} %refs_7_.7, f32[1,384]{1,0:T(1,128)} %refs_8_.7, ...), custom_call_target="tpu_custom_call" | custom-call | tf_op jit(solution)/shard_map/front/pallas_call | solution.py:1006
  4.5 7.3 %all-to-all-start = ((bf16[32,8,768]{2,1,0:T(8,128)(2,1)}), bf16[32,8,768]{2,1,0:T(8,128)(2,1)S(1)}, u32[]{:S(2)}, u32[]{:S(2)}) async-start(bf16[32,8,768]{2,1,0:T(8,128)(2,1)} %front.1), calls=%async_computation | async-start | bytes 786432 | tf_op jit(solution)/shard_map/all_to_all | solution.py:1022
  11.8 0.0 copy-start
  11.9 0.0 copy-start.1
  11.9 7.0 %side.1 = (bf16[32,8,640]{2,1,0:T(8,128)(2,1)}, bf16[616,384]{1,0:T(8,128)(2,1)}, bf16[616,384]{1,0:T(8,128)(2,1)}, f32[48,616]{1,0:T(8,128)}, f32[192,384]{1,0:...) custom-call(s32[8]{0:T(128)} %refs_2_.1, ...), custom_call_target="tpu_custom_call" | custom-call | tf_op jit(solution)/shard_map/side/pallas_call | solution.py:1006
  18.9 6.1 %all-to-all-done = bf16[32,8,768]{2,1,0:T(8,128)(2,1)S(1)} async-done(((bf16[32,8,768]{2,1,0:T(8,128)(2,1)}), bf16[32,8,768]{2,1,0:T(8,128)(2,1)S(1)}, u32[]{:S(2)}, u32[]{:S(2)}) %all-to-all-start) | async-done | bytes 393248 | tf_op jit(solution)/shard_map/all_to_all | solution.py:1022
  25.0 2.6 %all-to-all-start.1 = ((bf16[32,8,640]{2,1,0:T(8,128)(2,1)}), bf16[32,8,640]{2,1,0:T(8,128)(2,1)S(1)}, u32[]{:S(2)}, u32[]{:S(2)}) async-start(bf16[32,8,640]{2,1,0:T(8,128)(2,1)} %get-tuple-element.58), calls=%async_computation.1 | async-start | bytes 655360 | tf_op jit(solution)/shard_map/all_to_all | solution.py:1022
  27.7 0.3 collective-permute-start
  28.6 0.8 %collective-permute-done.refs_3_ = bf16[256,768]{1,0:T(8,128)(2,1)S(1)} collective-permute-done((bf16[256,768]{1,0:T(8,128)(2,1)S(1)}, bf16[256,768]{1,0:T(8,128)(2,1)S(1)}, u32[]{:S(2)}, u32[]{:S(2)}) %collective-permute-start) | collective-permute-done | bytes 393248 | tf_op jit(solution)/shard_map/ppermute | solution.py:1026
  29.5 0.0 copy-done
  29.5 0.0 copy-done.1
  29.5 10.7 %middle.1 = (bf16[32,8,1024]{2,1,0:T(8,128)(2,1)}, bf16[256,1536]{1,0:T(8,128)(2,1)}, f32[64,384]{1,0:T(8,128)}, bf16[48,616]{1,0:T(8,128)(2,1)}, f32[64,384]{1,0:T(8,128)}, /*index=5*/bf16[48,400]{1,0:T(8,128)(2,1)}) custom-call(s32[1]{0:T(128)} %bitcast.refs_0_, f32[1]{0:T(128)S(6)} %copy.33.refs_1_, bf16[256,768]{1,0:T(8,128)(2,1)S(1)} %bitcast.13, ...), custom_call_target="tpu_custom_call" | custom-call | tf_op jit(solution)/shard_map/middle/pallas_call | solution.py:1006
  40.2 0.0 all-to-all-done.1
  40.2 0.0 copy-start.2
  40.2 6.0 %all-to-all-start.2 = ((bf16[32,8,1024]{2,1,0:T(8,128)(2,1)}), bf16[32,8,1024]{2,1,0:T(8,128)(2,1)S(1)}, u32[]{:S(2)}, u32[]{:S(2)}) async-start(bf16[32,8,1024]{2,1,0:T(8,128)(2,1)} %get-tuple-element.65), calls=%async_computation.2 | async-start | bytes 1048576 | tf_op jit(solution)/shard_map/all_to_all | solution.py:1022
  46.3 0.0 copy-done.2
  46.3 14.7 %tail.1 = (f32[1]{0:T(128)}, f32[1]{0:T(128)}, f32[440,128]{1,0:T(8,128)S(1)}, f32[77,8,384]{2,1,0:T(8,128)}, f32[440,128]{1,0:T(8,128)S(1)}, /*index=5*/f32[50,...) custom-call(s32[1]{0:T(128)} %bitcast.refs_0_, ...), custom_call_target="tpu_custom_call" | custom-call | tf_op jit(solution)/shard_map/tail/pallas_call | solution.py:1006
  60.9 0.7 %all-to-all-done.2 = bf16[32,8,1024]{2,1,0:T(8,128)(2,1)S(1)} async-done(((bf16[32,8,1024]{2,1,0:T(8,128)(2,1)}), bf16[32,8,1024]{2,1,0:T(8,128)(2,1)S(1)}, u32[]{:S(2)}, u32[]{:S(2)}) %all-to-all-start.2) | async-done | bytes 524320 | tf_op jit(solution)/shard_map/all_to_all | solution.py:1022
  61.7 0.1 collective-permute-start.1
  61.7 1.6 %collective-permute-done.1 = bf16[32,8,640]{2,1,0:T(8,128)(2,1)S(1)} collective-permute-done((bf16[32,8,640]{2,1,0:T(8,128)(2,1)S(1)}, bf16[32,8,640]{2,1,0:T(8,128)(2,1)S(1)}, u32[]{:S(2)}, u32[]{:S(2)}) %collective-permute-start.1) | collective-permute-done | bytes 327712 | tf_op jit(solution)/shard_map/ppermute | solution.py:1026
  63.4 2.0 %last.1 = (f32[1,55344]{1,0:T(1,128)}, f32[1,55344]{1,0:T(1,128)}) custom-call(s32[1]{0:T(128)} %bitcast.refs_0_, f32[440,128]{1,0:T(8,128)S(1)} %get-tuple-element.63.refs_1_, f32[440,128]{1,0:T(8,128)S(1)} %get-tuple-element.64.refs_2_, bf16[256,128]{1,0:T(8,128)(2,1)S(1)} %get-tuple-element.67.refs_3_, bf16[256,768]{1,0:T(8,128)(2,1)S(1)} %get-tuple-element.68.refs_4_, ...), custom_call_target="tpu_custom_call" | custom-call | tf_op jit(solution)/shard_map/last/pallas_call | solution.py:1006
  (1 shorter events, 0.0 us)
Async XLA Ops:
  4.5 20.5 %all-to-all-start = ((bf16[32,8,768]{2,1,0:T(8,128)(2,1)}), bf16[32,8,768]{2,1,0:T(8,128)(2,1)S(1)}, u32[]{:S(2)}, u32[]{:S(2)}) async-start(bf16[32,8,768]{2,1,0:T(8,128)(2,1)} %front.1), calls=%async_computation | async-start | bytes 786432 | tf_op jit(solution)/shard_map/all_to_all | solution.py:1022
  11.8 17.6 %copy-start = (bf16[1,384,1536]{2,1,0:T(8,128)(2,1)S(1)}, bf16[1,384,1536]{2,1,0:T(8,128)(2,1)}, u32[]{:S(2)}) copy-start(bf16[1,384,1536]{2,1,0:T(8,128)(2,1)} %refs_24_.3) | copy-start | bytes 3538948
  11.9 17.6 %copy-start.1 = (bf16[1,384,1536]{2,1,0:T(8,128)(2,1)S(1)}, bf16[1,384,1536]{2,1,0:T(8,128)(2,1)}, u32[]{:S(2)}) copy-start(bf16[1,384,1536]{2,1,0:T(8,128)(2,1)} %refs_25_.1) | copy-start | bytes 3538948
  25.0 15.2 %all-to-all-start.1 = ((bf16[32,8,640]{2,1,0:T(8,128)(2,1)}), bf16[32,8,640]{2,1,0:T(8,128)(2,1)S(1)}, u32[]{:S(2)}, u32[]{:S(2)}) async-start(bf16[32,8,640]{2,1,0:T(8,128)(2,1)} %get-tuple-element.58), calls=%async_computation.1 | async-start | bytes 655360 | tf_op jit(solution)/shard_map/all_to_all | solution.py:1022
  27.7 1.8 %collective-permute-start = (bf16[256,768]{1,0:T(8,128)(2,1)S(1)}, bf16[256,768]{1,0:T(8,128)(2,1)S(1)}, u32[]{:S(2)}, u32[]{:S(2)}) collective-permute-start(bf16[256,768]{1,0:T(8,128)(2,1)S(1)} %bitcast.12), channel_id=1, source_target_pairs={{0,1},{1,0},{2,3},{3,2},{4,5},{5,4},{6,7},{7,6},{8,9},{9,8},{10,11... | collective-permute-start | bytes 1179656 | tf_op jit(solution)/shard_map/ppermute | solution.py:1026
  40.2 6.0 %copy-start.2 = (bf16[32,8,640]{2,1,0:T(8,128)(2,1)}, bf16[32,8,640]{2,1,0:T(8,128)(2,1)S(1)}, u32[]{:S(2)}) copy-start(bf16[32,8,640]{2,1,0:T(8,128)(2,1)S(1)} %all-to-all-done.1) | copy-start | bytes 983044
  40.2 21.4 %all-to-all-start.2 = ((bf16[32,8,1024]{2,1,0:T(8,128)(2,1)}), bf16[32,8,1024]{2,1,0:T(8,128)(2,1)S(1)}, u32[]{:S(2)}, u32[]{:S(2)}) async-start(bf16[32,8,1024]{2,1,0:T(8,128)(2,1)} %get-tuple-element.65), calls=%async_computation.2 | async-start | bytes 1048576 | tf_op jit(solution)/shard_map/all_to_all | solution.py:1022
  61.7 1.7 %collective-permute-start.1 = (bf16[32,8,640]{2,1,0:T(8,128)(2,1)S(1)}, bf16[32,8,640]{2,1,0:T(8,128)(2,1)S(1)}, u32[]{:S(2)}, u32[]{:S(2)}) collective-permute-start(bf16[32,8,640]{2,1,0:T(8,128)(2,1)S(1)} %slice.6), channel_id=1, source_target_pairs={{0,1},{1,0},{2,3},{3,2},{4,5},{5,4},{6,7},{7,6},{8,9},{9,8},{10,11... | collective-permute-start | bytes 983048 | tf_op jit(solution)/shard_map/ppermute | solution.py:1026

commit v5 on v4

--- a/solution.py
+++ b/solution.py
@@ -852,14 +852,12 @@
                     for tower, values in enumerate(received if core == 0 else received[::-1]):
                         grad_query[:, tower * dim : (tower + 1) * dim] = values[:, -dim:]
 
-            @pl.when(device == 0)
-            def _():
-                for tower, values in enumerate((sent_ref[:, first * LANES :], swapped[...])):
-                    sums = values[:, :-dim].astype(F32).reshape(plan.devices, caps, -1)
-                    put_tile(flat.at[tower], 0, spare_row(plan, jnp.sum(sums, 0), first, dim))
-                    grads = grad_query[:, tower * dim : (tower + 1) * dim]
-                    row = summed_through(grads, w_query[tower])
-                    put_tile(flat.at[tower], tiles, row + bias[tower : tower + 1, :])
+            for tower, values in enumerate((sent_ref[:, first * LANES :], swapped[...])):
+                sums = values[:, :-dim].astype(F32).reshape(plan.devices, caps, -1)
+                put_tile(flat.at[tower], 0, spare_row(plan, jnp.sum(sums, 0), first, dim))
+                grads = grad_query[:, tower * dim : (tower + 1) * dim]
+                row = summed_through(grads, w_query[tower])
+                put_tile(flat.at[tower], tiles, row + bias[tower : tower + 1, :])
 
             query_part = dot_tn(windows[...], grad_query[...])
             end = last_head(plan, sent_ref, heads)

time: 66 us -> 65.7 us (level)
  transfers between devices with their start and end apart: 5 -> 5, of which waited for: 4 -> 4; matrix products, arithmetic and copies ran while one was open for 0% -> 0% of each run, Pallas kernels for 49% -> 50%
where the time goes in v5:
time: 65.7 us; the launch traced here: 65.3 us
  Pallas kernels  38 us (58%)
  starting transfers between devices  16.3 us (25%)
  waiting for transfers between devices  9.26 us (14%)
  between operations  1.55 us (2%)
    pallas_call x5, Pallas kernels, run(): pl.pallas_call(kernel, name=name, out_shape=[{Place.FAR: pltpu.HBM, Place...  38 us
    all_to_all x3, starting transfers between devices, exchange(): return lax.all_to_all(array, 'dp', split_axis=0, concat_axis=0, tiled=True)  16 us
    all_to_all x3, waiting for transfers between devices, exchange(): return lax.all_to_all(array, 'dp', split_axis=0, concat_axis=0, tiled=True)  6.83 us
    ppermute x2, waiting for transfers between devices, swap(): return lax.ppermute(array, 'dp', [(i, i ^ 1) for i in range(devices)])  2.44 us
  transfers between devices with their start and end apart: 5, of which 4 were waited for; matrix products, arithmetic and copies ran while one was open for 0% of the time, Pallas kernels for 50%

profile of v5, /device:TPU:0, one launch (start us, length us, event | category | flops | bytes accessed | tf_op | source)
XLA Modules:
  0.0 65.3 jit_solution(2372852189066813301)
XLA Ops:
  0.6 3.9 %front.1 = bf16[32,8,768]{2,1,0:T(8,128)(2,1)} custom-call(s32[8]{0:T(128)} %refs_2_.1, bf16[77,8,384]{2,1,0:T(8,128)(2,1)} %bitcast.15, bf16[50,8,384]{2,1,0:T(8,128)(2,1)} %bitcast.18, f32[1,384]{1,0:T(1,128)} %refs_5_.7, f32[1,384]{1,0:T(1,128)} %refs_6_.7, f32[1,384]{1,0:T(1,128)} %refs_7_.7, f32[1,384]{1,0:T(1,128)} %refs_8_.7, ...), custom_call_target="tpu_custom_call" | custom-call | tf_op jit(solution)/shard_map/front/pallas_call | solution.py:1004
  4.5 7.3 %all-to-all-start = ((bf16[32,8,768]{2,1,0:T(8,128)(2,1)}), bf16[32,8,768]{2,1,0:T(8,128)(2,1)S(1)}, u32[]{:S(2)}, u32[]{:S(2)}) async-start(bf16[32,8,768]{2,1,0:T(8,128)(2,1)} %front.1), calls=%async_computation | async-start | bytes 786432 | tf_op jit(solution)/shard_map/all_to_all | solution.py:1020
  11.8 0.0 copy-start
  11.9 0.0 copy-start.1
  11.9 7.0 %side.1 = (bf16[32,8,640]{2,1,0:T(8,128)(2,1)}, bf16[616,384]{1,0:T(8,128)(2,1)}, bf16[616,384]{1,0:T(8,128)(2,1)}, f32[48,616]{1,0:T(8,128)}, f32[192,384]{1,0:...) custom-call(s32[8]{0:T(128)} %refs_2_.1, ...), custom_call_target="tpu_custom_call" | custom-call | tf_op jit(solution)/shard_map/side/pallas_call | solution.py:1004
  18.9 6.1 %all-to-all-done = bf16[32,8,768]{2,1,0:T(8,128)(2,1)S(1)} async-done(((bf16[32,8,768]{2,1,0:T(8,128)(2,1)}), bf16[32,8,768]{2,1,0:T(8,128)(2,1)S(1)}, u32[]{:S(2)}, u32[]{:S(2)}) %all-to-all-start) | async-done | bytes 393248 | tf_op jit(solution)/shard_map/all_to_all | solution.py:1020
  25.0 2.6 %all-to-all-start.1 = ((bf16[32,8,640]{2,1,0:T(8,128)(2,1)}), bf16[32,8,640]{2,1,0:T(8,128)(2,1)S(1)}, u32[]{:S(2)}, u32[]{:S(2)}) async-start(bf16[32,8,640]{2,1,0:T(8,128)(2,1)} %get-tuple-element.58), calls=%async_computation.1 | async-start | bytes 655360 | tf_op jit(solution)/shard_map/all_to_all | solution.py:1020
  27.7 0.3 collective-permute-start
  28.6 0.8 %collective-permute-done.refs_3_ = bf16[256,768]{1,0:T(8,128)(2,1)S(1)} collective-permute-done((bf16[256,768]{1,0:T(8,128)(2,1)S(1)}, bf16[256,768]{1,0:T(8,128)(2,1)S(1)}, u32[]{:S(2)}, u32[]{:S(2)}) %collective-permute-start) | collective-permute-done | bytes 393248 | tf_op jit(solution)/shard_map/ppermute | solution.py:1024
  29.5 0.0 copy-done
  29.5 0.0 copy-done.1
  29.5 10.7 %middle.1 = (bf16[32,8,1024]{2,1,0:T(8,128)(2,1)}, bf16[256,1536]{1,0:T(8,128)(2,1)}, f32[64,384]{1,0:T(8,128)}, bf16[48,616]{1,0:T(8,128)(2,1)}, f32[64,384]{1,0:T(8,128)}, /*index=5*/bf16[48,400]{1,0:T(8,128)(2,1)}) custom-call(s32[1]{0:T(128)} %bitcast.refs_0_, f32[1]{0:T(128)S(6)} %copy.33.refs_1_, bf16[256,768]{1,0:T(8,128)(2,1)S(1)} %bitcast.13, ...), custom_call_target="tpu_custom_call" | custom-call | tf_op jit(solution)/shard_map/middle/pallas_call | solution.py:1004
  40.2 0.0 all-to-all-done.1
  40.2 0.0 copy-start.2
  40.2 6.0 %all-to-all-start.2 = ((bf16[32,8,1024]{2,1,0:T(8,128)(2,1)}), bf16[32,8,1024]{2,1,0:T(8,128)(2,1)S(1)}, u32[]{:S(2)}, u32[]{:S(2)}) async-start(bf16[32,8,1024]{2,1,0:T(8,128)(2,1)} %get-tuple-element.65), calls=%async_computation.2 | async-start | bytes 1048576 | tf_op jit(solution)/shard_map/all_to_all | solution.py:1020
  46.3 0.0 copy-done.2
  46.3 14.7 %tail.1 = (f32[1]{0:T(128)}, f32[1]{0:T(128)}, f32[440,128]{1,0:T(8,128)S(1)}, f32[77,8,384]{2,1,0:T(8,128)}, f32[440,128]{1,0:T(8,128)S(1)}, /*index=5*/f32[50,...) custom-call(s32[1]{0:T(128)} %bitcast.refs_0_, ...), custom_call_target="tpu_custom_call" | custom-call | tf_op jit(solution)/shard_map/tail/pallas_call | solution.py:1004
  60.9 0.7 %all-to-all-done.2 = bf16[32,8,1024]{2,1,0:T(8,128)(2,1)S(1)} async-done(((bf16[32,8,1024]{2,1,0:T(8,128)(2,1)}), bf16[32,8,1024]{2,1,0:T(8,128)(2,1)S(1)}, u32[]{:S(2)}, u32[]{:S(2)}) %all-to-all-start.2) | async-done | bytes 524320 | tf_op jit(solution)/shard_map/all_to_all | solution.py:1020
  61.7 0.1 collective-permute-start.1
  61.7 1.6 %collective-permute-done.1 = bf16[32,8,640]{2,1,0:T(8,128)(2,1)S(1)} collective-permute-done((bf16[32,8,640]{2,1,0:T(8,128)(2,1)S(1)}, bf16[32,8,640]{2,1,0:T(8,128)(2,1)S(1)}, u32[]{:S(2)}, u32[]{:S(2)}) %collective-permute-start.1) | collective-permute-done | bytes 327712 | tf_op jit(solution)/shard_map/ppermute | solution.py:1024
  63.4 1.7 %last.1 = (f32[1,55344]{1,0:T(1,128)}, f32[1,55344]{1,0:T(1,128)}) custom-call(s32[1]{0:T(128)} %bitcast.refs_0_, f32[440,128]{1,0:T(8,128)S(1)} %get-tuple-element.63.refs_1_, f32[440,128]{1,0:T(8,128)S(1)} %get-tuple-element.64.refs_2_, bf16[256,128]{1,0:T(8,128)(2,1)S(1)} %get-tuple-element.67.refs_3_, bf16[256,768]{1,0:T(8,128)(2,1)S(1)} %get-tuple-element.68.refs_4_, ...), custom_call_target="tpu_custom_call" | custom-call | tf_op jit(solution)/shard_map/last/pallas_call | solution.py:1004
  (1 shorter events, 0.0 us)
Async XLA Ops:
  4.5 20.5 %all-to-all-start = ((bf16[32,8,768]{2,1,0:T(8,128)(2,1)}), bf16[32,8,768]{2,1,0:T(8,128)(2,1)S(1)}, u32[]{:S(2)}, u32[]{:S(2)}) async-start(bf16[32,8,768]{2,1,0:T(8,128)(2,1)} %front.1), calls=%async_computation | async-start | bytes 786432 | tf_op jit(solution)/shard_map/all_to_all | solution.py:1020
  11.8 17.6 %copy-start = (bf16[1,384,1536]{2,1,0:T(8,128)(2,1)S(1)}, bf16[1,384,1536]{2,1,0:T(8,128)(2,1)}, u32[]{:S(2)}) copy-start(bf16[1,384,1536]{2,1,0:T(8,128)(2,1)} %refs_24_.3) | copy-start | bytes 3538948
  11.9 17.6 %copy-start.1 = (bf16[1,384,1536]{2,1,0:T(8,128)(2,1)S(1)}, bf16[1,384,1536]{2,1,0:T(8,128)(2,1)}, u32[]{:S(2)}) copy-start(bf16[1,384,1536]{2,1,0:T(8,128)(2,1)} %refs_25_.1) | copy-start | bytes 3538948
  25.0 15.2 %all-to-all-start.1 = ((bf16[32,8,640]{2,1,0:T(8,128)(2,1)}), bf16[32,8,640]{2,1,0:T(8,128)(2,1)S(1)}, u32[]{:S(2)}, u32[]{:S(2)}) async-start(bf16[32,8,640]{2,1,0:T(8,128)(2,1)} %get-tuple-element.58), calls=%async_computation.1 | async-start | bytes 655360 | tf_op jit(solution)/shard_map/all_to_all | solution.py:1020
  27.7 1.8 %collective-permute-start = (bf16[256,768]{1,0:T(8,128)(2,1)S(1)}, bf16[256,768]{1,0:T(8,128)(2,1)S(1)}, u32[]{:S(2)}, u32[]{:S(2)}) collective-permute-start(bf16[256,768]{1,0:T(8,128)(2,1)S(1)} %bitcast.12), channel_id=1, source_target_pairs={{0,1},{1,0},{2,3},{3,2},{4,5},{5,4},{6,7},{7,6},{8,9},{9,8},{10,11... | collective-permute-start | bytes 1179656 | tf_op jit(solution)/shard_map/ppermute | solution.py:1024
  40.2 6.0 %copy-start.2 = (bf16[32,8,640]{2,1,0:T(8,128)(2,1)}, bf16[32,8,640]{2,1,0:T(8,128)(2,1)S(1)}, u32[]{:S(2)}) copy-start(bf16[32,8,640]{2,1,0:T(8,128)(2,1)S(1)} %all-to-all-done.1) | copy-start | bytes 983044
  40.2 21.4 %all-to-all-start.2 = ((bf16[32,8,1024]{2,1,0:T(8,128)(2,1)}), bf16[32,8,1024]{2,1,0:T(8,128)(2,1)S(1)}, u32[]{:S(2)}, u32[]{:S(2)}) async-start(bf16[32,8,1024]{2,1,0:T(8,128)(2,1)} %get-tuple-element.65), calls=%async_computation.2 | async-start | bytes 1048576 | tf_op jit(solution)/shard_map/all_to_all | solution.py:1020
  61.7 1.7 %collective-permute-start.1 = (bf16[32,8,640]{2,1,0:T(8,128)(2,1)S(1)}, bf16[32,8,640]{2,1,0:T(8,128)(2,1)S(1)}, u32[]{:S(2)}, u32[]{:S(2)}) collective-permute-start(bf16[32,8,640]{2,1,0:T(8,128)(2,1)S(1)} %slice.6), channel_id=1, source_target_pairs={{0,1},{1,0},{2,3},{3,2},{4,5},{5,4},{6,7},{7,6},{8,9},{9,8},{10,11... | collective-permute-start | bytes 983048 | tf_op jit(solution)/shard_map/ppermute | solution.py:1024

commit v6 on v5

--- a/solution.py
+++ b/solution.py
@@ -327,10 +327,8 @@
         ]
         rows = outs[K.ROWS].ref
 
-        @pl.loop(0, rows.shape[0] // 2)
-        def _(chip):
-            for core in range(2):
-                rows[2 * chip + core] = payload[core]
+        for device in range(rows.shape[0]):
+            rows[device] = payload[device % 2]
 
     return body
 

time: 65.7 us -> 65.6 us (level)
  no operation moved by 1% of the time
where the time goes in v6:
time: 65.6 us; the launch traced here: 65.2 us
  Pallas kernels  38 us (58%)
  starting transfers between devices  16.3 us (25%)
  waiting for transfers between devices  9.26 us (14%)
  between operations  1.55 us (2%)
    pallas_call x5, Pallas kernels, run(): pl.pallas_call(kernel, name=name, out_shape=[{Place.FAR: pltpu.HBM, Place...  38 us
    all_to_all x3, starting transfers between devices, exchange(): return lax.all_to_all(array, 'dp', split_axis=0, concat_axis=0, tiled=True)  16 us
    all_to_all x3, waiting for transfers between devices, exchange(): return lax.all_to_all(array, 'dp', split_axis=0, concat_axis=0, tiled=True)  6.82 us
    ppermute x2, waiting for transfers between devices, swap(): return lax.ppermute(array, 'dp', [(i, i ^ 1) for i in range(devices)])  2.44 us
  transfers between devices with their start and end apart: 5, of which 4 were waited for; matrix products, arithmetic and copies ran while one was open for 0% of the time, Pallas kernels for 50%

profile of v6, /device:TPU:0, one launch (start us, length us, event | category | flops | bytes accessed | tf_op | source)
XLA Modules:
  0.0 65.2 jit_solution(5747273660594861078)
XLA Ops:
  0.6 3.8 %front.1 = bf16[32,8,768]{2,1,0:T(8,128)(2,1)} custom-call(s32[8]{0:T(128)} %refs_2_.1, bf16[77,8,384]{2,1,0:T(8,128)(2,1)} %bitcast.15, bf16[50,8,384]{2,1,0:T(8,128)(2,1)} %bitcast.18, f32[1,384]{1,0:T(1,128)} %refs_5_.7, f32[1,384]{1,0:T(1,128)} %refs_6_.7, f32[1,384]{1,0:T(1,128)} %refs_7_.7, f32[1,384]{1,0:T(1,128)} %refs_8_.7, ...), custom_call_target="tpu_custom_call" | custom-call | tf_op jit(solution)/shard_map/front/pallas_call | solution.py:1002
  4.5 7.3 %all-to-all-start = ((bf16[32,8,768]{2,1,0:T(8,128)(2,1)}), bf16[32,8,768]{2,1,0:T(8,128)(2,1)S(1)}, u32[]{:S(2)}, u32[]{:S(2)}) async-start(bf16[32,8,768]{2,1,0:T(8,128)(2,1)} %front.1), calls=%async_computation | async-start | bytes 786432 | tf_op jit(solution)/shard_map/all_to_all | solution.py:1018
  11.8 0.0 copy-start
  11.8 0.0 copy-start.1
  11.8 7.0 %side.1 = (bf16[32,8,640]{2,1,0:T(8,128)(2,1)}, bf16[616,384]{1,0:T(8,128)(2,1)}, bf16[616,384]{1,0:T(8,128)(2,1)}, f32[48,616]{1,0:T(8,128)}, f32[192,384]{1,0:...) custom-call(s32[8]{0:T(128)} %refs_2_.1, ...), custom_call_target="tpu_custom_call" | custom-call | tf_op jit(solution)/shard_map/side/pallas_call | solution.py:1002
  18.8 6.1 %all-to-all-done = bf16[32,8,768]{2,1,0:T(8,128)(2,1)S(1)} async-done(((bf16[32,8,768]{2,1,0:T(8,128)(2,1)}), bf16[32,8,768]{2,1,0:T(8,128)(2,1)S(1)}, u32[]{:S(2)}, u32[]{:S(2)}) %all-to-all-start) | async-done | bytes 393248 | tf_op jit(solution)/shard_map/all_to_all | solution.py:1018
  24.9 2.6 %all-to-all-start.1 = ((bf16[32,8,640]{2,1,0:T(8,128)(2,1)}), bf16[32,8,640]{2,1,0:T(8,128)(2,1)S(1)}, u32[]{:S(2)}, u32[]{:S(2)}) async-start(bf16[32,8,640]{2,1,0:T(8,128)(2,1)} %get-tuple-element.58), calls=%async_computation.1 | async-start | bytes 655360 | tf_op jit(solution)/shard_map/all_to_all | solution.py:1018
  27.6 0.3 collective-permute-start
  28.6 0.8 %collective-permute-done.refs_3_ = bf16[256,768]{1,0:T(8,128)(2,1)S(1)} collective-permute-done((bf16[256,768]{1,0:T(8,128)(2,1)S(1)}, bf16[256,768]{1,0:T(8,128)(2,1)S(1)}, u32[]{:S(2)}, u32[]{:S(2)}) %collective-permute-start) | collective-permute-done | bytes 393248 | tf_op jit(solution)/shard_map/ppermute | solution.py:1022
  29.4 0.0 copy-done
  29.4 0.0 copy-done.1
  29.4 10.7 %middle.1 = (bf16[32,8,1024]{2,1,0:T(8,128)(2,1)}, bf16[256,1536]{1,0:T(8,128)(2,1)}, f32[64,384]{1,0:T(8,128)}, bf16[48,616]{1,0:T(8,128)(2,1)}, f32[64,384]{1,0:T(8,128)}, /*index=5*/bf16[48,400]{1,0:T(8,128)(2,1)}) custom-call(s32[1]{0:T(128)} %bitcast.refs_0_, f32[1]{0:T(128)S(6)} %copy.33.refs_1_, bf16[256,768]{1,0:T(8,128)(2,1)S(1)} %bitcast.13, ...), custom_call_target="tpu_custom_call" | custom-call | tf_op jit(solution)/shard_map/middle/pallas_call | solution.py:1002
  40.1 0.0 all-to-all-done.1
  40.1 0.0 copy-start.2
  40.2 6.0 %all-to-all-start.2 = ((bf16[32,8,1024]{2,1,0:T(8,128)(2,1)}), bf16[32,8,1024]{2,1,0:T(8,128)(2,1)S(1)}, u32[]{:S(2)}, u32[]{:S(2)}) async-start(bf16[32,8,1024]{2,1,0:T(8,128)(2,1)} %get-tuple-element.65), calls=%async_computation.2 | async-start | bytes 1048576 | tf_op jit(solution)/shard_map/all_to_all | solution.py:1018
  46.2 0.0 copy-done.2
  46.2 14.7 %tail.1 = (f32[1]{0:T(128)}, f32[1]{0:T(128)}, f32[440,128]{1,0:T(8,128)S(1)}, f32[77,8,384]{2,1,0:T(8,128)}, f32[440,128]{1,0:T(8,128)S(1)}, /*index=5*/f32[50,...) custom-call(s32[1]{0:T(128)} %bitcast.refs_0_, ...), custom_call_target="tpu_custom_call" | custom-call | tf_op jit(solution)/shard_map/tail/pallas_call | solution.py:1002
  60.9 0.7 %all-to-all-done.2 = bf16[32,8,1024]{2,1,0:T(8,128)(2,1)S(1)} async-done(((bf16[32,8,1024]{2,1,0:T(8,128)(2,1)}), bf16[32,8,1024]{2,1,0:T(8,128)(2,1)S(1)}, u32[]{:S(2)}, u32[]{:S(2)}) %all-to-all-start.2) | async-done | bytes 524320 | tf_op jit(solution)/shard_map/all_to_all | solution.py:1018
  61.6 0.1 collective-permute-start.1
  61.7 1.6 %collective-permute-done.1 = bf16[32,8,640]{2,1,0:T(8,128)(2,1)S(1)} collective-permute-done((bf16[32,8,640]{2,1,0:T(8,128)(2,1)S(1)}, bf16[32,8,640]{2,1,0:T(8,128)(2,1)S(1)}, u32[]{:S(2)}, u32[]{:S(2)}) %collective-permute-start.1) | collective-permute-done | bytes 327712 | tf_op jit(solution)/shard_map/ppermute | solution.py:1022
  63.3 1.7 %last.1 = (f32[1,55344]{1,0:T(1,128)}, f32[1,55344]{1,0:T(1,128)}) custom-call(s32[1]{0:T(128)} %bitcast.refs_0_, f32[440,128]{1,0:T(8,128)S(1)} %get-tuple-element.63.refs_1_, f32[440,128]{1,0:T(8,128)S(1)} %get-tuple-element.64.refs_2_, bf16[256,128]{1,0:T(8,128)(2,1)S(1)} %get-tuple-element.67.refs_3_, bf16[256,768]{1,0:T(8,128)(2,1)S(1)} %get-tuple-element.68.refs_4_, ...), custom_call_target="tpu_custom_call" | custom-call | tf_op jit(solution)/shard_map/last/pallas_call | solution.py:1002
  (1 shorter events, 0.0 us)
Async XLA Ops:
  4.5 20.5 %all-to-all-start = ((bf16[32,8,768]{2,1,0:T(8,128)(2,1)}), bf16[32,8,768]{2,1,0:T(8,128)(2,1)S(1)}, u32[]{:S(2)}, u32[]{:S(2)}) async-start(bf16[32,8,768]{2,1,0:T(8,128)(2,1)} %front.1), calls=%async_computation | async-start | bytes 786432 | tf_op jit(solution)/shard_map/all_to_all | solution.py:1018
  11.8 17.6 %copy-start = (bf16[1,384,1536]{2,1,0:T(8,128)(2,1)S(1)}, bf16[1,384,1536]{2,1,0:T(8,128)(2,1)}, u32[]{:S(2)}) copy-start(bf16[1,384,1536]{2,1,0:T(8,128)(2,1)} %refs_24_.3) | copy-start | bytes 3538948
  11.8 17.6 %copy-start.1 = (bf16[1,384,1536]{2,1,0:T(8,128)(2,1)S(1)}, bf16[1,384,1536]{2,1,0:T(8,128)(2,1)}, u32[]{:S(2)}) copy-start(bf16[1,384,1536]{2,1,0:T(8,128)(2,1)} %refs_25_.1) | copy-start | bytes 3538948
  24.9 15.2 %all-to-all-start.1 = ((bf16[32,8,640]{2,1,0:T(8,128)(2,1)}), bf16[32,8,640]{2,1,0:T(8,128)(2,1)S(1)}, u32[]{:S(2)}, u32[]{:S(2)}) async-start(bf16[32,8,640]{2,1,0:T(8,128)(2,1)} %get-tuple-element.58), calls=%async_computation.1 | async-start | bytes 655360 | tf_op jit(solution)/shard_map/all_to_all | solution.py:1018
  27.6 1.8 %collective-permute-start = (bf16[256,768]{1,0:T(8,128)(2,1)S(1)}, bf16[256,768]{1,0:T(8,128)(2,1)S(1)}, u32[]{:S(2)}, u32[]{:S(2)}) collective-permute-start(bf16[256,768]{1,0:T(8,128)(2,1)S(1)} %bitcast.12), channel_id=1, source_target_pairs={{0,1},{1,0},{2,3},{3,2},{4,5},{5,4},{6,7},{7,6},{8,9},{9,8},{10,11... | collective-permute-start | bytes 1179656 | tf_op jit(solution)/shard_map/ppermute | solution.py:1022
  40.1 6.0 %copy-start.2 = (bf16[32,8,640]{2,1,0:T(8,128)(2,1)}, bf16[32,8,640]{2,1,0:T(8,128)(2,1)S(1)}, u32[]{:S(2)}) copy-start(bf16[32,8,640]{2,1,0:T(8,128)(2,1)S(1)} %all-to-all-done.1) | copy-start | bytes 983044
  40.2 21.4 %all-to-all-start.2 = ((bf16[32,8,1024]{2,1,0:T(8,128)(2,1)}), bf16[32,8,1024]{2,1,0:T(8,128)(2,1)S(1)}, u32[]{:S(2)}, u32[]{:S(2)}) async-start(bf16[32,8,1024]{2,1,0:T(8,128)(2,1)} %get-tuple-element.65), calls=%async_computation.2 | async-start | bytes 1048576 | tf_op jit(solution)/shard_map/all_to_all | solution.py:1018
  61.6 1.7 %collective-permute-start.1 = (bf16[32,8,640]{2,1,0:T(8,128)(2,1)S(1)}, bf16[32,8,640]{2,1,0:T(8,128)(2,1)S(1)}, u32[]{:S(2)}, u32[]{:S(2)}) collective-permute-start(bf16[32,8,640]{2,1,0:T(8,128)(2,1)S(1)} %slice.6), channel_id=1, source_target_pairs={{0,1},{1,0},{2,3},{3,2},{4,5},{5,4},{6,7},{7,6},{8,9},{9,8},{10,11... | collective-permute-start | bytes 983048 | tf_op jit(solution)/shard_map/ppermute | solution.py:1022
